TPU v7x, 32 devices: a whole 2x2x4 slice. The times are simulated.
32 devices in a mesh: seq: 8 (over y, x, core), mdl: 4 (over z).
Axes of the slice: x: 2, y: 2, z: 4, core: 2. Of those that a mesh axis runs over, the one named last changes fastest.
Arguments:
- layer_in: float32 [4, 2, 1024, 2048], P(None, None, ('seq', 'mdl')), may hold values from -6 to 6
- doc_ids: int32 [4, 2, 1024], replicated, may hold values from -1 to 20, as said below
- cotangent: float32 [4, 2, 1024, 2048], P(None, None, ('seq', 'mdl')), may hold values from -6 to 6
- norm_params: float32 [4, 2048], replicated
- w_qkv: float32 [2048, 3, 2048], P('seq', None, 'mdl'), may hold values from -0.125 to 0.125
- w_out: float32 [2048, 2048], P('seq', 'mdl'), may hold values from -0.375 to 0.375
- w_up: float32 [2048, 8192], P('seq', 'mdl'), may hold values from -0.125 to 0.125
- w_down: float32 [2048, 8192], P('seq', 'mdl'), may hold values from -0.0625 to 0.0625
- norm_moment: float32 [4, 2048], replicated, may hold values from -543.058 to 543.058
- norm_average: float32 [4, 2048], replicated, may hold values from 0.5 to 1.5
- qkv_moment: float32 [2048, 3, 2048], P('seq', None, 'mdl'), may hold values from -452.54834 to 452.54834
- qkv_average: float32 [2048, 3, 2048], P('seq', None, 'mdl'), may hold values from -0.125 to 0.125
- out_moment: float32 [2048, 2048], P('seq', 'mdl'), may hold values from -452.54834 to 452.54834
- out_average: float32 [2048, 2048], P('seq', 'mdl'), may hold values from -0.375 to 0.375
- up_moment: float32 [2048, 8192], P('seq', 'mdl'), may hold values from -452.54834 to 452.54834
- up_average: float32 [2048, 8192], P('seq', 'mdl'), may hold values from -0.125 to 0.125
- down_moment: float32 [2048, 8192], P('seq', 'mdl'), may hold values from -452.54834 to 452.54834
- down_average: float32 [2048, 8192], P('seq', 'mdl'), may hold values from -0.0625 to 0.0625
Outputs:
- layer_out: float32 [4, 2, 1024, 2048], P(None, None, ('seq', 'mdl'))
- input_grad: float32 [4, 2, 1024, 2048], P(None, None, ('seq', 'mdl'))
- norm_moment_new: float32 [4, 2048], replicated
- norm_average_new: float32 [4, 2048], replicated
- norm_params_new: float32 [4, 2048], replicated
- norm_params_half: bfloat16 [4, 2048], replicated
- qkv_moment_new: float32 [2048, 3, 2048], P('seq', None, 'mdl')
- qkv_average_new: float32 [2048, 3, 2048], P('seq', None, 'mdl')
- qkv_weight_new: float32 [2048, 3, 2048], P('seq', None, 'mdl')
- qkv_weight_half: bfloat16 [2048, 3, 2048], P('seq', None, 'mdl')
- out_moment_new: float32 [2048, 2048], P('seq', 'mdl')
- out_average_new: float32 [2048, 2048], P('seq', 'mdl')
- out_weight_new: float32 [2048, 2048], P('seq', 'mdl')
- out_weight_half: bfloat16 [2048, 2048], P('seq', 'mdl')
- up_moment_new: float32 [2048, 8192], P('seq', 'mdl')
- up_average_new: float32 [2048, 8192], P('seq', 'mdl')
- up_weight_new: float32 [2048, 8192], P('seq', 'mdl')
- up_weight_half: bfloat16 [2048, 8192], P('seq', 'mdl')
- down_moment_new: float32 [2048, 8192], P('seq', 'mdl')
- down_average_new: float32 [2048, 8192], P('seq', 'mdl')
- down_weight_new: float32 [2048, 8192], P('seq', 'mdl')
- down_weight_half: bfloat16 [2048, 8192], P('seq', 'mdl')
Inputs may be any that keep to these rules, and one draw needn't show every extreme that they name: `doc_ids`: documents are numbered from 0 and never fall along a row; each row ends in 1 to 128 padding slots marked -1; every document of a row but the last holds 51 to 1024 slots, and the last may be cut short by the row's padding; some row holds one document over all its slots but its padding.
All inputs are finite; a program needn't handle non-finite values.
Results may differ from a plain program's by a relative error of at most 0.015.
Values may be sent and summed in bfloat16 or wider, within the bound.
No kernel may reach another device: no remote copies, remote signals or barrier semaphores. Data moves between devices by JAX's collectives and lax.ppermute only.
A program may use at most 320 MiB of HBM per device.

v0:
```python
import jax
import jax.numpy as jnp
from jax import lax
from jax.sharding import PartitionSpec as P

HD = 64


EPSILON = 1e-05
HALF_ROOT = 0.7071067811865476
INV_ROOT_TWO_PI = 0.3989422804014327


def for_sending(value):

    def short(part):
        return part.astype(jnp.bfloat16) if part.dtype == jnp.float32 else part

    return jax.tree.map(short, value)


def norm_forward(values, gain, shift):
    row_mean = jnp.mean(values, -1, keepdims=True)
    centred = values - row_mean
    inv_std = lax.rsqrt(jnp.mean(centred * centred, -1, keepdims=True) + EPSILON)
    normed = centred * inv_std
    return (normed * gain + shift, normed, inv_std)


def norm_backward(upstream, normed, inv_std, gain):
    scaled = upstream * gain
    return inv_std * (
        scaled
        - jnp.mean(scaled, -1, keepdims=True)
        - normed * jnp.mean(scaled * normed, -1, keepdims=True)
    )


def gelu_value(inputs):
    return 0.5 * inputs * (1.0 + lax.erf(inputs * HALF_ROOT))


def gelu_slope(inputs):
    return (
        0.5 * (1.0 + lax.erf(inputs * HALF_ROOT))
        + inputs * jnp.exp(-0.5 * inputs * inputs) * INV_ROOT_TWO_PI
    )


def masked_scores(query_heads, key_heads, allowed, factor):
    scores = (
        jnp.einsum("rqhd,rkhd->rhqk", query_heads, key_heads, preferred_element_type=jnp.float32)
        * factor
    )
    return jnp.where(allowed[:, None], scores, -1e30)


def update_param(weight, grad, moment, average, rate):
    new_moment = 0.5 * moment + grad
    new_weight = weight - rate * (grad + 0.5 * new_moment)
    new_average = 0.5 * average + 0.5 * new_weight
    return (new_moment, new_average, new_weight, new_weight.astype(jnp.bfloat16))


def per_device(
    layer_in,
    doc_ids,
    cotangent,
    norm_params,
    w_qkv,
    w_out,
    w_up,
    w_down,
    norm_moment,
    norm_average,
    qkv_moment,
    qkv_average,
    out_moment,
    out_average,
    up_moment,
    up_average,
    down_moment,
    down_average,
):
    mdl_count = lax.axis_size("mdl")
    micro, rows, short, width = layer_in.shape
    slot_dev = short * mdl_count
    slots = doc_ids.shape[2]
    head_dim = HD
    local_heads = w_qkv.shape[2] // head_dim
    factor = head_dim ** (-0.5)
    seq_index = lax.axis_index("seq")
    qkv_full, out_full, up_full, down_full = (
        lax.all_gather(w_qkv.astype(jnp.bfloat16), "seq", axis=0, tiled=True),
        lax.all_gather(w_out.astype(jnp.bfloat16), "seq", axis=0, tiled=True),
        lax.all_gather(w_up.astype(jnp.bfloat16), "seq", axis=0, tiled=True),
        lax.all_gather(w_down.astype(jnp.bfloat16), "seq", axis=0, tiled=True),
    )
    query_pos = seq_index * slot_dev + jnp.arange(slot_dev, dtype=jnp.int32)
    key_pos = jnp.arange(slots, dtype=jnp.int32)
    causal = key_pos[None, :] <= query_pos[:, None]
    diagonal = key_pos[None, :] == query_pos[:, None]
    grad_sums = (
        jnp.zeros(qkv_full.shape, jnp.float32),
        jnp.zeros(out_full.shape, jnp.float32),
        jnp.zeros(up_full.shape, jnp.float32),
        jnp.zeros(down_full.shape, jnp.float32),
    )
    norm_sums = jnp.zeros((4, width), jnp.float32)
    outputs = []
    input_grads = []
    for batch_index in range(micro):
        inputs = layer_in[batch_index]
        doc_row = doc_ids[batch_index]
        upstream = cotangent[batch_index]
        query_docs = lax.dynamic_slice_in_dim(doc_row, seq_index * slot_dev, slot_dev, 1)
        allowed = (query_docs[:, :, None] == doc_row[:, None, :]) & (
            query_docs[:, :, None] >= 0
        ) & causal[None] | diagonal[None]
        normed_one, hat_one, inv_one = norm_forward(inputs, norm_params[0], norm_params[1])
        rows_one = lax.all_gather(normed_one.astype(jnp.bfloat16), "mdl", axis=1, tiled=True)
        projected = jnp.einsum(
            "rsd,dct->rsct", rows_one, qkv_full, preferred_element_type=jnp.float32
        ).astype(jnp.bfloat16)
        queries = projected[:, :, 0]
        keys_own = projected[:, :, 1]
        values_own = projected[:, :, 2]
        keys_all, values_all = (
            lax.all_gather(keys_own, "seq", axis=1, tiled=True),
            lax.all_gather(values_own, "seq", axis=1, tiled=True),
        )
        query_heads = queries.reshape(rows, slot_dev, local_heads, head_dim)
        key_heads = keys_all.reshape(rows, slots, local_heads, head_dim)
        value_heads = values_all.reshape(rows, slots, local_heads, head_dim)
        scores = masked_scores(query_heads, key_heads, allowed, factor)
        row_max = jnp.max(scores, -1, keepdims=True)
        expos = jnp.exp(scores - row_max)
        row_total = jnp.sum(expos, -1, keepdims=True)
        log_total = row_max + jnp.log(row_total)
        probs = (expos / row_total).astype(jnp.bfloat16)
        attended = (
            jnp.einsum("rhqk,rkhd->rqhd", probs, value_heads, preferred_element_type=jnp.float32)
            .astype(jnp.bfloat16)
            .reshape(rows, slot_dev, -1)
        )
        mixed = lax.psum_scatter(
            jnp.einsum("rse,de->rsd", attended, out_full, preferred_element_type=jnp.float32),
            "mdl",
            scatter_dimension=1,
            tiled=True,
        )
        middle = inputs + mixed
        normed_two, hat_two, inv_two = norm_forward(middle, norm_params[2], norm_params[3])
        rows_two = lax.all_gather(normed_two.astype(jnp.bfloat16), "mdl", axis=1, tiled=True)
        up_proj = jnp.einsum("rsd,df->rsf", rows_two, up_full, preferred_element_type=jnp.float32)
        hidden = gelu_value(up_proj).astype(jnp.bfloat16)
        branch = lax.psum_scatter(
            jnp.einsum("rsf,df->rsd", hidden, down_full, preferred_element_type=jnp.float32).astype(
                jnp.bfloat16
            ),
            "mdl",
            scatter_dimension=1,
            tiled=True,
        ).astype(jnp.float32)
        outputs.append(middle + branch)
        back_rows = lax.all_gather(upstream.astype(jnp.bfloat16), "mdl", axis=1, tiled=True)
        down_grad = jnp.einsum("rsd,rsf->df", back_rows, hidden, preferred_element_type=jnp.float32)
        hidden_grad = jnp.einsum(
            "rsd,df->rsf", back_rows, down_full, preferred_element_type=jnp.float32
        )
        up_back = (hidden_grad * gelu_slope(up_proj)).astype(jnp.bfloat16)
        up_grad = jnp.einsum("rsd,rsf->df", rows_two, up_back, preferred_element_type=jnp.float32)
        second_in = lax.psum_scatter(
            jnp.einsum("rsf,df->rsd", up_back, up_full, preferred_element_type=jnp.float32),
            "mdl",
            scatter_dimension=1,
            tiled=True,
        )
        middle_grad = upstream + norm_backward(second_in, hat_two, inv_two, norm_params[2])
        resid_rows = lax.all_gather(middle_grad.astype(jnp.bfloat16), "mdl", axis=1, tiled=True)
        out_grad = jnp.einsum(
            "rsd,rse->de", resid_rows, attended, preferred_element_type=jnp.float32
        )
        attended_back = jnp.einsum(
            "rsd,de->rse", resid_rows, out_full, preferred_element_type=jnp.float32
        )
        attended_back = attended_back.astype(jnp.bfloat16).reshape(
            rows, slot_dev, local_heads, head_dim
        )
        probs_back = jnp.exp(masked_scores(query_heads, key_heads, allowed, factor) - log_total)
        prob_grad = jnp.einsum(
            "rqhd,rkhd->rhqk", attended_back, value_heads, preferred_element_type=jnp.float32
        )
        weighted = jnp.sum(probs_back * prob_grad, -1, keepdims=True)
        score_back = (probs_back * (prob_grad - weighted)).astype(jnp.bfloat16)
        query_back = (
            factor
            * jnp.einsum(
                "rhqk,rkhd->rqhd", score_back, key_heads, preferred_element_type=jnp.float32
            )
        ).astype(jnp.bfloat16)
        value_part = jnp.einsum(
            "rhqk,rqhd->rkhd",
            probs_back.astype(jnp.bfloat16),
            attended_back,
            preferred_element_type=jnp.float32,
        )
        key_part = factor * jnp.einsum(
            "rhqk,rqhd->rkhd", score_back, query_heads, preferred_element_type=jnp.float32
        )
        key_grad, value_grad = (
            lax.psum_scatter(
                key_part.reshape(rows, slots, -1).astype(jnp.bfloat16),
                "seq",
                scatter_dimension=1,
                tiled=True,
            ).astype(jnp.float32),
            lax.psum_scatter(
                value_part.reshape(rows, slots, -1).astype(jnp.bfloat16),
                "seq",
                scatter_dimension=1,
                tiled=True,
            ).astype(jnp.float32),
        )
        proj_back = jnp.stack(
            [
                query_back.reshape(rows, slot_dev, -1),
                key_grad.astype(jnp.bfloat16),
                value_grad.astype(jnp.bfloat16),
            ],
            axis=2,
        )
        qkv_grad = jnp.einsum(
            "rsd,rsct->dct", rows_one, proj_back, preferred_element_type=jnp.float32
        )
        first_in = lax.psum_scatter(
            jnp.einsum(
                "rsct,dct->rsd", proj_back, qkv_full, preferred_element_type=jnp.float32
            ).astype(jnp.bfloat16),
            "mdl",
            scatter_dimension=1,
            tiled=True,
        ).astype(jnp.float32)
        input_grads.append(middle_grad + norm_backward(first_in, hat_one, inv_one, norm_params[0]))
        norm_sums = norm_sums + jnp.stack(
            [
                jnp.sum(first_in * hat_one, (0, 1)),
                jnp.sum(first_in, (0, 1)),
                jnp.sum(second_in * hat_two, (0, 1)),
                jnp.sum(second_in, (0, 1)),
            ]
        )
        local_grads = (qkv_grad, out_grad, up_grad, down_grad)
        grad_sums = tuple(
            (total_part + new_part for total_part, new_part in zip(grad_sums, local_grads))
        )
    final_grads = jax.tree.map(
        lambda part: part.astype(jnp.float32),
        lax.psum_scatter(for_sending(grad_sums), "seq", scatter_dimension=0, tiled=True),
    )
    norm_total = lax.psum(norm_sums, ("seq", "mdl"))
    total_tokens = micro * rows * slots
    weight_rate = 0.02 * total_tokens ** (-0.5)
    norm_rate = 0.15 * total_tokens ** (-0.5)
    norm_new = update_param(norm_params, norm_total, norm_moment, norm_average, norm_rate)
    qkv_new = update_param(w_qkv, final_grads[0], qkv_moment, qkv_average, weight_rate)
    out_new = update_param(w_out, final_grads[1], out_moment, out_average, weight_rate)
    up_new = update_param(w_up, final_grads[2], up_moment, up_average, weight_rate)
    down_new = update_param(w_down, final_grads[3], down_moment, down_average, weight_rate)
    return (
        jnp.stack(outputs),
        jnp.stack(input_grads),
        norm_new[0],
        norm_new[1],
        norm_new[2],
        norm_new[3],
        qkv_new[0],
        qkv_new[1],
        qkv_new[2],
        qkv_new[3],
        out_new[0],
        out_new[1],
        out_new[2],
        out_new[3],
        up_new[0],
        up_new[1],
        up_new[2],
        up_new[3],
        down_new[0],
        down_new[1],
        down_new[2],
        down_new[3],
    )


def solution(mesh):
    placed = (
        P(None, None, ("seq", "mdl"), None),
        P(),
        P(None, None, ("seq", "mdl"), None),
        P(),
        P("seq", None, "mdl"),
        P("seq", "mdl"),
        P("seq", "mdl"),
        P("seq", "mdl"),
        P(),
        P(),
        P("seq", None, "mdl"),
        P("seq", None, "mdl"),
        P("seq", "mdl"),
        P("seq", "mdl"),
        P("seq", "mdl"),
        P("seq", "mdl"),
        P("seq", "mdl"),
        P("seq", "mdl"),
    )
    return jax.shard_map(
        per_device,
        mesh=mesh,
        in_specs=placed,
        out_specs=(
            P(None, None, ("seq", "mdl"), None),
            P(None, None, ("seq", "mdl"), None),
            P(),
            P(),
            P(),
            P(),
            P("seq", None, "mdl"),
            P("seq", None, "mdl"),
            P("seq", None, "mdl"),
            P("seq", None, "mdl"),
            P("seq", "mdl"),
            P("seq", "mdl"),
            P("seq", "mdl"),
            P("seq", "mdl"),
            P("seq", "mdl"),
            P("seq", "mdl"),
            P("seq", "mdl"),
            P("seq", "mdl"),
            P("seq", "mdl"),
            P("seq", "mdl"),
            P("seq", "mdl"),
            P("seq", "mdl"),
        ),
        check_vma=False,
    )
```

profile of v0, /device:TPU:0, one launch (start us, length us, event | category | flops | bytes accessed | tf_op | source)
XLA Modules:
  0.0 2173.5 jit_solution(4068363414027990106)
XLA Ops:
  13.6 28.3 %all-gather.49.cloned.1.call-done = bf16[2,128,2048]{2,1,0:T(8,128)(2,1)} async-done(((bf16[2,32,2048]{2,1,0:T(8,128)(2,1)}), bf16[2,128,2048]{2,1,0:T(8,128)(2,1)}) %all-gather.49.cloned.1.call-update) | async-done | bytes 1048592 | tf_op jit(solution)/shard_map/all_gather | solution.py:121
  41.9 47.5 %all-gather.39.cloned.1.call-done = bf16[2048,3,512]{2,0,1:T(8,128)(2,1)} async-done(((bf16[256,3,512]{2,0,1:T(8,128)(2,1)}), bf16[2048,3,512]{2,0,1:T(8,128)(2,1)}) %all-gather.39.cloned.1.call-update) | async-done | bytes 6291472 | tf_op jit(solution)/shard_map/all_gather | solution.py:94
  99.2 24.1 %all-gather.81.cloned.1.call-done = bf16[2,1024,1,512]{3,1,2,0:T(8,128)(2,1)} async-done(((bf16[2,128,1,512]{3,1,2,0:T(8,128)(2,1)}), bf16[2,1024,1,512]{3,1,2,0:T(8,128)(2,1)}) %all-gather.81.cloned.1.call-update) | async-done | bytes 2097168 | tf_op jit(solution)/shard_map/all_gather | solution.py:130
  127.2 26.3 %all-gather.83.cloned.1.call-done = bf16[2,1024,1,512]{3,1,2,0:T(8,128)(2,1)} async-done(((bf16[2,128,1,512]{3,1,2,0:T(8,128)(2,1)}), bf16[2,1024,1,512]{3,1,2,0:T(8,128)(2,1)}) %all-gather.83.cloned.1.call-update) | async-done | bytes 2097168 | tf_op jit(solution)/shard_map/all_gather | solution.py:129
  190.3 41.2 %reduce-scatter.33.cloned.1.call-done = f32[2,32,2048]{2,1,0:T(8,128)} async-done(((f32[2,128,2048]{2,1,0:T(8,128)}), f32[2,32,2048]{2,1,0:T(8,128)}) %reduce-scatter.33.cloned.1.call-update) | async-done | bytes 524304 | tf_op jit(solution)/shard_map/reduce_scatter | solution.py:146
  239.4 48.4 %all-gather.45.cloned.1.call-done = bf16[2048,2048]{1,0:T(8,128)(2,1)} async-done(((bf16[256,2048]{1,0:T(8,128)(2,1)}), bf16[2048,2048]{1,0:T(8,128)(2,1)}) %all-gather.45.cloned.1.call-update) | async-done | bytes 8388624 | tf_op jit(solution)/shard_map/all_gather | solution.py:96
  287.9 30.2 %all-gather.51.cloned.1.call-done = bf16[2,128,2048]{2,1,0:T(8,128)(2,1)} async-done(((bf16[2,32,2048]{2,1,0:T(8,128)(2,1)}), bf16[2,128,2048]{2,1,0:T(8,128)(2,1)}) %all-gather.51.cloned.1.call-update) | async-done | bytes 1048592 | tf_op jit(solution)/shard_map/all_gather | solution.py:154
  325.5 49.1 %all-gather.47.cloned.1.call-done = bf16[2048,2048]{1,0:T(8,128)(2,1)} async-done(((bf16[256,2048]{1,0:T(8,128)(2,1)}), bf16[2048,2048]{1,0:T(8,128)(2,1)}) %all-gather.47.cloned.1.call-update) | async-done | bytes 8388624 | tf_op jit(solution)/shard_map/all_gather | solution.py:97
  434.3 45.3 %reduce-scatter.53.cloned.1.call-done = f32[2,32,2048]{2,1,0:T(8,128)} async-done(((f32[2,128,2048]{2,1,0:T(8,128)}), f32[2,32,2048]{2,1,0:T(8,128)}) %reduce-scatter.53.cloned.1.call-update) | async-done | bytes 524304 | tf_op jit(solution)/shard_map/reduce_scatter | solution.py:173
  484.7 27.3 %all-gather.67.cloned.1.call-done = bf16[2,128,2048]{2,1,0:T(8,128)(2,1)} async-done(((bf16[2,32,2048]{2,1,0:T(8,128)(2,1)}), bf16[2,128,2048]{2,1,0:T(8,128)(2,1)}) %all-gather.67.cloned.1.call-update) | async-done | bytes 1048592 | tf_op jit(solution)/shard_map/all_gather | solution.py:180
  566.1 44.9 %reduce-scatter.55.cloned.1.call-done = bf16[2,128,512]{2,1,0:T(8,128)(2,1)} async-done(((bf16[2,1024,512]{2,1,0:T(8,128)(2,1)}), bf16[2,128,512]{2,1,0:T(8,128)(2,1)}) %reduce-scatter.55.cloned.1.call-update) | async-done | bytes 262160 | tf_op jit(solution)/shard_map/reduce_scatter | solution.py:212
  616.9 27.2 %reduce-scatter.59.cloned.1.call-done = bf16[2,32,2048]{2,1,0:T(8,128)(2,1)} async-done(((bf16[2,128,2048]{2,1,0:T(8,128)(2,1)}), bf16[2,32,2048]{2,1,0:T(8,128)(2,1)}) %reduce-scatter.59.cloned.1.call-update) | async-done | bytes 262160 | tf_op jit(solution)/shard_map/reduce_scatter | solution.py:236
  648.7 25.4 %all-gather.37.cloned.1.call-done = bf16[2,128,2048]{2,1,0:T(8,128)(2,1)} async-done(((bf16[2,32,2048]{2,1,0:T(8,128)(2,1)}), bf16[2,128,2048]{2,1,0:T(8,128)(2,1)}) %all-gather.37.cloned.1.call-update) | async-done | bytes 1048592 | tf_op jit(solution)/shard_map/all_gather | solution.py:121
  766.8 26.5 %all-gather.79.cloned.1.call-done = bf16[2,1024,1,512]{3,1,2,0:T(8,128)(2,1)} async-done(((bf16[2,128,1,512]{3,1,2,0:T(8,128)(2,1)}), bf16[2,1024,1,512]{3,1,2,0:T(8,128)(2,1)}) %all-gather.79.cloned.1.call-update) | async-done | bytes 2097168 | tf_op jit(solution)/shard_map/all_gather | solution.py:129
  827.6 26.5 %all-gather.87.cloned.1.call-done = bf16[2,1024,1,512]{3,1,2,0:T(8,128)(2,1)} async-done(((bf16[2,128,1,512]{3,1,2,0:T(8,128)(2,1)}), bf16[2,1024,1,512]{3,1,2,0:T(8,128)(2,1)}) %all-gather.87.cloned.1.call-update) | async-done | bytes 2097168 | tf_op jit(solution)/shard_map/all_gather | solution.py:129
  888.3 26.5 %all-gather.91.cloned.1.call-done = bf16[2,1024,1,512]{3,1,2,0:T(8,128)(2,1)} async-done(((bf16[2,128,1,512]{3,1,2,0:T(8,128)(2,1)}), bf16[2,1024,1,512]{3,1,2,0:T(8,128)(2,1)}) %all-gather.91.cloned.1.call-update) | async-done | bytes 2097168 | tf_op jit(solution)/shard_map/all_gather | solution.py:129
  930.1 31.3 %reduce-scatter.29.cloned.1.call-done = f32[2,32,2048]{2,1,0:T(8,128)} async-done(((f32[2,128,2048]{2,1,0:T(8,128)}), f32[2,32,2048]{2,1,0:T(8,128)}) %reduce-scatter.29.cloned.1.call-update) | async-done | bytes 524304 | tf_op jit(solution)/shard_map/reduce_scatter | solution.py:146
  961.4 46.1 %reduce-scatter.37.cloned.1.call-done = f32[2,32,2048]{2,1,0:T(8,128)} async-done(((f32[2,128,2048]{2,1,0:T(8,128)}), f32[2,32,2048]{2,1,0:T(8,128)}) %reduce-scatter.37.cloned.1.call-update) | async-done | bytes 524304 | tf_op jit(solution)/shard_map/reduce_scatter | solution.py:146
  1007.5 45.5 %reduce-scatter.41.cloned.1.call-done = f32[2,32,2048]{2,1,0:T(8,128)} async-done(((f32[2,128,2048]{2,1,0:T(8,128)}), f32[2,32,2048]{2,1,0:T(8,128)}) %reduce-scatter.41.cloned.1.call-update) | async-done | bytes 524304 | tf_op jit(solution)/shard_map/reduce_scatter | solution.py:146
  1278.5 45.4 %reduce-scatter.69.cloned.1.call-done = f32[2,32,2048]{2,1,0:T(8,128)} async-done(((f32[2,128,2048]{2,1,0:T(8,128)}), f32[2,32,2048]{2,1,0:T(8,128)}) %reduce-scatter.69.cloned.1.call-update) | async-done | bytes 524304 | tf_op jit(solution)/shard_map/reduce_scatter | solution.py:173
  1323.8 45.5 %reduce-scatter.45.cloned.1.call-done = f32[2,32,2048]{2,1,0:T(8,128)} async-done(((f32[2,128,2048]{2,1,0:T(8,128)}), f32[2,32,2048]{2,1,0:T(8,128)}) %reduce-scatter.45.cloned.1.call-update) | async-done | bytes 524304 | tf_op jit(solution)/shard_map/reduce_scatter | solution.py:173
  1372.0 26.7 %reduce-scatter.43.cloned.1.call-done = bf16[2,32,2048]{2,1,0:T(8,128)(2,1)} async-done(((bf16[2,128,2048]{2,1,0:T(8,128)(2,1)}), bf16[2,32,2048]{2,1,0:T(8,128)(2,1)}) %reduce-scatter.43.cloned.1.call-update) | async-done | bytes 262160 | tf_op jit(solution)/shard_map/reduce_scatter | solution.py:157
  1398.7 28.7 %reduce-scatter.39.cloned.1.call-done = bf16[2,32,2048]{2,1,0:T(8,128)(2,1)} async-done(((bf16[2,128,2048]{2,1,0:T(8,128)(2,1)}), bf16[2,32,2048]{2,1,0:T(8,128)(2,1)}) %reduce-scatter.39.cloned.1.call-update) | async-done | bytes 262160 | tf_op jit(solution)/shard_map/reduce_scatter | solution.py:157
  1430.7 25.3 %reduce-scatter.31.cloned.1.call-done = bf16[2,32,2048]{2,1,0:T(8,128)(2,1)} async-done(((bf16[2,128,2048]{2,1,0:T(8,128)(2,1)}), bf16[2,32,2048]{2,1,0:T(8,128)(2,1)}) %reduce-scatter.31.cloned.1.call-update) | async-done | bytes 262160 | tf_op jit(solution)/shard_map/reduce_scatter | solution.py:157
  1459.4 25.5 %all-gather.71.cloned.1.call-done = bf16[2,128,2048]{2,1,0:T(8,128)(2,1)} async-done(((bf16[2,32,2048]{2,1,0:T(8,128)(2,1)}), bf16[2,128,2048]{2,1,0:T(8,128)(2,1)}) %all-gather.71.cloned.1.call-update) | async-done | bytes 1048592 | tf_op jit(solution)/shard_map/all_gather | solution.py:180
  1588.5 45.0 %reduce-scatter.63.cloned.1.call-done = bf16[2,128,512]{2,1,0:T(8,128)(2,1)} async-done(((bf16[2,1024,512]{2,1,0:T(8,128)(2,1)}), bf16[2,128,512]{2,1,0:T(8,128)(2,1)}) %reduce-scatter.63.cloned.1.call-update) | async-done | bytes 262160 | tf_op jit(solution)/shard_map/reduce_scatter | solution.py:212
  1651.4 26.7 %reduce-scatter.49.cloned.1.call-done = bf16[2,128,512]{2,1,0:T(8,128)(2,1)} async-done(((bf16[2,1024,512]{2,1,0:T(8,128)(2,1)}), bf16[2,128,512]{2,1,0:T(8,128)(2,1)}) %reduce-scatter.49.cloned.1.call-update) | async-done | bytes 262160 | tf_op jit(solution)/shard_map/reduce_scatter | solution.py:218
  1678.2 45.0 %reduce-scatter.47.cloned.1.call-done = bf16[2,128,512]{2,1,0:T(8,128)(2,1)} async-done(((bf16[2,1024,512]{2,1,0:T(8,128)(2,1)}), bf16[2,128,512]{2,1,0:T(8,128)(2,1)}) %reduce-scatter.47.cloned.1.call-update) | async-done | bytes 262160 | tf_op jit(solution)/shard_map/reduce_scatter | solution.py:212
  1768.4 45.0 %reduce-scatter.71.cloned.1.call-done = bf16[2,128,512]{2,1,0:T(8,128)(2,1)} async-done(((bf16[2,1024,512]{2,1,0:T(8,128)(2,1)}), bf16[2,128,512]{2,1,0:T(8,128)(2,1)}) %reduce-scatter.71.cloned.1.call-update) | async-done | bytes 262160 | tf_op jit(solution)/shard_map/reduce_scatter | solution.py:212
  1948.3 39.6 %psum.7 = f32[4,2048]{1,0:T(4,128)S(1)} all-reduce(f32[4,2048]{1,0:T(4,128)S(1)} %fusion.273), channel_id=1, replica_groups=mesh['seq'=8,'mdl'=4] {'seq','mdl'}, use_global_device_ids=true, to_apply=%region_84.85 | all-reduce | flops 8192 | bytes 65536 | tf_op jit(solution)/shard_map/psum | solution.py:261
  2027.1 67.6 %reduce-scatter.83.cloned.1.call-done = bf16[256,2048]{1,0:T(8,128)(2,1)} async-done(((bf16[2048,2048]{1,0:T(8,128)(2,1)}), bf16[256,2048]{1,0:T(8,128)(2,1)}) %reduce-scatter.83.cloned.1.call-update) | async-done | bytes 1048592 | tf_op jit(solution)/shard_map/reduce_scatter | solution.py:259
  2101.9 58.4 %reduce-scatter.77.cloned.1.call-done = bf16[256,3,512]{2,0,1:T(8,128)(2,1)} async-done(((bf16[2048,3,512]{2,0,1:T(8,128)(2,1)}), bf16[256,3,512]{2,0,1:T(8,128)(2,1)}) %reduce-scatter.77.cloned.1.call-update) | async-done | bytes 786448 | tf_op jit(solution)/shard_map/reduce_scatter | solution.py:259
  (608 shorter events, 964.6 us)
Async XLA Ops:
  233.8 140.8 %all-gather.47.cloned.1.call-start = ((), (), s32[]{:S(2)}) async-start(), calls=%async_computation.34 | async-start | bytes 9437184 | tf_op jit(solution)/shard_map/all_gather | solution.py:97
  236.6 168.0 %all-gather.65.cloned.1.call-start = ((), (), s32[]{:S(2)}) async-start(), calls=%async_computation.54 | async-start | bytes 1310720 | tf_op jit(solution)/shard_map/all_gather | solution.py:166
  239.2 195.1 %reduce-scatter.35.cloned.1.call-start = ((), (), s32[]{:S(2)}) async-start(), calls=%async_computation.39 | async-start | bytes 1310720 | tf_op jit(solution)/shard_map/reduce_scatter | solution.py:157
  680.7 143.1 %all-gather.85.cloned.1.call-start = ((), (), s32[]{:S(2)}) async-start(), calls=%async_computation.80 | async-start | bytes 2359296 | tf_op jit(solution)/shard_map/all_gather | solution.py:130
  709.4 144.8 %all-gather.87.cloned.1.call-start = ((), (), s32[]{:S(2)}) async-start(), calls=%async_computation.81 | async-start | bytes 2359296 | tf_op jit(solution)/shard_map/all_gather | solution.py:129
  710.1 174.3 %all-gather.89.cloned.1.call-start = ((), (), s32[]{:S(2)}) async-start(), calls=%async_computation.82 | async-start | bytes 2359296 | tf_op jit(solution)/shard_map/all_gather | solution.py:130
  739.0 175.9 %all-gather.91.cloned.1.call-start = ((), (), s32[]{:S(2)}) async-start(), calls=%async_computation.83 | async-start | bytes 2359296 | tf_op jit(solution)/shard_map/all_gather | solution.py:129
  739.7 221.7 %reduce-scatter.29.cloned.1.call-start = ((), (), s32[]{:S(2)}) async-start(), calls=%async_computation.31 | async-start | bytes 2621440 | tf_op jit(solution)/shard_map/reduce_scatter | solution.py:146
  809.2 198.2 %reduce-scatter.37.cloned.1.call-start = ((), (), s32[]{:S(2)}) async-start(), calls=%async_computation.41 | async-start | bytes 2621440 | tf_op jit(solution)/shard_map/reduce_scatter | solution.py:146
  870.1 182.9 %reduce-scatter.41.cloned.1.call-start = ((), (), s32[]{:S(2)}) async-start(), calls=%async_computation.45 | async-start | bytes 2621440 | tf_op jit(solution)/shard_map/reduce_scatter | solution.py:146
  930.1 153.9 %all-gather.55.cloned.1.call-start = ((), (), s32[]{:S(2)}) async-start(), calls=%async_computation.42 | async-start | bytes 1310720 | tf_op jit(solution)/shard_map/all_gather | solution.py:154
  1058.6 143.8 %all-gather.43.cloned.1.call-start = ((), (), s32[]{:S(2)}) async-start(), calls=%async_computation.32 | async-start | bytes 1310720 | tf_op jit(solution)/shard_map/all_gather | solution.py:154
  1059.2 172.9 %all-gather.61.cloned.1.call-start = ((), (), s32[]{:S(2)}) async-start(), calls=%async_computation.48 | async-start | bytes 1310720 | tf_op jit(solution)/shard_map/all_gather | solution.py:166
  1059.9 218.5 %reduce-scatter.61.cloned.1.call-start = ((), (), s32[]{:S(2)}) async-start(), calls=%async_computation.61 | async-start | bytes 2621440 | tf_op jit(solution)/shard_map/reduce_scatter | solution.py:173
  1128.2 195.6 %reduce-scatter.69.cloned.1.call-start = ((), (), s32[]{:S(2)}) async-start(), calls=%async_computation.67 | async-start | bytes 2621440 | tf_op jit(solution)/shard_map/reduce_scatter | solution.py:173
  1188.1 181.2 %reduce-scatter.45.cloned.1.call-start = ((), (), s32[]{:S(2)}) async-start(), calls=%async_computation.49 | async-start | bytes 2621440 | tf_op jit(solution)/shard_map/reduce_scatter | solution.py:173
  1247.5 151.2 %reduce-scatter.43.cloned.1.call-start = ((), (), s32[]{:S(2)}) async-start(), calls=%async_computation.47 | async-start | bytes 1310720 | tf_op jit(solution)/shard_map/reduce_scatter | solution.py:157
  1255.0 172.3 %reduce-scatter.39.cloned.1.call-start = ((), (), s32[]{:S(2)}) async-start(), calls=%async_computation.43 | async-start | bytes 1310720 | tf_op jit(solution)/shard_map/reduce_scatter | solution.py:157
  1261.9 194.2 %reduce-scatter.31.cloned.1.call-start = ((), (), s32[]{:S(2)}) async-start(), calls=%async_computation.35 | async-start | bytes 1310720 | tf_op jit(solution)/shard_map/reduce_scatter | solution.py:157
  1269.5 215.3 %all-gather.71.cloned.1.call-start = ((), (), s32[]{:S(2)}) async-start(), calls=%async_computation.62 | async-start | bytes 1310720 | tf_op jit(solution)/shard_map/all_gather | solution.py:180
  1497.3 136.1 %reduce-scatter.63.cloned.1.call-start = ((), (), s32[]{:S(2)}) async-start(), calls=%async_computation.63 | async-start | bytes 2359296 | tf_op jit(solution)/shard_map/reduce_scatter | solution.py:212
  1514.9 163.3 %reduce-scatter.49.cloned.1.call-start = ((), (), s32[]{:S(2)}) async-start(), calls=%async_computation.52 | async-start | bytes 2359296 | tf_op jit(solution)/shard_map/reduce_scatter | solution.py:218
  1527.7 195.4 %reduce-scatter.47.cloned.1.call-start = ((), (), s32[]{:S(2)}) async-start(), calls=%async_computation.51 | async-start | bytes 2359296 | tf_op jit(solution)/shard_map/reduce_scatter | solution.py:212
  1545.3 223.1 %reduce-scatter.73.cloned.1.call-start = ((), (), s32[]{:S(2)}) async-start(), calls=%async_computation.70 | async-start | bytes 2359296 | tf_op jit(solution)/shard_map/reduce_scatter | solution.py:218
  1555.1 258.3 %reduce-scatter.71.cloned.1.call-start = ((), (), s32[]{:S(2)}) async-start(), calls=%async_computation.69 | async-start | bytes 2359296 | tf_op jit(solution)/shard_map/reduce_scatter | solution.py:212
  1570.8 349.2 %reduce-scatter.79.cloned.1.call-start = ((), (), s32[]{:S(2)}) async-start(), calls=%async_computation.73 | async-start | bytes 2359296 | tf_op jit(solution)/shard_map/reduce_scatter | solution.py:259
  1577.7 346.3 %reduce-scatter.67.cloned.1.call-start = ((), (), s32[]{:S(2)}) async-start(), calls=%async_computation.65 | async-start | bytes 1310720 | tf_op jit(solution)/shard_map/reduce_scatter | solution.py:236
  1639.3 284.7 %reduce-scatter.51.cloned.1.call-start = ((), (), s32[]{:S(2)}) async-start(), calls=%async_computation.53 | async-start | bytes 1310720 | tf_op jit(solution)/shard_map/reduce_scatter | solution.py:236
  1729.1 216.5 %reduce-scatter.75.cloned.1.call-start = ((), (), s32[]{:S(2)}) async-start(), calls=%async_computation.71 | async-start | bytes 1310720 | tf_op jit(solution)/shard_map/reduce_scatter | solution.py:236
  1819.3 200.7 %reduce-scatter.81.cloned.1.call-start = ((), (), s32[]{:S(2)}) async-start(), calls=%async_computation.74 | async-start | bytes 9437184 | tf_op jit(solution)/shard_map/reduce_scatter | solution.py:259
  1841.8 252.9 %reduce-scatter.83.cloned.1.call-start = ((), (), s32[]{:S(2)}) async-start(), calls=%async_computation.75 | async-start | bytes 9437184 | tf_op jit(solution)/shard_map/reduce_scatter | solution.py:259
  1879.9 280.3 %reduce-scatter.77.cloned.1.call-start = ((), (), s32[]{:S(2)}) async-start(), calls=%async_computation.72 | async-start | bytes 7077888 | tf_op jit(solution)/shard_map/reduce_scatter | solution.py:259
  (163 other events, 6279.2 us)
Sparse Core Ops, SparseCore 0:
  11.2 30.6 all-gather.48
  44.3 45.0 all-gather.38
  95.4 27.8 all-gather.80
  125.6 27.8 all-gather.82
  155.9 27.8 all-gather.40
  187.6 43.8 reduce-scatter.32
  234.1 53.6 all-gather.44
  290.1 27.9 all-gather.50
  320.7 53.8 all-gather.46
  376.7 27.9 all-gather.64
  437.0 42.5 reduce-scatter.52
  525.3 40.7 reduce-scatter.56
  569.8 41.1 reduce-scatter.54
  795.8 27.8 all-gather.84
  826.2 27.8 all-gather.86
  856.5 27.8 all-gather.88
  917.5 43.8 reduce-scatter.28
  964.2 43.1 reduce-scatter.36
  1009.8 43.1 reduce-scatter.40
  1235.1 43.3 reduce-scatter.60
  1280.6 43.1 reduce-scatter.68
  1326.1 43.1 reduce-scatter.44
  1547.7 40.7 reduce-scatter.64
  1592.2 41.1 reduce-scatter.62
  1636.9 41.2 reduce-scatter.48
  1681.9 41.1 reduce-scatter.46
  1727.2 41.2 reduce-scatter.72
  1772.2 41.1 reduce-scatter.70
  1817.0 41.2 reduce-scatter.78
  1949.4 70.5 reduce-scatter.80
  2023.4 71.2 reduce-scatter.82
  2098.5 61.7 reduce-scatter.76
  (24 shorter events, 646.8 us)
where the time goes:
time: 2180 us; the launch traced here: 2170 us
  waiting for transfers between devices  1530 us (70%)
  matrix products  390 us (18%)
  other arithmetic  99.4 us (5%)
  local copies, waits for them, and re-layouts  94.8 us (4%)
  blocking collectives  39.6 us (2%)
    reduce_scatter x4, waiting for transfers between devices, per_device(): lax.psum_scatter(key_part.reshape(rows, slots, -1).astype(jnp.bfloat16),...  180 us
    reduce_scatter x4, waiting for transfers between devices, per_device(): lax.psum_scatter(jnp.einsum('rse,de->rsd', attended, out_full, preferred_...  164 us
    reduce_scatter x4, waiting for transfers between devices, per_device(): lax.psum_scatter(for_sending(grad_sums), 'seq', scatter_dimension=0, tile...  148 us
    reduce_scatter x4, waiting for transfers between devices, per_device(): lax.psum_scatter(jnp.einsum('rsf,df->rsd', up_back, up_full, preferred_el...  145 us
    all_gather x4, waiting for transfers between devices, per_device(): lax.all_gather(keys_own, 'seq', axis=1, tiled=True)  106 us
    all_gather x4, waiting for transfers between devices, per_device(): lax.all_gather(normed_one.astype(jnp.bfloat16), 'mdl', axis=1, tiled=True)  99.5 us
    reduce_scatter x4, waiting for transfers between devices, per_device(): lax.psum_scatter(jnp.einsum('rsf,df->rsd', hidden, down_full, preferred_e...  95.1 us
    all_gather x4, waiting for transfers between devices, per_device(): lax.all_gather(upstream.astype(jnp.bfloat16), 'mdl', axis=1, tiled=True)  90.7 us
  transfers between devices with their start and end apart: 56, of which 51 were waited for; matrix products, arithmetic and copies ran while one was open for 23% of the time, Pallas kernels for 0%

commit v1 on v0

v1 whole, which is shorter than its diff:
```python
import functools

import jax
import jax.numpy as jnp
from jax import lax
from jax.experimental import pallas as pl
from jax.experimental.pallas import tpu as pltpu
from jax.sharding import PartitionSpec as P

HD = 64
LANES = 128
CHUNKS = 2

EPSILON = 1e-05
HALF_ROOT = 0.7071067811865476
INV_ROOT_TWO_PI = 0.3989422804014327
BF16 = jnp.bfloat16
F32 = jnp.float32


def norm_forward(values, gain, shift):
    row_mean = jnp.mean(values, -1, keepdims=True)
    centred = values - row_mean
    inv_std = lax.rsqrt(jnp.mean(centred * centred, -1, keepdims=True) + EPSILON)
    normed = centred * inv_std
    return (normed * gain + shift, normed, inv_std)


def norm_backward(upstream, normed, inv_std, gain):
    scaled = upstream * gain
    return inv_std * (
        scaled
        - jnp.mean(scaled, -1, keepdims=True)
        - normed * jnp.mean(scaled * normed, -1, keepdims=True)
    )


def update_param(weight, grad, moment, average, rate):
    new_moment = 0.5 * moment + grad
    new_weight = weight - rate * (grad + 0.5 * new_moment)
    new_average = 0.5 * average + 0.5 * new_weight
    return (new_moment, new_average, new_weight, new_weight.astype(BF16))


def dot(a, b, dims):
    return lax.dot_general(a, b, (dims, ((), ())), preferred_element_type=F32)


def ring_gather(block, axis):
    count = lax.axis_size(axis)
    pairs = [(i, (i + 1) % count) for i in range(count)]
    parts = [block]
    for _ in range(count - 1):
        parts.append(lax.ppermute(parts[-1], axis, pairs))
    return jnp.stack(parts)


def ring_scatter(parts, axis):
    count = lax.axis_size(axis)
    pairs = [(i, (i + 1) % count) for i in range(count)]
    carried = None
    for j in range(1, count):
        term = parts[j]
        if carried is not None:
            term = term + carried.astype(F32)
        carried = lax.ppermute(term.astype(BF16), axis, pairs)
    return parts[0] + carried.astype(F32)


def score_blocks(keys, queries, kpos, first, last, start, size):
    diag = dot(keys[start : start + size], queries, ((1,), (1,)))
    pos = kpos[start : start + size]
    diag = jnp.where((pos >= first) & (pos <= last), diag, -1e30)
    if not start:
        return [diag]
    ahead = dot(keys[:start], queries, ((1,), (1,)))
    return [jnp.where(kpos[:start] >= first, ahead, -1e30), diag]


def attend_kernel(kpos_ref, meta_ref, q_ref, k_ref, v_ref, o_ref, lse_ref, *, size, factor):
    slots = kpos_ref.shape[0]
    per = q_ref.shape[1] * q_ref.shape[2]
    heads = LANES // HD
    keys = k_ref[...].reshape(slots, LANES)
    values = v_ref[...].reshape(slots, LANES)
    kpos = kpos_ref[...]
    for start in range(0, slots, size):
        span = pl.ds(start // per, size // per)
        queries = q_ref[span].reshape(size, LANES) * factor
        first = meta_ref[0:1, start : start + size]
        last = meta_ref[1:2, start : start + size]
        outs = []
        for head in range(heads):
            cols = slice(head * HD, (head + 1) * HD)
            blocks = score_blocks(keys[:, cols], queries[:, cols], kpos, first, last, start, size)
            top = functools.reduce(jnp.maximum, [jnp.max(b, 0, keepdims=True) for b in blocks])
            blocks = [jnp.exp(b - top) for b in blocks]
            total = functools.reduce(jnp.add, [jnp.sum(b, 0, keepdims=True) for b in blocks])
            lse_ref[head : head + 1, start : start + size] = top + jnp.log(total)
            inverse = 1.0 / total
            out = None
            offset = 0
            for b in blocks:
                rows = slice(offset, offset + b.shape[0])
                offset += b.shape[0]
                term = dot(values[rows, cols], (b * inverse).astype(BF16), ((0,), (0,)))
                out = term if out is None else out + term
            outs.append(out)
        merged = jnp.concatenate(outs, 0).T.astype(BF16)
        o_ref[span] = merged.reshape(size // per, *o_ref.shape[1:])


def attend_back_kernel(
    kpos_ref, meta_ref, lse_ref, q_ref, k_ref, v_ref, g_ref, out_ref, dk_acc, dv_acc, *, size, factor
):
    slots = kpos_ref.shape[0]
    per = q_ref.shape[1] * q_ref.shape[2]
    heads = LANES // HD
    keys = k_ref[...].reshape(slots, LANES)
    values = v_ref[...].reshape(slots, LANES)
    kpos = kpos_ref[...]
    dk_acc[...] = jnp.zeros_like(dk_acc)
    dv_acc[...] = jnp.zeros_like(dv_acc)
    for start in range(0, slots, size):
        span = pl.ds(start // per, size // per)
        queries = q_ref[span].reshape(size, LANES) * factor
        upstream = g_ref[span].reshape(size, LANES)
        first = meta_ref[0:1, start : start + size]
        last = meta_ref[1:2, start : start + size]
        dqs, dks, dvs = [], [], []
        for head in range(heads):
            cols = slice(head * HD, (head + 1) * HD)
            blocks = score_blocks(keys[:, cols], queries[:, cols], kpos, first, last, start, size)
            lse = lse_ref[head : head + 1, start : start + size]
            probs = [jnp.exp(b - lse) for b in blocks]
            edges = [0] + ([start] if start else []) + [start + size]
            rows = [slice(a, b) for a, b in zip(edges[:-1], edges[1:])]
            back = [dot(values[r, cols], upstream[:, cols], ((1,), (1,))) for r in rows]
            terms = [p * b for p, b in zip(probs, back)]
            weighted = functools.reduce(jnp.add, [jnp.sum(t, 0, keepdims=True) for t in terms])
            score_back = [(t - p * weighted).astype(BF16) for t, p in zip(terms, probs)]
            dks.append([dot(s, queries[:, cols], ((1,), (0,))) for s in score_back])
            dvs.append([dot(p.astype(BF16), upstream[:, cols], ((1,), (0,))) for p in probs])
            dq = [dot(keys[r, cols], s, ((0,), (0,))) for r, s in zip(rows, score_back)]
            dqs.append(functools.reduce(jnp.add, dq) * factor)
        merged = jnp.concatenate(dqs, 0).T.astype(BF16)
        out_ref[span, 0] = merged.reshape(size // per, *out_ref.shape[2:])
        for i, r in enumerate(rows):
            dk_acc[r] += jnp.concatenate([d[i] for d in dks], 1)
            dv_acc[r] += jnp.concatenate([d[i] for d in dvs], 1)
    shape = (out_ref.shape[0], *out_ref.shape[2:])
    out_ref[:, 1] = dk_acc[...].astype(BF16).reshape(shape)
    out_ref[:, 2] = dv_acc[...].astype(BF16).reshape(shape)


def kind_spec(shape, kind):
    seq, _, _, blocks, short, lanes = shape
    return pl.BlockSpec(
        (seq, None, None, blocks, short, lanes), lambda r, kind=kind: (0, kind, r, 0, 0, 0)
    )


def attention(qkv, kpos, meta, size):
    seq, _, units, blocks, short, lanes = qkv.shape
    slots = kpos.shape[0]
    heads = LANES // HD
    work = units * heads * slots * slots * 5 // 8
    return pl.pallas_call(
        functools.partial(attend_kernel, size=size, factor=HD**-0.5),
        grid=(units,),
        in_specs=[
            pl.BlockSpec((slots, 1), lambda r: (0, 0)),
            pl.BlockSpec((None, 2, slots), lambda r: (r, 0, 0)),
            *(kind_spec(qkv.shape, kind) for kind in range(3)),
        ],
        out_specs=[
            pl.BlockSpec((seq, None, blocks, short, lanes), lambda r: (0, r, 0, 0, 0)),
            pl.BlockSpec((None, heads, slots), lambda r: (r, 0, 0)),
        ],
        out_shape=[
            jax.ShapeDtypeStruct((seq, units, blocks, short, lanes), BF16),
            jax.ShapeDtypeStruct((units, heads, slots), F32),
        ],
        compiler_params=pltpu.CompilerParams(vmem_limit_bytes=48 << 20),
        cost_estimate=pl.CostEstimate(
            flops=work * HD * 4 * 4, bytes_accessed=units * slots * LANES * 8, transcendentals=work
        ),
        name="attend",
    )(kpos, meta, qkv, qkv, qkv)


def attention_back(qkv, upstream, lse, kpos, meta, size):
    seq, _, units, blocks, short, lanes = qkv.shape
    slots = kpos.shape[0]
    heads = LANES // HD
    work = units * heads * slots * slots * 5 // 8
    return pl.pallas_call(
        functools.partial(attend_back_kernel, size=size, factor=HD**-0.5),
        grid=(units,),
        in_specs=[
            pl.BlockSpec((slots, 1), lambda r: (0, 0)),
            pl.BlockSpec((None, 2, slots), lambda r: (r, 0, 0)),
            pl.BlockSpec((None, heads, slots), lambda r: (r, 0, 0)),
            *(kind_spec(qkv.shape, kind) for kind in range(3)),
            pl.BlockSpec((seq, None, blocks, short, lanes), lambda r: (0, r, 0, 0, 0)),
        ],
        out_specs=pl.BlockSpec((seq, 3, None, blocks, short, lanes), lambda r: (0, 0, r, 0, 0, 0)),
        out_shape=jax.ShapeDtypeStruct(qkv.shape, BF16),
        scratch_shapes=[pltpu.VMEM((slots, LANES), F32), pltpu.VMEM((slots, LANES), F32)],
        compiler_params=pltpu.CompilerParams(vmem_limit_bytes=48 << 20),
        cost_estimate=pl.CostEstimate(
            flops=work * HD * 10 * 4, bytes_accessed=units * slots * LANES * 16, transcendentals=work
        ),
        name="attend_back",
    )(kpos, meta, lse, qkv, qkv, qkv, upstream)


def per_device(
    layer_in,
    doc_ids,
    cotangent,
    norm_params,
    w_qkv,
    w_out,
    w_up,
    w_down,
    norm_moment,
    norm_average,
    qkv_moment,
    qkv_average,
    out_moment,
    out_average,
    up_moment,
    up_average,
    down_moment,
    down_average,
):
    mdl_count = lax.axis_size("mdl")
    seq_count = lax.axis_size("seq")
    micro, rows, short, width = layer_in.shape
    slots = doc_ids.shape[2]
    slot_dev = short * mdl_count
    embed = w_qkv.shape[2]
    pairs = embed // LANES
    groups = seq_count // pairs
    chunks = CHUNKS
    while (micro * rows // chunks) % groups:
        chunks //= 2
    chunk_rows = micro * rows // chunks
    units = chunk_rows // groups
    size = slot_dev * max(1, 256 // slot_dev)
    seq_index = lax.axis_index("seq")
    mdl_index = lax.axis_index("mdl")

    behind = (mdl_index - jnp.arange(mdl_count, dtype=jnp.int32)) % mdl_count
    order = (
        jnp.arange(seq_count, dtype=jnp.int32)[:, None, None] * slot_dev
        + behind[None, :, None] * short
        + jnp.arange(short, dtype=jnp.int32)
    ).reshape(slots)
    docs = doc_ids.reshape(chunks, groups, units, slots)
    docs = lax.dynamic_index_in_dim(docs, seq_index % groups, 1, False)
    first = jnp.sum(
        ((docs[..., None, :] >= 0) & (docs[..., None, :] < docs[..., :, None])).astype(jnp.int32), -1
    )
    first = jnp.where(docs >= 0, first, jnp.arange(slots, dtype=jnp.int32))
    first = first.reshape(chunks, units, seq_count, mdl_count, short)
    first = jnp.stack(
        [lax.dynamic_index_in_dim(first, behind[j], 3, False) for j in range(mdl_count)], 3
    ).reshape(chunks, units, slots)
    meta = jnp.stack([first, jnp.broadcast_to(order, first.shape)], 2)
    kpos = order[:, None]

    qkv_full = lax.all_gather(w_qkv.astype(BF16), "seq", axis=0, tiled=True).reshape(width, 3 * embed)
    out_full = lax.all_gather(w_out.astype(BF16), "seq", axis=0, tiled=True)
    up_full = lax.all_gather(w_up.astype(BF16), "seq", axis=0, tiled=True)
    down_full = lax.all_gather(w_down.astype(BF16), "seq", axis=0, tiled=True)

    def exchange(value):
        return lax.all_to_all(value, "seq", 0, 0, tiled=True)

    def gather(value):
        return ring_gather(value, "mdl").reshape(-1, width)

    def scatter(value):
        return ring_scatter(value.reshape(mdl_count, chunk_rows * short, width), "mdl")

    def to_units(value, kinds):
        value = value.reshape(mdl_count, groups, units, short, kinds, pairs, LANES)
        value = value.transpose(5, 1, 4, 2, 0, 3, 6)
        return value.reshape(seq_count, kinds, units, mdl_count, short, LANES)

    def from_units(value, kinds):
        value = value.reshape(pairs, groups, kinds, units, mdl_count, short, LANES)
        value = value.transpose(4, 1, 3, 5, 2, 0, 6)
        return value.reshape(mdl_count * chunk_rows * short, kinds * embed)

    span = micro // chunks
    saved = []
    outputs, input_grads = [], []
    norm_sums = jnp.zeros((4, width), F32)
    for c in range(chunks):
        inputs = layer_in[c * span : (c + 1) * span].reshape(-1, width)
        upstream = cotangent[c * span : (c + 1) * span].reshape(-1, width)
        normed_one, hat_one, inv_one = norm_forward(inputs, norm_params[0], norm_params[1])
        rows_one = gather(normed_one.astype(BF16))
        projected = dot(rows_one, qkv_full, ((1,), (0,))).astype(BF16)
        qkv = exchange(to_units(projected, 3))
        out, lse = attention(qkv, kpos, meta[c], size)
        attended = from_units(exchange(out), 1)
        mixed = scatter(dot(attended, out_full, ((1,), (1,))))
        middle = inputs + mixed
        normed_two, hat_two, inv_two = norm_forward(middle, norm_params[2], norm_params[3])
        rows_two = gather(normed_two.astype(BF16))
        up_proj = dot(rows_two, up_full, ((1,), (0,)))
        cdf = 0.5 * (1.0 + lax.erf(up_proj * HALF_ROOT))
        hidden = (up_proj * cdf).astype(BF16)
        slope = cdf + up_proj * jnp.exp(-0.5 * up_proj * up_proj) * INV_ROOT_TWO_PI
        branch = scatter(dot(hidden, down_full, ((1,), (1,))))
        outputs.append(middle + branch)
        back_rows = gather(upstream.astype(BF16))
        hidden_grad = dot(back_rows, down_full, ((1,), (0,)))
        up_back = (hidden_grad * slope).astype(BF16)
        second_in = scatter(dot(up_back, up_full, ((1,), (1,))))
        middle_grad = upstream + norm_backward(second_in, hat_two, inv_two, norm_params[2])
        resid_rows = gather(middle_grad.astype(BF16))
        attended_back = dot(resid_rows, out_full, ((1,), (0,))).astype(BF16)
        unit_back = exchange(to_units(attended_back, 1))[:, 0]
        qkv_back = attention_back(qkv, unit_back, lse, kpos, meta[c], size)
        proj_back = from_units(exchange(qkv_back), 3)
        first_in = scatter(dot(proj_back, qkv_full, ((1,), (1,))))
        input_grads.append(middle_grad + norm_backward(first_in, hat_one, inv_one, norm_params[0]))
        norm_sums = norm_sums + jnp.stack(
            [
                jnp.sum(first_in * hat_one, 0),
                jnp.sum(first_in, 0),
                jnp.sum(second_in * hat_two, 0),
                jnp.sum(second_in, 0),
            ]
        )
        saved.append((rows_one, proj_back, resid_rows, attended, rows_two, up_back, back_rows, hidden))

    whole = [jnp.concatenate(parts, 0) for parts in zip(*saved)]
    rows_one, proj_back, resid_rows, attended, rows_two, up_back, back_rows, hidden = whole

    def grad(left, right):
        return lax.psum_scatter(
            dot(left, right, ((0,), (0,))).astype(BF16), "seq", scatter_dimension=0, tiled=True
        ).astype(F32)

    down_grad = grad(back_rows, hidden)
    up_grad = grad(rows_two, up_back)
    out_grad = grad(resid_rows, attended)
    qkv_grad = grad(rows_one, proj_back).reshape(w_qkv.shape)
    norm_total = lax.psum(norm_sums, ("seq", "mdl"))
    total_tokens = micro * rows * slots
    weight_rate = 0.02 * total_tokens ** (-0.5)
    norm_rate = 0.15 * total_tokens ** (-0.5)
    shape = layer_in.shape
    return (
        jnp.concatenate(outputs, 0).reshape(shape),
        jnp.concatenate(input_grads, 0).reshape(shape),
        *update_param(norm_params, norm_total, norm_moment, norm_average, norm_rate),
        *update_param(w_qkv, qkv_grad, qkv_moment, qkv_average, weight_rate),
        *update_param(w_out, out_grad, out_moment, out_average, weight_rate),
        *update_param(w_up, up_grad, up_moment, up_average, weight_rate),
        *update_param(w_down, down_grad, down_moment, down_average, weight_rate),
    )


def solution(mesh):
    slots = P(None, None, ("seq", "mdl"), None)
    wide = P("seq", None, "mdl")
    flat = P("seq", "mdl")
    return jax.shard_map(
        per_device,
        mesh=mesh,
        in_specs=(
            *(slots, P(), slots, P(), wide, flat, flat, flat),
            *(P(), P(), wide, wide, flat, flat, flat, flat, flat, flat),
        ),
        out_specs=(
            *(slots, slots, P(), P(), P(), P()),
            *(wide,) * 4,
            *(flat,) * 12,
        ),
        check_vma=False,
    )
```

time: 2180 us -> 1100 us (0.50)
  waiting for transfers between devices: 1530 us -> 652 us
  matrix products: 390 us -> 146 us
  starting transfers between devices: 5.61 us -> 55.1 us
  Pallas kernels: 0 us -> 41.2 us
  other arithmetic: 99.4 us -> 70.8 us
  local copies, waits for them, and re-layouts: 94.8 us -> 67.8 us
    reduce_scatter x28 -> x4, waiting for transfers between devices: 851 us -> 69.5 us  [grad(): lax.psum_scatter(dot(left, right, ((0,), (0,))).astype(BF16), 'seq', scat...]
    all_gather x28 -> x4, waiting for transfers between devices: 668 us -> 54.3 us  [the longest x1 54.3 us: per_device(): down_full = lax.all_gather(w_down.astype(BF16), 'seq', axis=0, tiled=True)]
    ppermute x0 -> x48, waiting for transfers between devices: none -> 459 us  [the longest x24 233 us: ring_scatter(): carried = lax.ppermute(term.astype(BF16), axis, pairs)]
    dot_general x72 -> x20, matrix products: 390 us -> 146 us  [dot(): return lax.dot_general(a, b, (dims, ((), ())), preferred_element_type=F32)]
    all_to_all x0 -> x8, waiting for transfers between devices: none -> 68.3 us  [exchange(): return lax.all_to_all(value, 'seq', 0, 0, tiled=True)]
    pallas_call x0 -> x4, Pallas kernels: none -> 41.2 us  [the longest x2 23.9 us: attention_back(): pl.pallas_call(functools.partial(attend_back_kernel, size=size, factor=HD...]
    all_to_all x0 -> x8, starting transfers between devices: none -> 33 us  [exchange(): return lax.all_to_all(value, 'seq', 0, 0, tiled=True)]
    convert_element_type x13 -> x0, local copies, waits for them, and re-layouts: 32 us -> none  [the longest x4 14.5 us: per_device(): value_part.reshape(rows, slots, -1).astype(jnp.bfloat16)]
  transfers between devices with their start and end apart: 56 -> 64, of which waited for: 51 -> 47; matrix products, arithmetic and copies ran while one was open for 23% -> 18% of each run, Pallas kernels for 0% -> 4%
where the time goes in v1:
time: 1100 us; the launch traced here: 1090 us
  waiting for transfers between devices  652 us (59%)
  matrix products  146 us (13%)
  other arithmetic  70.8 us (6%)
  local copies, waits for them, and re-layouts  67.8 us (6%)
  starting transfers between devices  55.1 us (5%)
  Pallas kernels  41.2 us (4%)
  blocking collectives  38.5 us (4%)
  between operations  23.7 us (2%)
    ppermute x24, waiting for transfers between devices, ring_scatter(): carried = lax.ppermute(term.astype(BF16), axis, pairs)  233 us
    ppermute x24, waiting for transfers between devices, ring_gather(): parts.append(lax.ppermute(parts[-1], axis, pairs))  226 us
    dot_general x20, matrix products, dot(): return lax.dot_general(a, b, (dims, ((), ())), preferred_element_type=F32)  146 us
    reduce_scatter x4, waiting for transfers between devices, grad(): lax.psum_scatter(dot(left, right, ((0,), (0,))).astype(BF16), 'seq', scat...  69.5 us
    all_to_all x8, waiting for transfers between devices, exchange(): return lax.all_to_all(value, 'seq', 0, 0, tiled=True)  68.3 us
    all_gather x1, waiting for transfers between devices, per_device(): down_full = lax.all_gather(w_down.astype(BF16), 'seq', axis=0, tiled=True)  54.3 us
    psum x1, blocking collectives, per_device(): norm_total = lax.psum(norm_sums, ('seq', 'mdl'))  38.5 us
    all_to_all x8, starting transfers between devices, exchange(): return lax.all_to_all(value, 'seq', 0, 0, tiled=True)  33 us
  transfers between devices with their start and end apart: 64, of which 47 were waited for; matrix products, arithmetic and copies ran while one was open for 18% of the time, Pallas kernels for 4%

profile of v1, /device:TPU:0, one launch (start us, length us, event | category | flops | bytes accessed | tf_op | source)
XLA Modules:
  0.0 1094.6 jit_solution(16927992020899307026)
XLA Ops:
  23.1 12.1 %collective-permute-done.12 = bf16[128,2048]{1,0:T(8,128)(2,1)} collective-permute-done((bf16[128,2048]{1,0:T(8,128)(2,1)S(1)}, bf16[128,2048]{1,0:T(8,128)(2,1)}, u32[]{:S(2)}, u32[]{:S(2)}) %collective-permute-start.12) | collective-permute-done | bytes 524320 | tf_op jit(solution)/shard_map/ppermute | solution.py:54
  35.4 11.0 %collective-permute-done = bf16[128,2048]{1,0:T(8,128)(2,1)} collective-permute-done((bf16[128,2048]{1,0:T(8,128)(2,1)S(1)}, bf16[128,2048]{1,0:T(8,128)(2,1)}, u32[]{:S(2)}, u32[]{:S(2)}) %collective-permute-start) | collective-permute-done | bytes 524320 | tf_op jit(solution)/shard_map/ppermute | solution.py:54
  46.5 11.1 %collective-permute-done.13 = bf16[128,2048]{1,0:T(8,128)(2,1)S(1)} collective-permute-done((bf16[128,2048]{1,0:T(8,128)(2,1)}, bf16[128,2048]{1,0:T(8,128)(2,1)S(1)}, u32[]{:S(2)}, u32[]{:S(2)}) %collective-permute-start.13) | collective-permute-done | bytes 524320 | tf_op jit(solution)/shard_map/ppermute | solution.py:54
  68.8 11.2 %collective-permute-done.14 = bf16[128,2048]{1,0:T(8,128)(2,1)S(1)} collective-permute-done((bf16[128,2048]{1,0:T(8,128)(2,1)S(1)}, bf16[128,2048]{1,0:T(8,128)(2,1)S(1)}, u32[]{:S(2)}, u32[]{:S(2)}) %collective-permute-start.14) | collective-permute-done | bytes 524320 | tf_op jit(solution)/shard_map/ppermute | solution.py:54
  152.3 20.7 %all-to-all-done.q_ref.k_ref.v_ref = bf16[8,3,2,4,32,128]{5,4,3,2,1,0:T(8,128)(2,1)S(1)} async-done(((bf16[8,3,2,4,32,128]{5,4,3,2,1,0:T(8,128)(2,1)}), bf16[8,3,2,4,32,128]{5,4,3,2,1,0:T(8,128)(2,1)S(1)}, u32[]{:S(2)}, u32[]{:S(2)}) %all-to-all-start) | async-done | bytes 1572896 | tf_op jit(solution)/shard_map/all_to_all | solution.py:280
  228.5 11.0 %collective-permute-done.16 = bf16[128,2048]{1,0:T(8,128)(2,1)S(1)} collective-permute-done((bf16[128,2048]{1,0:T(8,128)(2,1)S(1)}, bf16[128,2048]{1,0:T(8,128)(2,1)S(1)}, u32[]{:S(2)}, u32[]{:S(2)}) %collective-permute-start.16) | collective-permute-done | bytes 524320 | tf_op jit(solution)/shard_map/ppermute | solution.py:66
  239.9 22.1 %collective-permute-done.4 = bf16[128,2048]{1,0:T(8,128)(2,1)S(1)} collective-permute-done((bf16[128,2048]{1,0:T(8,128)(2,1)S(1)}, bf16[128,2048]{1,0:T(8,128)(2,1)S(1)}, u32[]{:S(2)}, u32[]{:S(2)}) %collective-permute-start.4) | collective-permute-done | bytes 524320 | tf_op jit(solution)/shard_map/ppermute | solution.py:66
  262.2 11.0 %collective-permute-done.17 = bf16[128,2048]{1,0:T(8,128)(2,1)S(1)} collective-permute-done((bf16[128,2048]{1,0:T(8,128)(2,1)S(1)}, bf16[128,2048]{1,0:T(8,128)(2,1)S(1)}, u32[]{:S(2)}, u32[]{:S(2)}) %collective-permute-start.17) | collective-permute-done | bytes 524320 | tf_op jit(solution)/shard_map/ppermute | solution.py:66
  273.8 21.3 %collective-permute-done.5 = bf16[128,2048]{1,0:T(8,128)(2,1)S(1)} collective-permute-done((bf16[128,2048]{1,0:T(8,128)(2,1)S(1)}, bf16[128,2048]{1,0:T(8,128)(2,1)S(1)}, u32[]{:S(2)}, u32[]{:S(2)}) %collective-permute-start.5) | collective-permute-done | bytes 524320 | tf_op jit(solution)/shard_map/ppermute | solution.py:66
  301.4 11.7 %collective-permute-done.18 = bf16[128,2048]{1,0:T(8,128)(2,1)S(1)} collective-permute-done((bf16[128,2048]{1,0:T(8,128)(2,1)S(1)}, bf16[128,2048]{1,0:T(8,128)(2,1)S(1)}, u32[]{:S(2)}, u32[]{:S(2)}) %collective-permute-start.18) | collective-permute-done | bytes 524320 | tf_op jit(solution)/shard_map/ppermute | solution.py:54
  313.1 11.2 %collective-permute-done.25 = bf16[128,2048]{1,0:T(8,128)(2,1)S(1)} collective-permute-done((bf16[128,2048]{1,0:T(8,128)(2,1)S(1)}, bf16[128,2048]{1,0:T(8,128)(2,1)S(1)}, u32[]{:S(2)}, u32[]{:S(2)}) %collective-permute-start.25) | collective-permute-done | bytes 524320 | tf_op jit(solution)/shard_map/ppermute | solution.py:54
  324.3 11.2 %collective-permute-done.37 = bf16[128,2048]{1,0:T(8,128)(2,1)S(1)} collective-permute-done((bf16[128,2048]{1,0:T(8,128)(2,1)S(1)}, bf16[128,2048]{1,0:T(8,128)(2,1)S(1)}, u32[]{:S(2)}, u32[]{:S(2)}) %collective-permute-start.37) | collective-permute-done | bytes 524320 | tf_op jit(solution)/shard_map/ppermute | solution.py:54
  335.6 11.2 %collective-permute-done.6 = bf16[128,2048]{1,0:T(8,128)(2,1)S(1)} collective-permute-done((bf16[128,2048]{1,0:T(8,128)(2,1)S(1)}, bf16[128,2048]{1,0:T(8,128)(2,1)S(1)}, u32[]{:S(2)}, u32[]{:S(2)}) %collective-permute-start.6) | collective-permute-done | bytes 524320 | tf_op jit(solution)/shard_map/ppermute | solution.py:54
  347.0 11.1 %collective-permute-done.19 = bf16[128,2048]{1,0:T(8,128)(2,1)S(1)} collective-permute-done((bf16[128,2048]{1,0:T(8,128)(2,1)S(1)}, bf16[128,2048]{1,0:T(8,128)(2,1)S(1)}, u32[]{:S(2)}, u32[]{:S(2)}) %collective-permute-start.19) | collective-permute-done | bytes 524320 | tf_op jit(solution)/shard_map/ppermute | solution.py:54
  358.0 11.2 %collective-permute-done.26 = bf16[128,2048]{1,0:T(8,128)(2,1)S(1)} collective-permute-done((bf16[128,2048]{1,0:T(8,128)(2,1)S(1)}, bf16[128,2048]{1,0:T(8,128)(2,1)S(1)}, u32[]{:S(2)}, u32[]{:S(2)}) %collective-permute-start.26) | collective-permute-done | bytes 524320 | tf_op jit(solution)/shard_map/ppermute | solution.py:54
  370.9 20.9 %collective-permute-done.7 = bf16[128,2048]{1,0:T(8,128)(2,1)S(1)} collective-permute-done((bf16[128,2048]{1,0:T(8,128)(2,1)S(1)}, bf16[128,2048]{1,0:T(8,128)(2,1)S(1)}, u32[]{:S(2)}, u32[]{:S(2)}) %collective-permute-start.7) | collective-permute-done | bytes 524320 | tf_op jit(solution)/shard_map/ppermute | solution.py:54
  433.1 11.4 %convolution_convert_fusion = bf16[2048,2048]{1,0:T(8,128)(2,1)} fusion(bf16[512,2048]{1,0:T(8,128)(2,1)S(1)} %bitcast.200, bf16[512,2048]{1,0:T(8,128)(2,1)S(1)} %bitcast.196, bf16[512,2048]{1,0:T(8,128)(2,1)S(1)} %get-tuple-element.174, bf16[512,2048]{1,0:T(8,128)(2,1)S(1)} %get-tuple-element.176), kind=kOutput, calls=%fused_computation.1 | convolution fusion | flops 8610906112 | bytes 16777216 | tf_op jit(solution)/shard_map/dot_general | solution.py:46
  444.6 69.5 %reduce-scatter.11.cloned.1.call-done = bf16[256,2048]{1,0:T(8,128)(2,1)} async-done(((bf16[2048,2048]{1,0:T(8,128)(2,1)}), bf16[256,2048]{1,0:T(8,128)(2,1)}) %reduce-scatter.11.cloned.1.call-update) | async-done | bytes 1048592 | tf_op jit(solution)/shard_map/reduce_scatter | solution.py:347
  521.1 54.3 %all-gather.11.cloned.1.call-done = bf16[2048,2048]{1,0:T(8,128)(2,1)} async-done(((bf16[256,2048]{1,0:T(8,128)(2,1)}), bf16[2048,2048]{1,0:T(8,128)(2,1)}) %all-gather.11.cloned.1.call-update) | async-done | bytes 8388624 | tf_op jit(solution)/shard_map/all_gather | solution.py:277
  646.3 11.1 %collective-permute-done.40 = bf16[128,2048]{1,0:T(8,128)(2,1)S(1)} collective-permute-done((bf16[128,2048]{1,0:T(8,128)(2,1)S(1)}, bf16[128,2048]{1,0:T(8,128)(2,1)S(1)}, u32[]{:S(2)}, u32[]{:S(2)}) %collective-permute-start.40) | collective-permute-done | bytes 524320 | tf_op jit(solution)/shard_map/ppermute | solution.py:66
  657.6 22.3 %collective-permute-done.28 = bf16[128,2048]{1,0:T(8,128)(2,1)S(1)} collective-permute-done((bf16[128,2048]{1,0:T(8,128)(2,1)S(1)}, bf16[128,2048]{1,0:T(8,128)(2,1)S(1)}, u32[]{:S(2)}, u32[]{:S(2)}) %collective-permute-start.28) | collective-permute-done | bytes 524320 | tf_op jit(solution)/shard_map/ppermute | solution.py:66
  691.3 22.3 %collective-permute-done.29 = bf16[128,2048]{1,0:T(8,128)(2,1)S(1)} collective-permute-done((bf16[128,2048]{1,0:T(8,128)(2,1)S(1)}, bf16[128,2048]{1,0:T(8,128)(2,1)S(1)}, u32[]{:S(2)}, u32[]{:S(2)}) %collective-permute-start.29) | collective-permute-done | bytes 524320 | tf_op jit(solution)/shard_map/ppermute | solution.py:66
  747.3 11.2 %collective-permute-done.42 = bf16[128,2048]{1,0:T(8,128)(2,1)S(1)} collective-permute-done((bf16[128,2048]{1,0:T(8,128)(2,1)S(1)}, bf16[128,2048]{1,0:T(8,128)(2,1)S(1)}, u32[]{:S(2)}, u32[]{:S(2)}) %collective-permute-start.42) | collective-permute-done | bytes 524320 | tf_op jit(solution)/shard_map/ppermute | solution.py:54
  758.5 11.2 %collective-permute-done.31 = bf16[128,2048]{1,0:T(8,128)(2,1)S(1)} collective-permute-done((bf16[128,2048]{1,0:T(8,128)(2,1)S(1)}, bf16[128,2048]{1,0:T(8,128)(2,1)S(1)}, u32[]{:S(2)}, u32[]{:S(2)}) %collective-permute-start.31) | collective-permute-done | bytes 524320 | tf_op jit(solution)/shard_map/ppermute | solution.py:54
  769.7 11.2 %collective-permute-done.43 = bf16[128,2048]{1,0:T(8,128)(2,1)S(1)} collective-permute-done((bf16[128,2048]{1,0:T(8,128)(2,1)S(1)}, bf16[128,2048]{1,0:T(8,128)(2,1)S(1)}, u32[]{:S(2)}, u32[]{:S(2)}) %collective-permute-start.43) | collective-permute-done | bytes 524320 | tf_op jit(solution)/shard_map/ppermute | solution.py:54
  807.6 14.2 %convolution_convert_fusion.1 = bf16[2048,2048]{1,0:T(8,128)(2,1)} fusion(bf16[512,2048]{1,0:T(8,128)(2,1)} %bitcast.192, bf16[512,2048]{1,0:T(8,128)(2,1)} %bitcast.193, bf16[512,2048]{1,0:T(8,128)(2,1)} %copy-done.84, bf16[512,2048]{1,0:T(8,128)(2,1)} %fusion.5), kind=kOutput, calls=%fused_computation.2 | convolution fusion | flops 8610906112 | bytes 16777216 | tf_op jit(solution)/shard_map/dot_general | solution.py:46
  850.2 11.5 %attend_back.2 = bf16[8,3,2,4,32,128]{5,4,3,2,1,0:T(8,128)(2,1)S(1)} custom-call(s32[1024,1]{1,0:T(8,128)S(1)} %copy-done.3, s32[2,2,1024]{2,1,0:T(2,128)S(1)} %get-tuple-element.153.meta_ref, f32[2,2,1024]{2,1,0:T(2,128)S(1)} %get-tuple-element.28.lse_ref, bf16[8,3,2,4,32,128]{5,4,3,2,1,0:T(8,128)(2,1)S(1)} %all-to-all-done.q_ref.k_ref.v_ref, ...), custom_call_target="tpu_custom_call" | custom-call | flops 6710886400 | bytes 4194304 | tf_op jit(solution)/shard_map/attend_back/pallas_call | solution.py:197
  867.4 12.4 %attend_back.3 = bf16[8,3,2,4,32,128]{5,4,3,2,1,0:T(8,128)(2,1)} custom-call(s32[1024,1]{1,0:T(8,128)S(1)} %copy-done.4, s32[2,2,1024]{2,1,0:T(2,128)S(1)} %copy-done.8, f32[2,2,1024]{2,1,0:T(2,128)S(1)} %get-tuple-element.29.lse_ref, bf16[8,3,2,4,32,128]{5,4,3,2,1,0:T(8,128)(2,1)S(1)} %all-to-all-done.2.q_ref.k_ref.v_ref, ...), custom_call_target="tpu_custom_call" | custom-call | flops 6710886400 | bytes 4194304 | tf_op jit(solution)/shard_map/attend_back/pallas_call | solution.py:197
  879.7 19.6 %all-to-all-done.5 = bf16[8,3,2,4,32,128]{5,4,3,2,1,0:T(8,128)(2,1)} async-done(((bf16[8,3,2,4,32,128]{5,4,3,2,1,0:T(8,128)(2,1)}), bf16[8,3,2,4,32,128]{5,4,3,2,1,0:T(8,128)(2,1)}, u32[]{:S(2)}, u32[]{:S(2)}) %all-to-all-start.5) | async-done | bytes 1572896 | tf_op jit(solution)/shard_map/all_to_all | solution.py:280
  912.2 15.4 %all-to-all-done.7 = bf16[8,3,2,4,32,128]{5,4,3,2,1,0:T(8,128)(2,1)S(1)} async-done(((bf16[8,3,2,4,32,128]{5,4,3,2,1,0:T(8,128)(2,1)}), bf16[8,3,2,4,32,128]{5,4,3,2,1,0:T(8,128)(2,1)S(1)}, u32[]{:S(2)}, u32[]{:S(2)}) %all-to-all-start.7) | async-done | bytes 1572896 | tf_op jit(solution)/shard_map/all_to_all | solution.py:280
  964.1 11.0 %collective-permute-done.45 = bf16[128,2048]{1,0:T(8,128)(2,1)S(1)} collective-permute-done((bf16[128,2048]{1,0:T(8,128)(2,1)S(1)}, bf16[128,2048]{1,0:T(8,128)(2,1)S(1)}, u32[]{:S(2)}, u32[]{:S(2)}) %collective-permute-start.45) | collective-permute-done | bytes 524320 | tf_op jit(solution)/shard_map/ppermute | solution.py:66
  1021.4 38.5 %psum.7 = f32[4,2048]{1,0:T(4,128)S(1)} all-reduce(f32[4,2048]{1,0:T(4,128)S(1)} %maximum_add_fusion), channel_id=1, replica_groups=mesh['seq'=8,'mdl'=4] {'seq','mdl'}, use_global_device_ids=true, to_apply=%region_25.26 | all-reduce | flops 8192 | bytes 65536 | tf_op jit(solution)/shard_map/psum | solution.py:355
  (436 shorter events, 503.6 us)
Async XLA Ops:
  7.2 74.2 %all-gather.5.cloned.1.call-start = ((), (), s32[]{:S(2)}) async-start(), calls=%async_computation.12 | async-start | bytes 7077888 | tf_op jit(solution)/shard_map/all_gather | solution.py:274
  10.1 184.1 %all-gather.7.cloned.1.call-start = ((), (), s32[]{:S(2)}) async-start(), calls=%async_computation.13 | async-start | bytes 2359296 | tf_op jit(solution)/shard_map/all_gather | solution.py:275
  11.3 403.0 %all-gather.9.cloned.1.call-start = ((), (), s32[]{:S(2)}) async-start(), calls=%async_computation.14 | async-start | bytes 9437184 | tf_op jit(solution)/shard_map/all_gather | solution.py:276
  68.8 37.2 %collective-permute-start.2 = (bf16[128,2048]{1,0:T(8,128)(2,1)S(1)}, bf16[128,2048]{1,0:T(8,128)(2,1)}, u32[]{:S(2)}, u32[]{:S(2)}) collective-permute-start(bf16[128,2048]{1,0:T(8,128)(2,1)S(1)} %collective-permute-done.1), channel_id=1, source_target_pairs={{0,1},{1,2},{2,3},{3,0},{4,5},{5,6},{6,7},{7,4},{8,9},{9,10},{10,1... | collective-permute-start | bytes 1572872 | tf_op jit(solution)/shard_map/ppermute | solution.py:54
  94.6 36.3 %all-to-all-start.2 = ((bf16[8,3,2,4,32,128]{5,4,3,2,1,0:T(8,128)(2,1)}), bf16[8,3,2,4,32,128]{5,4,3,2,1,0:T(8,128)(2,1)S(1)}, u32[]{:S(2)}, u32[]{:S(2)}) async-start(bf16[8,3,2,4,32,128]{5,4,3,2,1,0:T(8,128)(2,1)} %bitcast.35), calls=%async_computation.2 | async-start | bytes 3145728 | tf_op jit(solution)/shard_map/all_to_all | solution.py:280
  130.9 42.1 %all-to-all-start = ((bf16[8,3,2,4,32,128]{5,4,3,2,1,0:T(8,128)(2,1)}), bf16[8,3,2,4,32,128]{5,4,3,2,1,0:T(8,128)(2,1)S(1)}, u32[]{:S(2)}, u32[]{:S(2)}) async-start(bf16[8,3,2,4,32,128]{5,4,3,2,1,0:T(8,128)(2,1)} %bitcast.182), calls=%async_computation | async-start | bytes 3145728 | tf_op jit(solution)/shard_map/all_to_all | solution.py:280
  191.9 322.1 %reduce-scatter.11.cloned.1.call-start = ((), (), s32[]{:S(2)}) async-start(), calls=%async_computation.19 | async-start | bytes 9437184 | tf_op jit(solution)/shard_map/reduce_scatter | solution.py:347
  218.7 77.8 %collective-permute-start.24 = (bf16[128,2048]{1,0:T(8,128)(2,1)S(1)}, bf16[128,2048]{1,0:T(8,128)(2,1)S(1)}, u32[]{:S(2)}, u32[]{:S(2)}) collective-permute-start(bf16[128,2048]{1,0:T(8,128)(2,1)S(1)} %bitcast_convert_fusion.1), channel_id=1, source_target_pairs={{0,1},{1,2},{2,3},{3,0},{4,5},{5,6},{6,7},{7,4},{8,9},{9,10},{10,1... | collective-permute-start | bytes 1572872 | tf_op jit(solution)/shard_map/ppermute | solution.py:54
  228.4 33.6 %collective-permute-start.4 = (bf16[128,2048]{1,0:T(8,128)(2,1)S(1)}, bf16[128,2048]{1,0:T(8,128)(2,1)S(1)}, u32[]{:S(2)}, u32[]{:S(2)}) collective-permute-start(bf16[128,2048]{1,0:T(8,128)(2,1)S(1)} %fusion.58), channel_id=1, source_target_pairs={{0,1},{1,2},{2,3},{3,0},{4,5},{5,6},{6,7},{7,4},{8,9},{9,10},{10,1... | collective-permute-start | bytes 1572872 | tf_op jit(solution)/shard_map/ppermute | solution.py:66
  239.7 33.6 %collective-permute-start.17 = (bf16[128,2048]{1,0:T(8,128)(2,1)S(1)}, bf16[128,2048]{1,0:T(8,128)(2,1)S(1)}, u32[]{:S(2)}, u32[]{:S(2)}) collective-permute-start(bf16[128,2048]{1,0:T(8,128)(2,1)S(1)} %fusion.53), channel_id=1, source_target_pairs={{0,1},{1,2},{2,3},{3,0},{4,5},{5,6},{6,7},{7,4},{8,9},{9,10},{10,1... | collective-permute-start | bytes 1572872 | tf_op jit(solution)/shard_map/ppermute | solution.py:66
  239.8 56.7 %collective-permute-start.36 = (bf16[128,2048]{1,0:T(8,128)(2,1)S(1)}, bf16[128,2048]{1,0:T(8,128)(2,1)S(1)}, u32[]{:S(2)}, u32[]{:S(2)}) collective-permute-start(bf16[128,2048]{1,0:T(8,128)(2,1)S(1)} %bitcast_convert_fusion), channel_id=1, source_target_pairs={{0,1},{1,2},{2,3},{3,0},{4,5},{5,6},{6,7},{7,4},{8,9},{9,10},{10,1... | collective-permute-start | bytes 1572872 | tf_op jit(solution)/shard_map/ppermute | solution.py:54
  262.1 33.0 %collective-permute-start.5 = (bf16[128,2048]{1,0:T(8,128)(2,1)S(1)}, bf16[128,2048]{1,0:T(8,128)(2,1)S(1)}, u32[]{:S(2)}, u32[]{:S(2)}) collective-permute-start(bf16[128,2048]{1,0:T(8,128)(2,1)S(1)} %fusion.59), channel_id=1, source_target_pairs={{0,1},{1,2},{2,3},{3,0},{4,5},{5,6},{6,7},{7,4},{8,9},{9,10},{10,1... | collective-permute-start | bytes 1572872 | tf_op jit(solution)/shard_map/ppermute | solution.py:66
  296.5 39.1 %collective-permute-start.37 = (bf16[128,2048]{1,0:T(8,128)(2,1)S(1)}, bf16[128,2048]{1,0:T(8,128)(2,1)S(1)}, u32[]{:S(2)}, u32[]{:S(2)}) collective-permute-start(bf16[128,2048]{1,0:T(8,128)(2,1)S(1)} %collective-permute-done.36), channel_id=1, source_target_pairs={{0,1},{1,2},{2,3},{3,0},{4,5},{5,6},{6,7},{7,4},{8,9},{9,10},{10,1... | collective-permute-start | bytes 1572872 | tf_op jit(solution)/shard_map/ppermute | solution.py:54
  297.2 49.6 %collective-permute-start.6 = (bf16[128,2048]{1,0:T(8,128)(2,1)S(1)}, bf16[128,2048]{1,0:T(8,128)(2,1)S(1)}, u32[]{:S(2)}, u32[]{:S(2)}) collective-permute-start(bf16[128,2048]{1,0:T(8,128)(2,1)S(1)} %get-tuple-element.159), channel_id=1, source_target_pairs={{0,1},{1,2},{2,3},{3,0},{4,5},{5,6},{6,7},{7,4},{8,9},{9,10},{10,1... | collective-permute-start | bytes 1572872 | tf_op jit(solution)/shard_map/ppermute | solution.py:54
  313.1 44.9 %collective-permute-start.19 = (bf16[128,2048]{1,0:T(8,128)(2,1)S(1)}, bf16[128,2048]{1,0:T(8,128)(2,1)S(1)}, u32[]{:S(2)}, u32[]{:S(2)}) collective-permute-start(bf16[128,2048]{1,0:T(8,128)(2,1)S(1)} %collective-permute-done.18), channel_id=1, source_target_pairs={{0,1},{1,2},{2,3},{3,0},{4,5},{5,6},{6,7},{7,4},{8,9},{9,10},{10,1... | collective-permute-start | bytes 1572872 | tf_op jit(solution)/shard_map/ppermute | solution.py:54
  324.3 44.9 %collective-permute-start.26 = (bf16[128,2048]{1,0:T(8,128)(2,1)S(1)}, bf16[128,2048]{1,0:T(8,128)(2,1)S(1)}, u32[]{:S(2)}, u32[]{:S(2)}) collective-permute-start(bf16[128,2048]{1,0:T(8,128)(2,1)S(1)} %collective-permute-done.25), channel_id=1, source_target_pairs={{0,1},{1,2},{2,3},{3,0},{4,5},{5,6},{6,7},{7,4},{8,9},{9,10},{10,1... | collective-permute-start | bytes 1572872 | tf_op jit(solution)/shard_map/ppermute | solution.py:54
  335.6 56.2 %collective-permute-start.38 = (bf16[128,2048]{1,0:T(8,128)(2,1)S(1)}, bf16[128,2048]{1,0:T(8,128)(2,1)S(1)}, u32[]{:S(2)}, u32[]{:S(2)}) collective-permute-start(bf16[128,2048]{1,0:T(8,128)(2,1)S(1)} %collective-permute-done.37), channel_id=1, source_target_pairs={{0,1},{1,2},{2,3},{3,0},{4,5},{5,6},{6,7},{7,4},{8,9},{9,10},{10,1... | collective-permute-start | bytes 1572872 | tf_op jit(solution)/shard_map/ppermute | solution.py:54
  346.8 44.9 %collective-permute-start.7 = (bf16[128,2048]{1,0:T(8,128)(2,1)S(1)}, bf16[128,2048]{1,0:T(8,128)(2,1)S(1)}, u32[]{:S(2)}, u32[]{:S(2)}) collective-permute-start(bf16[128,2048]{1,0:T(8,128)(2,1)S(1)} %collective-permute-done.6), channel_id=1, source_target_pairs={{0,1},{1,2},{2,3},{3,0},{4,5},{5,6},{6,7},{7,4},{8,9},{9,10},{10,1... | collective-permute-start | bytes 1572872 | tf_op jit(solution)/shard_map/ppermute | solution.py:54
  358.0 44.9 %collective-permute-start.20 = (bf16[128,2048]{1,0:T(8,128)(2,1)S(1)}, bf16[128,2048]{1,0:T(8,128)(2,1)S(1)}, u32[]{:S(2)}, u32[]{:S(2)}) collective-permute-start(bf16[128,2048]{1,0:T(8,128)(2,1)S(1)} %collective-permute-done.19), channel_id=1, source_target_pairs={{0,1},{1,2},{2,3},{3,0},{4,5},{5,6},{6,7},{7,4},{8,9},{9,10},{10,1... | collective-permute-start | bytes 1572872 | tf_op jit(solution)/shard_map/ppermute | solution.py:54
  444.5 130.9 %all-gather.11.cloned.1.call-start = ((), (), s32[]{:S(2)}) async-start(), calls=%async_computation.15 | async-start | bytes 9437184 | tf_op jit(solution)/shard_map/all_gather | solution.py:277
  520.9 477.9 %reduce-scatter.7.cloned.1.call-start = ((), (), s32[]{:S(2)}) async-start(), calls=%async_computation.17 | async-start | bytes 2359296 | tf_op jit(solution)/shard_map/reduce_scatter | solution.py:347
  592.4 35.0 %collective-permute-start.39 = (bf16[128,2048]{1,0:T(8,128)(2,1)S(1)}, bf16[128,2048]{1,0:T(8,128)(2,1)}, u32[]{:S(2)}, u32[]{:S(2)}) collective-permute-start(bf16[128,2048]{1,0:T(8,128)(2,1)S(1)} %slice.395), channel_id=1, source_target_pairs={{0,1},{1,2},{2,3},{3,0},{4,5},{5,6},{6,7},{7,4},{8,9},{9,10},{10,1... | collective-permute-start | bytes 1572872 | tf_op jit(solution)/shard_map/ppermute | solution.py:66
  631.2 48.8 %collective-permute-start.10 = (bf16[128,2048]{1,0:T(8,128)(2,1)S(1)}, bf16[128,2048]{1,0:T(8,128)(2,1)S(1)}, u32[]{:S(2)}, u32[]{:S(2)}) collective-permute-start(bf16[128,2048]{1,0:T(8,128)(2,1)S(1)} %fusion.55), channel_id=1, source_target_pairs={{0,1},{1,2},{2,3},{3,0},{4,5},{5,6},{6,7},{7,4},{8,9},{9,10},{10,1... | collective-permute-start | bytes 1572872 | tf_op jit(solution)/shard_map/ppermute | solution.py:66
  636.2 43.7 %collective-permute-start.28 = (bf16[128,2048]{1,0:T(8,128)(2,1)S(1)}, bf16[128,2048]{1,0:T(8,128)(2,1)S(1)}, u32[]{:S(2)}, u32[]{:S(2)}) collective-permute-start(bf16[128,2048]{1,0:T(8,128)(2,1)S(1)} %fusion.47), channel_id=1, source_target_pairs={{0,1},{1,2},{2,3},{3,0},{4,5},{5,6},{6,7},{7,4},{8,9},{9,10},{10,1... | collective-permute-start | bytes 1572872 | tf_op jit(solution)/shard_map/ppermute | solution.py:66
  646.3 44.8 %collective-permute-start.22 = (bf16[128,2048]{1,0:T(8,128)(2,1)S(1)}, bf16[128,2048]{1,0:T(8,128)(2,1)S(1)}, u32[]{:S(2)}, u32[]{:S(2)}) collective-permute-start(bf16[128,2048]{1,0:T(8,128)(2,1)S(1)} %fusion.49), channel_id=1, source_target_pairs={{0,1},{1,2},{2,3},{3,0},{4,5},{5,6},{6,7},{7,4},{8,9},{9,10},{10,1... | collective-permute-start | bytes 1572872 | tf_op jit(solution)/shard_map/ppermute | solution.py:66
  657.5 56.6 %collective-permute-start.41 = (bf16[128,2048]{1,0:T(8,128)(2,1)S(1)}, bf16[128,2048]{1,0:T(8,128)(2,1)S(1)}, u32[]{:S(2)}, u32[]{:S(2)}) collective-permute-start(bf16[128,2048]{1,0:T(8,128)(2,1)S(1)} %fusion.44), channel_id=1, source_target_pairs={{0,1},{1,2},{2,3},{3,0},{4,5},{5,6},{6,7},{7,4},{8,9},{9,10},{10,1... | collective-permute-start | bytes 1572872 | tf_op jit(solution)/shard_map/ppermute | solution.py:66
  680.0 33.6 %collective-permute-start.29 = (bf16[128,2048]{1,0:T(8,128)(2,1)S(1)}, bf16[128,2048]{1,0:T(8,128)(2,1)S(1)}, u32[]{:S(2)}, u32[]{:S(2)}) collective-permute-start(bf16[128,2048]{1,0:T(8,128)(2,1)S(1)} %fusion.48), channel_id=1, source_target_pairs={{0,1},{1,2},{2,3},{3,0},{4,5},{5,6},{6,7},{7,4},{8,9},{9,10},{10,1... | collective-permute-start | bytes 1572872 | tf_op jit(solution)/shard_map/ppermute | solution.py:66
  680.2 44.6 %collective-permute-start.11 = (bf16[128,2048]{1,0:T(8,128)(2,1)S(1)}, bf16[128,2048]{1,0:T(8,128)(2,1)S(1)}, u32[]{:S(2)}, u32[]{:S(2)}) collective-permute-start(bf16[128,2048]{1,0:T(8,128)(2,1)S(1)} %fusion.56), channel_id=1, source_target_pairs={{0,1},{1,2},{2,3},{3,0},{4,5},{5,6},{6,7},{7,4},{8,9},{9,10},{10,1... | collective-permute-start | bytes 1572872 | tf_op jit(solution)/shard_map/ppermute | solution.py:66
  691.2 44.8 %collective-permute-start.23 = (bf16[128,2048]{1,0:T(8,128)(2,1)S(1)}, bf16[128,2048]{1,0:T(8,128)(2,1)S(1)}, u32[]{:S(2)}, u32[]{:S(2)}) collective-permute-start(bf16[128,2048]{1,0:T(8,128)(2,1)S(1)} %fusion.50), channel_id=1, source_target_pairs={{0,1},{1,2},{2,3},{3,0},{4,5},{5,6},{6,7},{7,4},{8,9},{9,10},{10,1... | collective-permute-start | bytes 1572872 | tf_op jit(solution)/shard_map/ppermute | solution.py:66
  807.5 257.4 %reduce-scatter.9.cloned.1.call-start = ((), (), s32[]{:S(2)}) async-start(), calls=%async_computation.18 | async-start | bytes 9437184 | tf_op jit(solution)/shard_map/reduce_scatter | solution.py:347
  862.9 36.4 %all-to-all-start.5 = ((bf16[8,3,2,4,32,128]{5,4,3,2,1,0:T(8,128)(2,1)}), bf16[8,3,2,4,32,128]{5,4,3,2,1,0:T(8,128)(2,1)}, u32[]{:S(2)}, u32[]{:S(2)}) async-start(bf16[8,3,2,4,32,128]{5,4,3,2,1,0:T(8,128)(2,1)} %copy-done), calls=%async_computation.5 | async-start | bytes 3145728 | tf_op jit(solution)/shard_map/all_to_all | solution.py:280
  902.9 169.4 %reduce-scatter.5.cloned.1.call-start = ((), (), s32[]{:S(2)}) async-start(), calls=%async_computation.16 | async-start | bytes 7077888 | tf_op jit(solution)/shard_map/reduce_scatter | solution.py:347
  (120 other events, 1952.2 us)
Sparse Core Ops, SparseCore 0:
  10.5 49.3 all-gather.4
  62.3 27.8 all-gather.6
  92.7 84.6 all-gather.8
  444.7 69.3 reduce-scatter.10
  521.0 54.3 all-gather.10
  807.7 39.6 reduce-scatter.6
  850.8 92.5 reduce-scatter.8
  947.2 61.7 reduce-scatter.4

commit v2 on v1

--- a/solution.py
+++ b/solution.py
@@ -9,7 +9,7 @@
 
 HD = 64
 LANES = 128
-CHUNKS = 2
+CHUNKS = 1
 
 EPSILON = 1e-05
 HALF_ROOT = 0.7071067811865476
@@ -46,25 +46,18 @@
     return lax.dot_general(a, b, (dims, ((), ())), preferred_element_type=F32)
 
 
-def ring_gather(block, axis):
-    count = lax.axis_size(axis)
-    pairs = [(i, (i + 1) % count) for i in range(count)]
-    parts = [block]
-    for _ in range(count - 1):
-        parts.append(lax.ppermute(parts[-1], axis, pairs))
-    return jnp.stack(parts)
-
-
-def ring_scatter(parts, axis):
-    count = lax.axis_size(axis)
-    pairs = [(i, (i + 1) % count) for i in range(count)]
-    carried = None
-    for j in range(1, count):
-        term = parts[j]
-        if carried is not None:
-            term = term + carried.astype(F32)
-        carried = lax.ppermute(term.astype(BF16), axis, pairs)
-    return parts[0] + carried.astype(F32)
+def tied(value, earlier):
+    return lax.optimization_barrier((value, earlier))
+
+
+def whole_sum(value, axes):
+    for axis in axes:
+        count = lax.axis_size(axis)
+        step = 1
+        while step < count:
+            value = value + lax.ppermute(value, axis, [(i, i ^ step) for i in range(count)])
+            step *= 2
+    return value
 
 
 def score_blocks(keys, queries, kpos, first, last, start, size):
@@ -77,9 +70,11 @@
     return [jnp.where(kpos[:start] >= first, ahead, -1e30), diag]
 
 
-def attend_kernel(kpos_ref, meta_ref, q_ref, k_ref, v_ref, o_ref, lse_ref, *, size, factor):
+def attend_kernel(own_ref, kpos_ref, meta_ref, q_ref, k_ref, v_ref, o_ref, lse_ref, *, size, factor):
     slots = kpos_ref.shape[0]
-    per = q_ref.shape[1] * q_ref.shape[2]
+    count, short = q_ref.shape[1:3]
+    per = count * short
+    own = own_ref[0]
     heads = LANES // HD
     keys = k_ref[...].reshape(slots, LANES)
     values = v_ref[...].reshape(slots, LANES)
@@ -107,14 +102,20 @@
                 out = term if out is None else out + term
             outs.append(out)
         merged = jnp.concatenate(outs, 0).T.astype(BF16)
-        o_ref[span] = merged.reshape(size // per, *o_ref.shape[1:])
+        for j in range(count):
+            place = lax.rem(own + (count - j), count)
+            for k in range(size // per):
+                rows = slice(k * per + j * short, k * per + (j + 1) * short)
+                o_ref[start // per + k, place] = merged[rows]
 
 
 def attend_back_kernel(
-    kpos_ref, meta_ref, lse_ref, q_ref, k_ref, v_ref, g_ref, out_ref, dk_acc, dv_acc, *, size, factor
+    own_ref, kpos_ref, meta_ref, lse_ref, q_ref, k_ref, v_ref, g_ref, out_ref, dk_acc, dv_acc, *, size, factor
 ):
     slots = kpos_ref.shape[0]
-    per = q_ref.shape[1] * q_ref.shape[2]
+    count, short = q_ref.shape[1:3]
+    per = count * short
+    own = own_ref[0]
     heads = LANES // HD
     keys = k_ref[...].reshape(slots, LANES)
     values = v_ref[...].reshape(slots, LANES)
@@ -124,7 +125,14 @@
     for start in range(0, slots, size):
         span = pl.ds(start // per, size // per)
         queries = q_ref[span].reshape(size, LANES) * factor
-        upstream = g_ref[span].reshape(size, LANES)
+        upstream = jnp.concatenate(
+            [
+                g_ref[start // per + k, lax.rem(own + (count - j), count)]
+                for k in range(size // per)
+                for j in range(count)
+            ],
+            0,
+        )
         first = meta_ref[0:1, start : start + size]
         last = meta_ref[1:2, start : start + size]
         dqs, dks, dvs = [], [], []
@@ -160,7 +168,7 @@
     )
 
 
-def attention(qkv, kpos, meta, size):
+def attention(own, qkv, kpos, meta, size):
     seq, _, units, blocks, short, lanes = qkv.shape
     slots = kpos.shape[0]
     heads = LANES // HD
@@ -169,16 +177,17 @@
         functools.partial(attend_kernel, size=size, factor=HD**-0.5),
         grid=(units,),
         in_specs=[
+            pl.BlockSpec(memory_space=pltpu.SMEM),
             pl.BlockSpec((slots, 1), lambda r: (0, 0)),
             pl.BlockSpec((None, 2, slots), lambda r: (r, 0, 0)),
             *(kind_spec(qkv.shape, kind) for kind in range(3)),
         ],
         out_specs=[
-            pl.BlockSpec((seq, None, blocks, short, lanes), lambda r: (0, r, 0, 0, 0)),
+            pl.BlockSpec((seq, blocks, None, short, lanes), lambda r: (0, 0, r, 0, 0)),
             pl.BlockSpec((None, heads, slots), lambda r: (r, 0, 0)),
         ],
         out_shape=[
-            jax.ShapeDtypeStruct((seq, units, blocks, short, lanes), BF16),
+            jax.ShapeDtypeStruct((seq, blocks, units, short, lanes), BF16),
             jax.ShapeDtypeStruct((units, heads, slots), F32),
         ],
         compiler_params=pltpu.CompilerParams(vmem_limit_bytes=48 << 20),
@@ -186,10 +195,10 @@
             flops=work * HD * 4 * 4, bytes_accessed=units * slots * LANES * 8, transcendentals=work
         ),
         name="attend",
-    )(kpos, meta, qkv, qkv, qkv)
-
-
-def attention_back(qkv, upstream, lse, kpos, meta, size):
+    )(own, kpos, meta, qkv, qkv, qkv)
+
+
+def attention_back(own, qkv, upstream, lse, kpos, meta, size):
     seq, _, units, blocks, short, lanes = qkv.shape
     slots = kpos.shape[0]
     heads = LANES // HD
@@ -198,11 +207,12 @@
         functools.partial(attend_back_kernel, size=size, factor=HD**-0.5),
         grid=(units,),
         in_specs=[
+            pl.BlockSpec(memory_space=pltpu.SMEM),
             pl.BlockSpec((slots, 1), lambda r: (0, 0)),
             pl.BlockSpec((None, 2, slots), lambda r: (r, 0, 0)),
             pl.BlockSpec((None, heads, slots), lambda r: (r, 0, 0)),
             *(kind_spec(qkv.shape, kind) for kind in range(3)),
-            pl.BlockSpec((seq, None, blocks, short, lanes), lambda r: (0, r, 0, 0, 0)),
+            pl.BlockSpec((seq, blocks, None, short, lanes), lambda r: (0, 0, r, 0, 0)),
         ],
         out_specs=pl.BlockSpec((seq, 3, None, blocks, short, lanes), lambda r: (0, 0, r, 0, 0, 0)),
         out_shape=jax.ShapeDtypeStruct(qkv.shape, BF16),
@@ -212,7 +222,7 @@
             flops=work * HD * 10 * 4, bytes_accessed=units * slots * LANES * 16, transcendentals=work
         ),
         name="attend_back",
-    )(kpos, meta, lse, qkv, qkv, qkv, upstream)
+    )(own, kpos, meta, lse, qkv, qkv, qkv, upstream)
 
 
 def per_device(
@@ -270,20 +280,22 @@
     ).reshape(chunks, units, slots)
     meta = jnp.stack([first, jnp.broadcast_to(order, first.shape)], 2)
     kpos = order[:, None]
-
-    qkv_full = lax.all_gather(w_qkv.astype(BF16), "seq", axis=0, tiled=True).reshape(width, 3 * embed)
-    out_full = lax.all_gather(w_out.astype(BF16), "seq", axis=0, tiled=True)
-    up_full = lax.all_gather(w_up.astype(BF16), "seq", axis=0, tiled=True)
-    down_full = lax.all_gather(w_down.astype(BF16), "seq", axis=0, tiled=True)
+    own = mdl_index.reshape(1).astype(jnp.int32)
 
     def exchange(value):
         return lax.all_to_all(value, "seq", 0, 0, tiled=True)
 
-    def gather(value):
-        return ring_gather(value, "mdl").reshape(-1, width)
-
-    def scatter(value):
-        return ring_scatter(value.reshape(mdl_count, chunk_rows * short, width), "mdl")
+    def exchange_all(value):
+        shape = (seq_count * mdl_count, units, short, LANES)
+        return lax.all_to_all(value.reshape(shape), ("seq", "mdl"), 0, 0, tiled=True)
+
+    def own_heads(value):
+        value = value.reshape(pairs, groups, mdl_count, units, short, LANES)
+        return value.transpose(1, 3, 4, 2, 0, 5).reshape(chunk_rows * short, mdl_count * embed)
+
+    def own_units(value):
+        value = value.reshape(groups, units, short, mdl_count, pairs, LANES)
+        return value.transpose(4, 0, 3, 1, 2, 5).reshape(-1, units, short, LANES)
 
     def to_units(value, kinds):
         value = value.reshape(mdl_count, groups, units, short, kinds, pairs, LANES)
@@ -295,76 +307,222 @@
         value = value.transpose(4, 1, 3, 5, 2, 0, 6)
         return value.reshape(mdl_count * chunk_rows * short, kinds * embed)
 
-    span = micro // chunks
-    saved = []
-    outputs, input_grads = [], []
-    norm_sums = jnp.zeros((4, width), F32)
-    for c in range(chunks):
-        inputs = layer_in[c * span : (c + 1) * span].reshape(-1, width)
-        upstream = cotangent[c * span : (c + 1) * span].reshape(-1, width)
-        normed_one, hat_one, inv_one = norm_forward(inputs, norm_params[0], norm_params[1])
-        rows_one = gather(normed_one.astype(BF16))
-        projected = dot(rows_one, qkv_full, ((1,), (0,))).astype(BF16)
-        qkv = exchange(to_units(projected, 3))
-        out, lse = attention(qkv, kpos, meta[c], size)
-        attended = from_units(exchange(out), 1)
-        mixed = scatter(dot(attended, out_full, ((1,), (1,))))
-        middle = inputs + mixed
-        normed_two, hat_two, inv_two = norm_forward(middle, norm_params[2], norm_params[3])
-        rows_two = gather(normed_two.astype(BF16))
-        up_proj = dot(rows_two, up_full, ((1,), (0,)))
+    ring = [(i, (i + 1) % mdl_count) for i in range(mdl_count)]
+    members = range(mdl_count)
+    tokens = micro * rows * short
+
+    def pass_on(value):
+        return lax.ppermute(value, "mdl", ring)
+
+    held = {}
+
+    def behind(value, *names):
+        for name in names:
+            value, held[name] = tied(value, held[name])
+        return value
+
+    def ring_gather(value, gates=()):
+        parts = [value]
+        for j in members[1:]:
+            ahead = parts[-1]
+            if j <= len(gates) and gates[j - 1]:
+                ahead = behind(ahead, gates[j - 1])
+            parts.append(pass_on(ahead))
+        return parts
+
+    def ring_terms(parts):
+        carried = None
+        for j in members[1:]:
+            term = parts[j] if carried is None else parts[j] + carried.astype(F32)
+            carried = yield term.astype(BF16)
+
+    def ring_scatter(parts):
+        terms = ring_terms(parts)
+        term = next(terms)
+        while True:
+            carried = pass_on(term)
+            try:
+                term = terms.send(carried)
+            except StopIteration:
+                return carried
+
+    def spread(weight):
+        return lax.all_gather(weight, "seq", axis=0, tiled=True)
+
+    def by_member(parts):
+        placed = []
+        for k in members:
+            turns = (mdl_index - k) % mdl_count
+            value = parts[0]
+            for j in members[1:]:
+                value = jnp.where(turns == j, parts[j], value)
+            placed.append(value)
+        return jnp.concatenate(placed, 1)
+
+    def grad(left, right):
+        return dot(left, right, ((0,), (0,))).astype(BF16)
+
+    chips = seq_count // 2
+    cycle = [*range(0, chips, 2), *range(chips - 1, 0, -2)]
+    swap = [(i, i ^ 1) for i in range(seq_count)]
+    onward, blocks_behind = [], []
+    for index in range(seq_count):
+        place, way = cycle.index(index // 2), 1 - 2 * (index % 2)
+        onward.append((index, 2 * cycle[(place + way) % chips] + index % 2))
+        blocks_behind.append([cycle[(place - way * j) % chips] for j in range(chips)])
+    blocks_behind = lax.dynamic_index_in_dim(
+        jnp.array(blocks_behind, jnp.int32), seq_index, 0, False
+    )
+    core = seq_index % 2
+
+    def shared(value):
+        return lax.psum_scatter(value, "seq", scatter_dimension=0, tiled=True).astype(F32)
+
+    def share(value):
+        value = value.reshape(chips, 2, -1, value.shape[-1])
+        other = lax.ppermute(lax.dynamic_index_in_dim(value, 1 - core, 1, False), "seq", swap)
+
+        def term(j):
+            block = blocks_behind[j]
+            zero = jnp.zeros_like(block)
+            mine = lax.dynamic_slice(
+                value, (block, core, zero, zero), (1, 1, *value.shape[2:])
+            ).reshape(value.shape[2:])
+            return mine.astype(F32) + lax.dynamic_index_in_dim(other, block, 0, False).astype(F32)
+
+        carried = lax.ppermute(term(1).astype(BF16), "seq", onward)
+        for j in range(2, chips):
+            carried = lax.ppermute((term(j) + carried.astype(F32)).astype(BF16), "seq", onward)
+        return term(0) + carried.astype(F32)
+
+    total_tokens = micro * rows * slots
+    weight_rate = 0.02 * total_tokens ** (-0.5)
+    norm_rate = 0.15 * total_tokens ** (-0.5)
+    each = range(chunks)
+    inputs = layer_in.reshape(tokens, width)
+    upstream = cotangent.reshape(tokens, width)
+
+    low_qkv = w_qkv.astype(BF16).reshape(-1, 3 * embed)
+    normed, hat_one, inv_one = norm_forward(inputs, norm_params[0], norm_params[1])
+    normed, low_qkv = tied(normed.astype(BF16), low_qkv)
+    full_qkv = spread(low_qkv)
+    rows_one = ring_gather(normed)
+    low_up, full_qkv = tied(w_up.astype(BF16), full_qkv)
+    full_up = spread(low_up)
+    projected = [dot(part, full_qkv, ((1,), (0,))).astype(BF16) for part in rows_one]
+    low_out, projected = tied(w_out.astype(BF16), projected)
+    full_out = spread(lax.all_gather(low_out, "mdl", axis=1, tiled=True))
+    projected = jnp.stack(projected).reshape(mdl_count, chunks, -1, 3 * embed)
+    held["one"] = rows_one[-1]
+    held["qkv"] = [exchange(to_units(projected[:, c], 3)) for c in each]
+    back = behind(upstream.astype(BF16), "one")
+    rows_one[-1] = held["one"]
+    rows_back = [back, pass_on(back)]
+    rows_back.append(pass_on(behind(rows_back[-1], "qkv")))
+
+    seen = [attention(own, held["qkv"][c], kpos, meta[c], size) for c in each]
+    held["seen"] = seen
+    full_down = spread(behind(w_down.astype(BF16), "seen"))
+    for _ in members[3:]:
+        rows_back.append(pass_on(behind(rows_back[-1], "seen")))
+    seen = held["seen"]
+    attended = [own_heads(exchange_all(value[0])) for value in seen]
+    attended = jnp.concatenate(attended, 0)
+    middle = inputs + dot(attended, full_out, ((1,), (1,)))
+    normed, hat_two, inv_two = norm_forward(middle, norm_params[2], norm_params[3])
+    normed = normed.astype(BF16)
+    normed, rows_back[-1] = tied(normed, rows_back[-1])
+
+    rows_two = ring_gather(normed)
+    hidden, up_back, second = [], [], []
+    for j in members:
+        up_proj = dot(rows_two[j], full_up, ((1,), (0,)))
         cdf = 0.5 * (1.0 + lax.erf(up_proj * HALF_ROOT))
-        hidden = (up_proj * cdf).astype(BF16)
         slope = cdf + up_proj * jnp.exp(-0.5 * up_proj * up_proj) * INV_ROOT_TWO_PI
-        branch = scatter(dot(hidden, down_full, ((1,), (1,))))
-        outputs.append(middle + branch)
-        back_rows = gather(upstream.astype(BF16))
-        hidden_grad = dot(back_rows, down_full, ((1,), (0,)))
-        up_back = (hidden_grad * slope).astype(BF16)
-        second_in = scatter(dot(up_back, up_full, ((1,), (1,))))
-        middle_grad = upstream + norm_backward(second_in, hat_two, inv_two, norm_params[2])
-        resid_rows = gather(middle_grad.astype(BF16))
-        attended_back = dot(resid_rows, out_full, ((1,), (0,))).astype(BF16)
-        unit_back = exchange(to_units(attended_back, 1))[:, 0]
-        qkv_back = attention_back(qkv, unit_back, lse, kpos, meta[c], size)
-        proj_back = from_units(exchange(qkv_back), 3)
-        first_in = scatter(dot(proj_back, qkv_full, ((1,), (1,))))
-        input_grads.append(middle_grad + norm_backward(first_in, hat_one, inv_one, norm_params[0]))
-        norm_sums = norm_sums + jnp.stack(
+        hidden.append((up_proj * cdf).astype(BF16))
+        up_back.append((dot(rows_back[j], full_down, ((1,), (0,))) * slope).astype(BF16))
+        second.append(dot(up_back[j], full_up, ((1,), (1,))))
+    second_sum = ring_scatter(second)
+    branch = [dot(value, full_down, ((1,), (1,))) for value in hidden]
+    down_part = grad(jnp.concatenate(rows_back, 0), jnp.concatenate(hidden, 0))
+    up_part = grad(jnp.concatenate(rows_two, 0), jnp.concatenate(up_back, 0))
+    second_sum, (down_part, up_part, branch) = tied(second_sum, (down_part, up_part, branch))
+    held["down"], held["up"] = shared(down_part), shared(up_part)
+    second_in = second[0] + second_sum.astype(F32)
+    middle_grad = upstream + norm_backward(second_in, hat_two, inv_two, norm_params[2])
+    middle_low = middle_grad.astype(BF16)
+
+    attended_back = dot(middle_low, full_out, ((1,), (0,))).astype(BF16)
+    held["back"] = attended_back
+    terms = ring_terms(branch)
+    carried = pass_on(next(terms))
+    attended_back = held["back"].reshape(chunks, -1, mdl_count * embed)
+    held["unit"] = [exchange_all(own_units(attended_back[c])) for c in each]
+    carried = pass_on(terms.send(behind(carried, "unit")))
+    held["out"] = shared(grad(behind(middle_low, "unit"), attended))
+    held["attg"] = [
+        attention_back(
+            own,
+            held["qkv"][c],
+            held["unit"][c].reshape(seq_count, mdl_count, units, short, LANES),
+            held["seen"][c][1],
+            kpos,
+            meta[c],
+            size,
+        )
+        for c in each
+    ]
+    for _ in members[3:]:
+        carried = pass_on(terms.send(behind(carried, "attg")))
+    proj_back = [
+        from_units(exchange(value), 3).reshape(mdl_count, -1, 3 * embed) for value in held["attg"]
+    ]
+    proj_back = jnp.concatenate(proj_back, 1)
+    proj_back = behind(proj_back, "down")
+    proj_back, carried = tied(proj_back, carried)
+    layer_out = middle + (branch[0] + carried.astype(F32))
+    first = [dot(proj_back[j], full_qkv, ((1,), (1,))) for j in members]
+    proj_back, first[1] = tied(proj_back.reshape(-1, 3 * embed), first[1])
+    first_sum = ring_scatter(first)
+    held["qkv_grad"] = share(grad(jnp.concatenate(rows_one, 0), proj_back))
+    columns = [
+        lax.dynamic_slice_in_dim(held["out"], embed * ((mdl_index - j) % mdl_count), embed, 1)
+        for j in members
+    ]
+    held["out_grad"] = columns[0] + ring_scatter(columns).astype(F32)
+    first_sum = behind(first_sum, "up", "out_grad", "qkv_grad")
+    down_grad, up_grad = held["down"], held["up"]
+    out_grad, qkv_grad = held["out_grad"], held["qkv_grad"]
+    first_in = first[0] + first_sum.astype(F32)
+    input_grad = middle_grad + norm_backward(first_in, hat_one, inv_one, norm_params[0])
+    norm_total = whole_sum(
+        jnp.stack(
             [
                 jnp.sum(first_in * hat_one, 0),
                 jnp.sum(first_in, 0),
                 jnp.sum(second_in * hat_two, 0),
                 jnp.sum(second_in, 0),
             ]
-        )
-        saved.append((rows_one, proj_back, resid_rows, attended, rows_two, up_back, back_rows, hidden))
-
-    whole = [jnp.concatenate(parts, 0) for parts in zip(*saved)]
-    rows_one, proj_back, resid_rows, attended, rows_two, up_back, back_rows, hidden = whole
-
-    def grad(left, right):
-        return lax.psum_scatter(
-            dot(left, right, ((0,), (0,))).astype(BF16), "seq", scatter_dimension=0, tiled=True
-        ).astype(F32)
-
-    down_grad = grad(back_rows, hidden)
-    up_grad = grad(rows_two, up_back)
-    out_grad = grad(resid_rows, attended)
-    qkv_grad = grad(rows_one, proj_back).reshape(w_qkv.shape)
-    norm_total = lax.psum(norm_sums, ("seq", "mdl"))
-    total_tokens = micro * rows * slots
-    weight_rate = 0.02 * total_tokens ** (-0.5)
-    norm_rate = 0.15 * total_tokens ** (-0.5)
+        ),
+        ("mdl", "seq"),
+    )
+    def updated(weight, total, moment, average):
+        if weight.ndim == 2:
+            return update_param(weight, total, moment, average, weight_rate)
+        kinds = [value.swapaxes(0, 1) for value in (weight, moment, average)]
+        total = jnp.stack(jnp.split(total, 3, 1))
+        new = update_param(kinds[0], total, *kinds[1:], weight_rate)
+        return [value.swapaxes(0, 1) for value in new]
+
     shape = layer_in.shape
     return (
-        jnp.concatenate(outputs, 0).reshape(shape),
-        jnp.concatenate(input_grads, 0).reshape(shape),
+        layer_out.reshape(shape),
+        input_grad.reshape(shape),
         *update_param(norm_params, norm_total, norm_moment, norm_average, norm_rate),
-        *update_param(w_qkv, qkv_grad, qkv_moment, qkv_average, weight_rate),
-        *update_param(w_out, out_grad, out_moment, out_average, weight_rate),
-        *update_param(w_up, up_grad, up_moment, up_average, weight_rate),
-        *update_param(w_down, down_grad, down_moment, down_average, weight_rate),
+        *updated(w_qkv, qkv_grad, qkv_moment, qkv_average),
+        *updated(w_out, out_grad, out_moment, out_average),
+        *updated(w_up, up_grad, up_moment, up_average),
+        *updated(w_down, down_grad, down_moment, down_average),
     )
 
 

time: 1100 us -> 798 us (0.73)
  waiting for transfers between devices: 652 us -> 394 us
  blocking collectives: 38.5 us -> 0 us
  local copies, waits for them, and re-layouts: 67.8 us -> 42.3 us
  matrix products: 146 us -> 167 us
    ppermute x48 -> x30, waiting for transfers between devices: 459 us -> 250 us  [the longest x21 220 us: pass_on(): return lax.ppermute(value, 'mdl', ring)]
    reduce_scatter x4 -> x3, waiting for transfers between devices: 69.5 us -> 13.8 us  [shared(): lax.psum_scatter(value, 'seq', scatter_dimension=0, tiled=True).astype(F32)]
    all_to_all x0 -> x2, waiting for transfers between devices: none -> 49 us  [exchange_all(): lax.all_to_all(value.reshape(shape), ('seq', 'mdl'), 0, 0, tiled=True)]
    psum x1 -> x0, blocking collectives: 38.5 us -> none  [per_device(): norm_total = lax.psum(norm_sums, ('seq', 'mdl'))]
    all_to_all x8 -> x2, starting transfers between devices: 33 us -> 8.28 us  [exchange(): return lax.all_to_all(value, 'seq', 0, 0, tiled=True)]
    all_gather x4 -> x5, waiting for transfers between devices: 54.3 us -> 30.6 us  [the longest x1 25.8 us: per_device(): full_out = spread(lax.all_gather(low_out, 'mdl', axis=1, tiled=True))]
    dot_general x20 -> x30, matrix products: 146 us -> 167 us  [dot(): return lax.dot_general(a, b, (dims, ((), ())), preferred_element_type=F32)]
    unnamed x185 -> x151, local copies, waits for them, and re-layouts: 32.1 us -> 12.9 us
  transfers between devices with their start and end apart: 64 -> 42, of which waited for: 47 -> 27; matrix products, arithmetic and copies ran while one was open for 18% -> 30% of each run, Pallas kernels for 4% -> 5%
where the time goes in v2:
time: 798 us; the launch traced here: 788 us
  waiting for transfers between devices  394 us (49%)
  matrix products  167 us (21%)
  other arithmetic  62.6 us (8%)
  starting transfers between devices  50.5 us (6%)
  local copies, waits for them, and re-layouts  42.3 us (5%)
  Pallas kernels  40.8 us (5%)
  between operations  31 us (4%)
    ppermute x21, waiting for transfers between devices, pass_on(): return lax.ppermute(value, 'mdl', ring)  220 us
    dot_general x30, matrix products, dot(): return lax.dot_general(a, b, (dims, ((), ())), preferred_element_type=F32)  167 us
    all_to_all x2, waiting for transfers between devices, exchange(): return lax.all_to_all(value, 'seq', 0, 0, tiled=True)  49.6 us
    all_to_all x2, waiting for transfers between devices, exchange_all(): lax.all_to_all(value.reshape(shape), ('seq', 'mdl'), 0, 0, tiled=True)  49 us
    ppermute x21, starting transfers between devices, pass_on(): return lax.ppermute(value, 'mdl', ring)  26 us
    all_gather x1, waiting for transfers between devices, per_device(): full_out = spread(lax.all_gather(low_out, 'mdl', axis=1, tiled=True))  25.8 us
    pallas_call x1, Pallas kernels, attention_back(): pl.pallas_call(functools.partial(attend_back_kernel, size=size, factor=HD...  23.4 us
    ppermute x2, waiting for transfers between devices, share(): lax.ppermute((term(j) + carried.astype(F32)).astype(BF16), 'seq', onward)  20.2 us
  transfers between devices with their start and end apart: 42, of which 27 were waited for; matrix products, arithmetic and copies ran while one was open for 30% of the time, Pallas kernels for 5%

profile of v2, /device:TPU:0, one launch (start us, length us, event | category | flops | bytes accessed | tf_op | source)
XLA Modules:
  0.0 787.9 jit_solution(8685584726119207445)
XLA Ops:
  17.1 25.4 %collective-permute-done = bf16[256,2048]{1,0:T(8,128)(2,1)S(1)} collective-permute-done((bf16[256,2048]{1,0:T(8,128)(2,1)}, bf16[256,2048]{1,0:T(8,128)(2,1)S(1)}, u32[]{:S(2)}, u32[]{:S(2)}) %collective-permute-start) | collective-permute-done | bytes 1048608 | tf_op jit(solution)/shard_map/ppermute | solution.py:315
  46.1 22.6 %collective-permute-done.1 = bf16[256,2048]{1,0:T(8,128)(2,1)} collective-permute-done((bf16[256,2048]{1,0:T(8,128)(2,1)S(1)}, bf16[256,2048]{1,0:T(8,128)(2,1)}, u32[]{:S(2)}, u32[]{:S(2)}) %collective-permute-start.1) | collective-permute-done | bytes 1048608 | tf_op jit(solution)/shard_map/ppermute | solution.py:315
  79.4 14.9 %collective-permute-done.2 = bf16[256,2048]{1,0:T(8,128)(2,1)} collective-permute-done((bf16[256,2048]{1,0:T(8,128)(2,1)}, bf16[256,2048]{1,0:T(8,128)(2,1)}, u32[]{:S(2)}, u32[]{:S(2)}) %collective-permute-start.2) | collective-permute-done | bytes 1048608 | tf_op jit(solution)/shard_map/ppermute | solution.py:315
  98.3 25.8 %all-gather.8.cloned.1.call-done = bf16[256,2048]{1,0:T(8,128)(2,1)} async-done(((bf16[256,512]{1,0:T(8,128)(2,1)}), bf16[256,2048]{1,0:T(8,128)(2,1)}) %all-gather.8.cloned.1.call-update) | async-done | bytes 1048592 | tf_op jit(solution)/shard_map/all_gather | solution.py:414
  155.8 17.4 %collective-permute-done.3 = bf16[256,2048]{1,0:T(8,128)(2,1)} collective-permute-done((bf16[256,2048]{1,0:T(8,128)(2,1)}, bf16[256,2048]{1,0:T(8,128)(2,1)}, u32[]{:S(2)}, u32[]{:S(2)}) %collective-permute-start.3) | collective-permute-done | bytes 1048608 | tf_op jit(solution)/shard_map/ppermute | solution.py:315
  173.2 8.6 %all-to-all-done.q_ref.k_ref.v_ref = bf16[8,3,4,4,32,128]{5,4,3,2,1,0:T(8,128)(2,1)S(1)} async-done(((bf16[8,3,4,4,32,128]{5,4,3,2,1,0:T(8,128)(2,1)}), bf16[8,3,4,4,32,128]{5,4,3,2,1,0:T(8,128)(2,1)S(1)}, u32[]{:S(2)}, u32[]{:S(2)}) %all-to-all-start) | async-done | bytes 3145760 | tf_op jit(solution)/shard_map/all_to_all | solution.py:286
  183.2 17.4 %attend.1 = (bf16[8,4,4,32,128]{4,3,2,1,0:T(8,128)(2,1)S(1)}, f32[4,2,1024]{2,1,0:T(2,128)S(1)}) custom-call(s32[1]{0:T(128)} %bitcast.7.own_ref, s32[1024,1]{1,0:T(8,128)S(1)} %copy-done.2, s32[4,2,1024]{2,1,0:T(2,128)S(1)} %add_bitcast_fusion.meta_ref, bf16[8,3,4,4,32,128]{5,4,3,2,1,0:T(8,128)(2,1)S(1)} %all-to-all-done.q_ref.k_ref.v_ref, ...), custom_call_target="tpu_custom_call" | custom-call | flops 5368709120 | bytes 4194304 | tf_op jit(solution)/shard_map/attend/pallas_call | solution.py:176
  203.2 22.8 %collective-permute-done.4 = bf16[256,2048]{1,0:T(8,128)(2,1)} collective-permute-done((bf16[256,2048]{1,0:T(8,128)(2,1)}, bf16[256,2048]{1,0:T(8,128)(2,1)}, u32[]{:S(2)}, u32[]{:S(2)}) %collective-permute-start.4) | collective-permute-done | bytes 1048608 | tf_op jit(solution)/shard_map/ppermute | solution.py:315
  233.3 45.7 %all-to-all-done.1 = bf16[32,4,32,128]{3,2,1,0:T(8,128)(2,1)S(1)} async-done(((bf16[32,4,32,128]{3,2,1,0:T(8,128)(2,1)}), bf16[32,4,32,128]{3,2,1,0:T(8,128)(2,1)S(1)}, u32[]{:S(2)}, u32[]{:S(2)}) %all-to-all-start.1) | async-done | bytes 1048608 | tf_op jit(solution)/shard_map/all_to_all | solution.py:290
  282.6 6.2 fusion.96
  293.7 8.1 %multiply_convert_fusion.3 = (bf16[256,2048]{1,0:T(8,128)(2,1)}, f32[256,2048]{1,0:T(8,128)}) fusion(bf16[256,2048]{1,0:T(8,128)(2,1)S(1)} %add_convert_fusion.6, bf16[2048,2048]{1,0:T(8,128)(2,1)} %all-gather.14.cloned.1.call-done), kind=kOutput, calls=%fused_computation.103 | convolution fusion | flops 2150105088 | bytes 12582912 | tf_op jit(solution)/shard_map/dot_general | solution.py:46
  301.8 16.2 %collective-permute-done.6 = bf16[256,2048]{1,0:T(8,128)(2,1)S(1)} collective-permute-done((bf16[256,2048]{1,0:T(8,128)(2,1)S(1)}, bf16[256,2048]{1,0:T(8,128)(2,1)S(1)}, u32[]{:S(2)}, u32[]{:S(2)}) %collective-permute-start.6) | collective-permute-done | bytes 1048608 | tf_op jit(solution)/shard_map/ppermute | solution.py:315
  327.0 7.1 fusion.35
  376.4 14.4 %collective-permute-done.8 = bf16[256,2048]{1,0:T(8,128)(2,1)S(1)} collective-permute-done((bf16[256,2048]{1,0:T(8,128)(2,1)}, bf16[256,2048]{1,0:T(8,128)(2,1)S(1)}, u32[]{:S(2)}, u32[]{:S(2)}) %collective-permute-start.8) | collective-permute-done | bytes 1048608 | tf_op jit(solution)/shard_map/ppermute | solution.py:315
  395.8 12.7 %convolution_convert_fusion.3 = bf16[2048,2048]{1,0:T(8,128)(2,1)} fusion(bf16[256,2048]{1,0:T(8,128)(2,1)} %collective-permute-done.5, bf16[256,2048]{1,0:T(8,128)(2,1)} %collective-permute-done.4, bf16[256,2048]{1,0:T(8,128)(2,1)} %collective-permute-done.3, bf16[256,2048]{1,0:T(8,128)(2,1)} %bitcast_convert_fusion, ...), kind=kOutput, calls=%fused_computation.4 | convolution fusion | flops 8627683328 | bytes 16777216 | tf_op jit(solution)/shard_map/dot_general | solution.py:46
  408.5 6.1 fusion.98
  417.2 12.4 %convolution_convert_fusion.2 = bf16[2048,2048]{1,0:T(8,128)(2,1)} fusion(bf16[256,2048]{1,0:T(8,128)(2,1)S(1)} %copy-done.56, bf16[256,2048]{1,0:T(8,128)(2,1)} %collective-permute-done.7, bf16[256,2048]{1,0:T(8,128)(2,1)S(1)} %collective-permute-done.6, bf16[256,2048]{1,0:T(8,128)(2,1)S(1)} %add_convert_fusion.6, bf16[256,2048]{1,0:T(8,128)(2,1)S(1)} %copy-done.62, ...), kind=kOutput, calls=%fused_computation.3 | convolution fusion | flops 8627683328 | bytes 16777216 | tf_op jit(solution)/shard_map/dot_general | solution.py:46
  429.6 7.1 fusion.103
  442.1 7.6 multiply_reduce_fusion
  454.3 7.1 convolution_convert_fusion.8
  468.9 42.4 %collective-permute-done.12 = bf16[256,2048]{1,0:T(8,128)(2,1)} collective-permute-done((bf16[256,2048]{1,0:T(8,128)(2,1)}, bf16[256,2048]{1,0:T(8,128)(2,1)}, u32[]{:S(2)}, u32[]{:S(2)}) %collective-permute-start.12) | collective-permute-done | bytes 1048608 | tf_op jit(solution)/shard_map/ppermute | solution.py:315
  514.6 7.3 convolution_convert_fusion.1
  528.1 23.4 %attend_back.1 = bf16[8,3,4,4,32,128]{5,4,3,2,1,0:T(8,128)(2,1)} custom-call(s32[1]{0:T(128)} %bitcast.7.own_ref, s32[1024,1]{1,0:T(8,128)S(1)} %copy-done.3, s32[4,2,1024]{2,1,0:T(2,128)S(1)} %add_bitcast_fusion.meta_ref, f32[4,2,1024]{2,1,0:T(2,128)S(1)} %get-tuple-element.96.lse_ref, bf16[8,3,4,4,32,128]{5,4,3,2,1,0:T(8,128)(2,1)} %copy-done, ...), custom_call_target="tpu_custom_call" | custom-call | flops 13421772800 | bytes 8388608 | tf_op jit(solution)/shard_map/attend_back/pallas_call | solution.py:206
  569.1 41.1 %all-to-all-done.3 = bf16[8,3,4,4,32,128]{5,4,3,2,1,0:T(8,128)(2,1)} async-done(((bf16[8,3,4,4,32,128]{5,4,3,2,1,0:T(8,128)(2,1)}), bf16[8,3,4,4,32,128]{5,4,3,2,1,0:T(8,128)(2,1)}, u32[]{:S(2)}, u32[]{:S(2)}) %all-to-all-start.3) | async-done | bytes 3145760 | tf_op jit(solution)/shard_map/all_to_all | solution.py:286
  616.1 6.2 reshape_reshape.3
  630.9 8.6 %convolution_convert_fusion = bf16[2048,1536]{1,0:T(8,128)(2,1)S(1)} fusion(bf16[1024,1536]{1,0:T(8,128)(2,1)S(1)} %bitcast.199, bf16[256,2048]{1,0:T(8,128)(2,1)} %collective-permute-done.2, bf16[256,2048]{1,0:T(8,128)(2,1)} %collective-permute-done.1, bf16[256,2048]{1,0:T(8,128)(2,1)S(1)} %copy-done.54, bf16[256,2048]{1,0:T(8,128)(2,1)S(1)} %copy-done.33), kind=kOutput, calls=%fused_computation.1 | convolution fusion | flops 6462373888 | bytes 13631488 | tf_op jit(solution)/shard_map/dot_general | solution.py:46
  643.7 9.6 %collective-permute-done.15 = bf16[256,2048]{1,0:T(8,128)(2,1)S(1)} collective-permute-done((bf16[256,2048]{1,0:T(8,128)(2,1)S(1)}, bf16[256,2048]{1,0:T(8,128)(2,1)S(1)}, u32[]{:S(2)}, u32[]{:S(2)}) %collective-permute-start.15) | collective-permute-done | bytes 1048608 | tf_op jit(solution)/shard_map/ppermute | solution.py:315
  664.1 20.9 %collective-permute-done.18 = bf16[256,512]{1,0:T(8,128)(2,1)S(1)} collective-permute-done((bf16[256,512]{1,0:T(8,128)(2,1)S(1)}, bf16[256,512]{1,0:T(8,128)(2,1)S(1)}, u32[]{:S(2)}, u32[]{:S(2)}) %collective-permute-start.18) | collective-permute-done | bytes 262176 | tf_op jit(solution)/shard_map/ppermute | solution.py:315
  685.2 6.3 add_convert_fusion
  700.9 13.8 %reduce-scatter.6.cloned.1.call-done = bf16[256,2048]{1,0:T(8,128)(2,1)} async-done(((bf16[2048,2048]{1,0:T(8,128)(2,1)}), bf16[256,2048]{1,0:T(8,128)(2,1)}) %reduce-scatter.6.cloned.1.call-update) | async-done | bytes 1048592 | tf_op jit(solution)/shard_map/reduce_scatter | solution.py:379
  730.3 11.1 %collective-permute-done.23 = bf16[256,1536]{1,0:T(8,128)(2,1)S(1)} collective-permute-done((bf16[256,1536]{1,0:T(8,128)(2,1)S(1)}, bf16[256,1536]{1,0:T(8,128)(2,1)S(1)}, u32[]{:S(2)}, u32[]{:S(2)}) %collective-permute-start.23) | collective-permute-done | bytes 786464 | tf_op jit(solution)/shard_map/ppermute | solution.py:395
  746.2 9.1 %collective-permute-done.24 = bf16[256,1536]{1,0:T(8,128)(2,1)S(1)} collective-permute-done((bf16[256,1536]{1,0:T(8,128)(2,1)S(1)}, bf16[256,1536]{1,0:T(8,128)(2,1)S(1)}, u32[]{:S(2)}, u32[]{:S(2)}) %collective-permute-start.24) | collective-permute-done | bytes 786464 | tf_op jit(solution)/shard_map/ppermute | solution.py:395
  (336 shorter events, 251.9 us)
Async XLA Ops:
  7.2 61.5 %all-gather.6.cloned.1.call-start = ((), (), s32[]{:S(2)}) async-start(), calls=%async_computation.7 | async-start | bytes 7077888 | tf_op jit(solution)/shard_map/all_gather | solution.py:350
  13.9 110.1 %all-gather.8.cloned.1.call-start = ((), (), s32[]{:S(2)}) async-start(), calls=%async_computation.8 | async-start | bytes 1310720 | tf_op jit(solution)/shard_map/all_gather | solution.py:414
  14.0 28.5 %collective-permute-start = (bf16[256,2048]{1,0:T(8,128)(2,1)}, bf16[256,2048]{1,0:T(8,128)(2,1)S(1)}, u32[]{:S(2)}, u32[]{:S(2)}) collective-permute-start(bf16[256,2048]{1,0:T(8,128)(2,1)} %add_convert_fusion.7), channel_id=1, source_target_pairs={{0,1},{1,2},{2,3},{3,0},{4,5},{5,6},{6,7},{7,4},{8,9},{9,10},{10,1... | collective-permute-start | bytes 3145736 | tf_op jit(solution)/shard_map/ppermute | solution.py:315
  42.5 26.2 %collective-permute-start.1 = (bf16[256,2048]{1,0:T(8,128)(2,1)S(1)}, bf16[256,2048]{1,0:T(8,128)(2,1)}, u32[]{:S(2)}, u32[]{:S(2)}) collective-permute-start(bf16[256,2048]{1,0:T(8,128)(2,1)S(1)} %collective-permute-done), channel_id=1, source_target_pairs={{0,1},{1,2},{2,3},{3,0},{4,5},{5,6},{6,7},{7,4},{8,9},{9,10},{10,1... | collective-permute-start | bytes 3145736 | tf_op jit(solution)/shard_map/ppermute | solution.py:315
  68.7 25.5 %collective-permute-start.2 = (bf16[256,2048]{1,0:T(8,128)(2,1)}, bf16[256,2048]{1,0:T(8,128)(2,1)}, u32[]{:S(2)}, u32[]{:S(2)}) collective-permute-start(bf16[256,2048]{1,0:T(8,128)(2,1)} %collective-permute-done.1), channel_id=1, source_target_pairs={{0,1},{1,2},{2,3},{3,0},{4,5},{5,6},{6,7},{7,4},{8,9},{9,10},{10,1... | collective-permute-start | bytes 3145736 | tf_op jit(solution)/shard_map/ppermute | solution.py:315
  98.2 184.4 %all-gather.10.cloned.1.call-start = ((), (), s32[]{:S(2)}) async-start(), calls=%async_computation.9 | async-start | bytes 9437184 | tf_op jit(solution)/shard_map/all_gather | solution.py:350
  124.1 169.7 %all-gather.14.cloned.1.call-start = ((), (), s32[]{:S(2)}) async-start(), calls=%async_computation.11 | async-start | bytes 9437184 | tf_op jit(solution)/shard_map/all_gather | solution.py:350
  131.1 50.7 %all-to-all-start = ((bf16[8,3,4,4,32,128]{5,4,3,2,1,0:T(8,128)(2,1)}), bf16[8,3,4,4,32,128]{5,4,3,2,1,0:T(8,128)(2,1)S(1)}, u32[]{:S(2)}, u32[]{:S(2)}) async-start(bf16[8,3,4,4,32,128]{5,4,3,2,1,0:T(8,128)(2,1)} %bitcast.188), calls=%async_computation | async-start | bytes 6291456 | tf_op jit(solution)/shard_map/all_to_all | solution.py:286
  135.0 192.1 %all-gather.12.cloned.1.call-start = ((), (), s32[]{:S(2)}) async-start(), calls=%async_computation.10 | async-start | bytes 9437184 | tf_op jit(solution)/shard_map/all_gather | solution.py:350
  145.6 27.6 %collective-permute-start.3 = (bf16[256,2048]{1,0:T(8,128)(2,1)}, bf16[256,2048]{1,0:T(8,128)(2,1)}, u32[]{:S(2)}, u32[]{:S(2)}) collective-permute-start(bf16[256,2048]{1,0:T(8,128)(2,1)} %bitcast_convert_fusion), channel_id=1, source_target_pairs={{0,1},{1,2},{2,3},{3,0},{4,5},{5,6},{6,7},{7,4},{8,9},{9,10},{10,1... | collective-permute-start | bytes 3145736 | tf_op jit(solution)/shard_map/ppermute | solution.py:315
  201.6 24.4 %collective-permute-start.4 = (bf16[256,2048]{1,0:T(8,128)(2,1)}, bf16[256,2048]{1,0:T(8,128)(2,1)}, u32[]{:S(2)}, u32[]{:S(2)}) collective-permute-start(bf16[256,2048]{1,0:T(8,128)(2,1)} %collective-permute-done.3), channel_id=1, source_target_pairs={{0,1},{1,2},{2,3},{3,0},{4,5},{5,6},{6,7},{7,4},{8,9},{9,10},{10,1... | collective-permute-start | bytes 3145736 | tf_op jit(solution)/shard_map/ppermute | solution.py:315
  226.0 52.9 %all-to-all-start.1 = ((bf16[32,4,32,128]{3,2,1,0:T(8,128)(2,1)}), bf16[32,4,32,128]{3,2,1,0:T(8,128)(2,1)S(1)}, u32[]{:S(2)}, u32[]{:S(2)}) async-start(bf16[32,4,32,128]{3,2,1,0:T(8,128)(2,1)} %bitcast.186), calls=%async_computation.1 | async-start | bytes 2097152 | tf_op jit(solution)/shard_map/all_to_all | solution.py:290
  231.4 390.9 %reduce-scatter.4.cloned.1.call-start = ((), (), s32[]{:S(2)}) async-start(), calls=%async_computation.12 | async-start | bytes 9437184 | tf_op jit(solution)/shard_map/reduce_scatter | solution.py:379
  231.5 58.7 %collective-permute-start.5 = (bf16[256,2048]{1,0:T(8,128)(2,1)}, bf16[256,2048]{1,0:T(8,128)(2,1)}, u32[]{:S(2)}, u32[]{:S(2)}) collective-permute-start(bf16[256,2048]{1,0:T(8,128)(2,1)} %collective-permute-done.4), channel_id=1, source_target_pairs={{0,1},{1,2},{2,3},{3,0},{4,5},{5,6},{6,7},{7,4},{8,9},{9,10},{10,1... | collective-permute-start | bytes 3145736 | tf_op jit(solution)/shard_map/ppermute | solution.py:315
  290.2 27.8 %collective-permute-start.6 = (bf16[256,2048]{1,0:T(8,128)(2,1)S(1)}, bf16[256,2048]{1,0:T(8,128)(2,1)S(1)}, u32[]{:S(2)}, u32[]{:S(2)}) collective-permute-start(bf16[256,2048]{1,0:T(8,128)(2,1)S(1)} %add_convert_fusion.6), channel_id=1, source_target_pairs={{0,1},{1,2},{2,3},{3,0},{4,5},{5,6},{6,7},{7,4},{8,9},{9,10},{10,1... | collective-permute-start | bytes 3145736 | tf_op jit(solution)/shard_map/ppermute | solution.py:315
  318.0 43.2 %collective-permute-start.7 = (bf16[256,2048]{1,0:T(8,128)(2,1)S(1)}, bf16[256,2048]{1,0:T(8,128)(2,1)}, u32[]{:S(2)}, u32[]{:S(2)}) collective-permute-start(bf16[256,2048]{1,0:T(8,128)(2,1)S(1)} %collective-permute-done.6), channel_id=1, source_target_pairs={{0,1},{1,2},{2,3},{3,0},{4,5},{5,6},{6,7},{7,4},{8,9},{9,10},{10,1... | collective-permute-start | bytes 3145736 | tf_op jit(solution)/shard_map/ppermute | solution.py:315
  337.5 33.6 %collective-permute-start.9 = (bf16[256,2048]{1,0:T(8,128)(2,1)S(1)}, bf16[256,2048]{1,0:T(8,128)(2,1)S(1)}, u32[]{:S(2)}, u32[]{:S(2)}) collective-permute-start(bf16[256,2048]{1,0:T(8,128)(2,1)S(1)} %convolution_convert_fusion.9), channel_id=1, source_target_pairs={{0,1},{1,2},{2,3},{3,0},{4,5},{5,6},{6,7},{7,4},{8,9},{9,10},{10,1... | collective-permute-start | bytes 3145736 | tf_op jit(solution)/shard_map/ppermute | solution.py:315
  361.2 29.5 %collective-permute-start.8 = (bf16[256,2048]{1,0:T(8,128)(2,1)}, bf16[256,2048]{1,0:T(8,128)(2,1)S(1)}, u32[]{:S(2)}, u32[]{:S(2)}) collective-permute-start(bf16[256,2048]{1,0:T(8,128)(2,1)} %collective-permute-done.7), channel_id=1, source_target_pairs={{0,1},{1,2},{2,3},{3,0},{4,5},{5,6},{6,7},{7,4},{8,9},{9,10},{10,1... | collective-permute-start | bytes 3145736 | tf_op jit(solution)/shard_map/ppermute | solution.py:315
  374.5 40.2 %collective-permute-start.10 = (bf16[256,2048]{1,0:T(8,128)(2,1)}, bf16[256,2048]{1,0:T(8,128)(2,1)S(1)}, u32[]{:S(2)}, u32[]{:S(2)}) collective-permute-start(bf16[256,2048]{1,0:T(8,128)(2,1)} %add_convert_fusion.5), channel_id=1, source_target_pairs={{0,1},{1,2},{2,3},{3,0},{4,5},{5,6},{6,7},{7,4},{8,9},{9,10},{10,1... | collective-permute-start | bytes 3145736 | tf_op jit(solution)/shard_map/ppermute | solution.py:315
  415.9 26.1 %collective-permute-start.11 = (bf16[256,2048]{1,0:T(8,128)(2,1)}, bf16[256,2048]{1,0:T(8,128)(2,1)}, u32[]{:S(2)}, u32[]{:S(2)}) collective-permute-start(bf16[256,2048]{1,0:T(8,128)(2,1)} %add_convert_fusion.4), channel_id=1, source_target_pairs={{0,1},{1,2},{2,3},{3,0},{4,5},{5,6},{6,7},{7,4},{8,9},{9,10},{10,1... | collective-permute-start | bytes 3145736 | tf_op jit(solution)/shard_map/ppermute | solution.py:315
  464.4 50.2 %all-to-all-start.2 = ((bf16[32,4,32,128]{3,2,1,0:T(8,128)(2,1)}), bf16[32,4,32,128]{3,2,1,0:T(8,128)(2,1)S(1)}, u32[]{:S(2)}, u32[]{:S(2)}) async-start(bf16[32,4,32,128]{3,2,1,0:T(8,128)(2,1)} %bitcast.197), calls=%async_computation.2 | async-start | bytes 2097152 | tf_op jit(solution)/shard_map/all_to_all | solution.py:290
  467.1 192.2 %reduce-scatter.8.cloned.1.call-start = ((), (), s32[]{:S(2)}) async-start(), calls=%async_computation.14 | async-start | bytes 9437184 | tf_op jit(solution)/shard_map/reduce_scatter | solution.py:379
  467.1 44.1 %collective-permute-start.12 = (bf16[256,2048]{1,0:T(8,128)(2,1)}, bf16[256,2048]{1,0:T(8,128)(2,1)}, u32[]{:S(2)}, u32[]{:S(2)}) collective-permute-start(bf16[256,2048]{1,0:T(8,128)(2,1)} %fusion.101), channel_id=1, source_target_pairs={{0,1},{1,2},{2,3},{3,0},{4,5},{5,6},{6,7},{7,4},{8,9},{9,10},{10,1... | collective-permute-start | bytes 3145736 | tf_op jit(solution)/shard_map/ppermute | solution.py:315
  521.9 192.8 %reduce-scatter.6.cloned.1.call-start = ((), (), s32[]{:S(2)}) async-start(), calls=%async_computation.13 | async-start | bytes 9437184 | tf_op jit(solution)/shard_map/reduce_scatter | solution.py:379
  524.9 27.2 %collective-permute-start.13 = (bf16[256,2048]{1,0:T(8,128)(2,1)S(1)}, bf16[256,2048]{1,0:T(8,128)(2,1)}, u32[]{:S(2)}, u32[]{:S(2)}) collective-permute-start(bf16[256,2048]{1,0:T(8,128)(2,1)S(1)} %add_convert_fusion.3), channel_id=1, source_target_pairs={{0,1},{1,2},{2,3},{3,0},{4,5},{5,6},{6,7},{7,4},{8,9},{9,10},{10,1... | collective-permute-start | bytes 3145736 | tf_op jit(solution)/shard_map/ppermute | solution.py:315
  552.2 58.0 %all-to-all-start.3 = ((bf16[8,3,4,4,32,128]{5,4,3,2,1,0:T(8,128)(2,1)}), bf16[8,3,4,4,32,128]{5,4,3,2,1,0:T(8,128)(2,1)}, u32[]{:S(2)}, u32[]{:S(2)}) async-start(bf16[8,3,4,4,32,128]{5,4,3,2,1,0:T(8,128)(2,1)} %attend_back.1), calls=%async_computation.3 | async-start | bytes 6291456 | tf_op jit(solution)/shard_map/all_to_all | solution.py:286
  560.0 64.0 %collective-permute-start.14 = (bf16[256,2048]{1,0:T(8,128)(2,1)}, bf16[256,2048]{1,0:T(8,128)(2,1)S(1)}, u32[]{:S(2)}, u32[]{:S(2)}) collective-permute-start(bf16[256,2048]{1,0:T(8,128)(2,1)} %add_convert_fusion.2), channel_id=1, source_target_pairs={{0,1},{1,2},{2,3},{3,0},{4,5},{5,6},{6,7},{7,4},{8,9},{9,10},{10,1... | collective-permute-start | bytes 3145736 | tf_op jit(solution)/shard_map/ppermute | solution.py:315
  643.7 51.8 %collective-permute-start.21 = (bf16[4,256,1536]{2,1,0:T(8,128)(2,1)}, bf16[4,256,1536]{2,1,0:T(8,128)(2,1)}, u32[]{:S(2)}, u32[]{:S(2)}) collective-permute-start(bf16[4,256,1536]{2,1,0:T(8,128)(2,1)} %dynamic-slice_bitcast_fusion), channel_id=1, source_target_pairs={{0,4},{4,0},{8,12},{12,8},{16,20},{20,16},{24,28},{28,24},{1,5},{5... | collective-permute-start | bytes 9437192 | tf_op jit(solution)/shard_map/ppermute | solution.py:383
  656.1 29.1 %collective-permute-start.16 = (bf16[256,2048]{1,0:T(8,128)(2,1)}, bf16[256,2048]{1,0:T(8,128)(2,1)}, u32[]{:S(2)}, u32[]{:S(2)}) collective-permute-start(bf16[256,2048]{1,0:T(8,128)(2,1)} %add_convert_fusion.1), channel_id=1, source_target_pairs={{0,1},{1,2},{2,3},{3,0},{4,5},{5,6},{6,7},{7,4},{8,9},{9,10},{10,1... | collective-permute-start | bytes 3145736 | tf_op jit(solution)/shard_map/ppermute | solution.py:315
  691.4 31.1 %collective-permute-start.17 = (bf16[256,2048]{1,0:T(8,128)(2,1)}, bf16[256,2048]{1,0:T(8,128)(2,1)}, u32[]{:S(2)}, u32[]{:S(2)}) collective-permute-start(bf16[256,2048]{1,0:T(8,128)(2,1)} %add_convert_fusion), channel_id=1, source_target_pairs={{0,1},{1,2},{2,3},{3,0},{4,5},{5,6},{6,7},{7,4},{8,9},{9,10},{10,1... | collective-permute-start | bytes 3145736 | tf_op jit(solution)/shard_map/ppermute | solution.py:315
  695.4 26.0 %collective-permute-start.20 = (bf16[256,512]{1,0:T(8,128)(2,1)S(1)}, bf16[256,512]{1,0:T(8,128)(2,1)S(1)}, u32[]{:S(2)}, u32[]{:S(2)}) collective-permute-start(bf16[256,512]{1,0:T(8,128)(2,1)S(1)} %add_convert_fusion.8), channel_id=1, source_target_pairs={{0,1},{1,2},{2,3},{3,0},{4,5},{5,6},{6,7},{7,4},{8,9},{9,10},{10,1... | collective-permute-start | bytes 786440 | tf_op jit(solution)/shard_map/ppermute | solution.py:315
  698.0 24.6 %collective-permute-start.22 = (bf16[256,1536]{1,0:T(8,128)(2,1)}, bf16[256,1536]{1,0:T(8,128)(2,1)S(1)}, u32[]{:S(2)}, u32[]{:S(2)}) collective-permute-start(bf16[256,1536]{1,0:T(8,128)(2,1)} %fusion.58), channel_id=1, source_target_pairs={{0,16},{4,12},{8,0},{12,28},{16,24},{20,4},{24,8},{28,20},{1,17},{... | collective-permute-start | bytes 2359304 | tf_op jit(solution)/shard_map/ppermute | solution.py:393
  (85 other events, 805.2 us)
Sparse Core Ops, SparseCore 0:
  14.1 49.3 all-gather.5
  98.3 25.6 all-gather.7
  125.9 81.9 all-gather.9
  210.3 59.1 all-gather.13
  271.8 55.1 all-gather.11
  442.1 80.8 reduce-scatter.3
  526.9 103.8 reduce-scatter.7
  634.2 80.4 reduce-scatter.5

commit v3 on v2

--- a/solution.py
+++ b/solution.py
@@ -1,4 +1,5 @@
 import functools
+import itertools
 
 import jax
 import jax.numpy as jnp
@@ -9,7 +10,6 @@
 
 HD = 64
 LANES = 128
-CHUNKS = 1
 
 EPSILON = 1e-05
 HALF_ROOT = 0.7071067811865476
@@ -225,6 +225,25 @@
     )(own, kpos, meta, lse, qkv, qkv, qkv, upstream)
 
 
+def place_kernel(*refs, moves):
+    *sources, target = refs
+    for which, source, destination in moves:
+        target[destination] = sources[which][source]
+
+
+def placed(values, shape, moves, name):
+    size = 2 * values[0].size * len(values)
+    return pl.pallas_call(
+        functools.partial(place_kernel, moves=moves),
+        in_specs=[pl.BlockSpec(memory_space=pltpu.VMEM)] * len(values),
+        out_specs=pl.BlockSpec(memory_space=pltpu.VMEM),
+        out_shape=jax.ShapeDtypeStruct(shape, BF16),
+        compiler_params=pltpu.CompilerParams(vmem_limit_bytes=32 << 20),
+        cost_estimate=pl.CostEstimate(flops=0, bytes_accessed=2 * size, transcendentals=0),
+        name=name,
+    )(*values)
+
+
 def per_device(
     layer_in,
     doc_ids,
@@ -253,11 +272,8 @@
     embed = w_qkv.shape[2]
     pairs = embed // LANES
     groups = seq_count // pairs
-    chunks = CHUNKS
-    while (micro * rows // chunks) % groups:
-        chunks //= 2
-    chunk_rows = micro * rows // chunks
-    units = chunk_rows // groups
+    units = micro * rows // groups
+    tokens = micro * rows * short
     size = slot_dev * max(1, 256 // slot_dev)
     seq_index = lax.axis_index("seq")
     mdl_index = lax.axis_index("mdl")
@@ -268,17 +284,17 @@
         + behind[None, :, None] * short
         + jnp.arange(short, dtype=jnp.int32)
     ).reshape(slots)
-    docs = doc_ids.reshape(chunks, groups, units, slots)
-    docs = lax.dynamic_index_in_dim(docs, seq_index % groups, 1, False)
+    docs = doc_ids.reshape(groups, units, slots)
+    docs = lax.dynamic_index_in_dim(docs, seq_index % groups, 0, False)
     first = jnp.sum(
         ((docs[..., None, :] >= 0) & (docs[..., None, :] < docs[..., :, None])).astype(jnp.int32), -1
     )
     first = jnp.where(docs >= 0, first, jnp.arange(slots, dtype=jnp.int32))
-    first = first.reshape(chunks, units, seq_count, mdl_count, short)
+    first = first.reshape(units, seq_count, mdl_count, short)
     first = jnp.stack(
-        [lax.dynamic_index_in_dim(first, behind[j], 3, False) for j in range(mdl_count)], 3
-    ).reshape(chunks, units, slots)
-    meta = jnp.stack([first, jnp.broadcast_to(order, first.shape)], 2)
+        [lax.dynamic_index_in_dim(first, behind[j], 2, False) for j in range(mdl_count)], 2
+    ).reshape(units, slots)
+    meta = jnp.stack([first, jnp.broadcast_to(order, first.shape)], 1)
     kpos = order[:, None]
     own = mdl_index.reshape(1).astype(jnp.int32)
 
@@ -289,27 +305,54 @@
         shape = (seq_count * mdl_count, units, short, LANES)
         return lax.all_to_all(value.reshape(shape), ("seq", "mdl"), 0, 0, tiled=True)
 
+    def row_tile(group, unit):
+        start = (group * units + unit) * short
+        return slice(start, start + short)
+
+    def column_tile(index, pair):
+        start = (index * pairs + pair) * LANES
+        return slice(start, start + LANES)
+
+    spots = list(itertools.product(range(groups), range(units), range(pairs)))
+
     def own_heads(value):
-        value = value.reshape(pairs, groups, mdl_count, units, short, LANES)
-        return value.transpose(1, 3, 4, 2, 0, 5).reshape(chunk_rows * short, mdl_count * embed)
+        moves = [
+            (0, ((p * groups + g) * mdl_count + m, u), (row_tile(g, u), column_tile(m, p)))
+            for g, u, p in spots
+            for m in range(mdl_count)
+        ]
+        return placed([value], (tokens, mdl_count * embed), moves, "own_heads")
 
     def own_units(value):
-        value = value.reshape(groups, units, short, mdl_count, pairs, LANES)
-        return value.transpose(4, 0, 3, 1, 2, 5).reshape(-1, units, short, LANES)
-
-    def to_units(value, kinds):
-        value = value.reshape(mdl_count, groups, units, short, kinds, pairs, LANES)
-        value = value.transpose(5, 1, 4, 2, 0, 3, 6)
-        return value.reshape(seq_count, kinds, units, mdl_count, short, LANES)
-
-    def from_units(value, kinds):
-        value = value.reshape(pairs, groups, kinds, units, mdl_count, short, LANES)
-        value = value.transpose(4, 1, 3, 5, 2, 0, 6)
-        return value.reshape(mdl_count * chunk_rows * short, kinds * embed)
+        moves = [
+            (0, (row_tile(g, u), column_tile(m, p)), ((p * groups + g) * mdl_count + m, u))
+            for g, u, p in spots
+            for m in range(mdl_count)
+        ]
+        shape = (seq_count * mdl_count, units, short, LANES)
+        return placed([value], shape, moves, "own_units")
+
+    def to_units(values):
+        moves = [
+            (j, (row_tile(g, u), column_tile(k, p)), (p * groups + g, k, u, j))
+            for g, u, p in spots
+            for k in range(3)
+            for j in range(mdl_count)
+        ]
+        shape = (seq_count, 3, units, mdl_count, short, LANES)
+        return placed(values, shape, moves, "to_units")
+
+    def from_units(value):
+        moves = [
+            (0, (p * groups + g, k, u, j), (j, row_tile(g, u), column_tile(k, p)))
+            for g, u, p in spots
+            for k in range(3)
+            for j in range(mdl_count)
+        ]
+        return placed([value], (mdl_count, tokens, 3 * embed), moves, "from_units")
 
     ring = [(i, (i + 1) % mdl_count) for i in range(mdl_count)]
     members = range(mdl_count)
-    tokens = micro * rows * short
 
     def pass_on(value):
         return lax.ppermute(value, "mdl", ring)
@@ -398,7 +441,6 @@
     total_tokens = micro * rows * slots
     weight_rate = 0.02 * total_tokens ** (-0.5)
     norm_rate = 0.15 * total_tokens ** (-0.5)
-    each = range(chunks)
     inputs = layer_in.reshape(tokens, width)
     upstream = cotangent.reshape(tokens, width)
 
@@ -407,105 +449,123 @@
     normed, low_qkv = tied(normed.astype(BF16), low_qkv)
     full_qkv = spread(low_qkv)
     rows_one = ring_gather(normed)
-    low_up, full_qkv = tied(w_up.astype(BF16), full_qkv)
+    low_out, (full_qkv, rows_one[1]) = tied(w_out.astype(BF16), (full_qkv, rows_one[1]))
+    wide = lax.all_gather(low_out, "mdl", axis=1, tiled=True)
+    wide, rows_one[-1] = tied(wide, rows_one[-1])
+    full_out = spread(wide)
+    units_in = to_units([dot(part, full_qkv, ((1,), (0,))).astype(BF16) for part in rows_one])
+    low_up, units_in = tied(w_up.astype(BF16), units_in)
     full_up = spread(low_up)
-    projected = [dot(part, full_qkv, ((1,), (0,))).astype(BF16) for part in rows_one]
-    low_out, projected = tied(w_out.astype(BF16), projected)
-    full_out = spread(lax.all_gather(low_out, "mdl", axis=1, tiled=True))
-    projected = jnp.stack(projected).reshape(mdl_count, chunks, -1, 3 * embed)
     held["one"] = rows_one[-1]
-    held["qkv"] = [exchange(to_units(projected[:, c], 3)) for c in each]
     back = behind(upstream.astype(BF16), "one")
     rows_one[-1] = held["one"]
     rows_back = [back, pass_on(back)]
-    rows_back.append(pass_on(behind(rows_back[-1], "qkv")))
-
-    seen = [attention(own, held["qkv"][c], kpos, meta[c], size) for c in each]
-    held["seen"] = seen
-    full_down = spread(behind(w_down.astype(BF16), "seen"))
-    for _ in members[3:]:
-        rows_back.append(pass_on(behind(rows_back[-1], "seen")))
-    seen = held["seen"]
-    attended = [own_heads(exchange_all(value[0])) for value in seen]
-    attended = jnp.concatenate(attended, 0)
+    qkv = exchange(units_in)
+    for j in members[2:]:
+        rows_back.append(pass_on(rows_back[-1]))
+    qkv, rows_back[-2] = tied(qkv, rows_back[-2])
+    rows_back[-1] = pass_on(rows_back[-2])
+
+    heads, lse = attention(own, qkv, kpos, meta, size)
+    low_down, held["lse"] = tied(w_down.astype(BF16), lse)
+    full_down = spread(low_down)
+    heads = exchange_all(heads)
+    heads, (full_up, rows_back[-1]) = tied(heads, (full_up, rows_back[-1]))
+    attended = own_heads(heads)
     middle = inputs + dot(attended, full_out, ((1,), (1,)))
     normed, hat_two, inv_two = norm_forward(middle, norm_params[2], norm_params[3])
     normed = normed.astype(BF16)
-    normed, rows_back[-1] = tied(normed, rows_back[-1])
-
-    rows_two = ring_gather(normed)
-    hidden, up_back, second = [], [], []
-    for j in members:
+
+    rows_two = [normed]
+    hidden, up_back, second = [None] * mdl_count, [None] * mdl_count, [None] * mdl_count
+
+    def feed(j):
         up_proj = dot(rows_two[j], full_up, ((1,), (0,)))
         cdf = 0.5 * (1.0 + lax.erf(up_proj * HALF_ROOT))
         slope = cdf + up_proj * jnp.exp(-0.5 * up_proj * up_proj) * INV_ROOT_TWO_PI
-        hidden.append((up_proj * cdf).astype(BF16))
-        up_back.append((dot(rows_back[j], full_down, ((1,), (0,))) * slope).astype(BF16))
-        second.append(dot(up_back[j], full_up, ((1,), (1,))))
-    second_sum = ring_scatter(second)
-    branch = [dot(value, full_down, ((1,), (1,))) for value in hidden]
+        hidden[j] = (up_proj * cdf).astype(BF16)
+        up_back[j] = (dot(rows_back[j], full_down, ((1,), (0,))) * slope).astype(BF16)
+        second[j] = dot(up_back[j], full_up, ((1,), (1,)))
+
+    for j in members[1:]:
+        ahead = rows_two[-1]
+        if j > 2:
+            ahead, hidden[j - 2] = tied(ahead, hidden[j - 2])
+            rows_two[-1] = ahead
+        rows_two.append(pass_on(ahead))
+        feed(j)
+    feed(0)
+    terms = ring_terms(second)
+    term = next(terms)
+    for j in members[2:]:
+        carried = pass_on(term)
+        term = terms.send(carried)
+        if j == 2:
+            rows_back[0], term = tied(rows_back[0], term)
+    rows_two[0], term = tied(rows_two[0], term)
+    second_sum = pass_on(term)
     down_part = grad(jnp.concatenate(rows_back, 0), jnp.concatenate(hidden, 0))
     up_part = grad(jnp.concatenate(rows_two, 0), jnp.concatenate(up_back, 0))
-    second_sum, (down_part, up_part, branch) = tied(second_sum, (down_part, up_part, branch))
-    held["down"], held["up"] = shared(down_part), shared(up_part)
+    second_sum, (down_part, up_part) = tied(second_sum, (down_part, up_part))
+    held["down"] = shared(down_part)
     second_in = second[0] + second_sum.astype(F32)
     middle_grad = upstream + norm_backward(second_in, hat_two, inv_two, norm_params[2])
     middle_low = middle_grad.astype(BF16)
 
     attended_back = dot(middle_low, full_out, ((1,), (0,))).astype(BF16)
-    held["back"] = attended_back
-    terms = ring_terms(branch)
-    carried = pass_on(next(terms))
-    attended_back = held["back"].reshape(chunks, -1, mdl_count * embed)
-    held["unit"] = [exchange_all(own_units(attended_back[c])) for c in each]
-    carried = pass_on(terms.send(behind(carried, "unit")))
-    held["out"] = shared(grad(behind(middle_low, "unit"), attended))
-    held["attg"] = [
-        attention_back(
-            own,
-            held["qkv"][c],
-            held["unit"][c].reshape(seq_count, mdl_count, units, short, LANES),
-            held["seen"][c][1],
-            kpos,
-            meta[c],
-            size,
-        )
-        for c in each
-    ]
+    hidden, attended_back = tied(hidden, attended_back)
+    branch = [dot(value, full_down, ((1,), (1,))) for value in hidden]
+    held["unit"] = exchange_all(own_units(attended_back))
+    branch_terms = ring_terms(branch)
+    held["unit"], branch[:] = tied(held["unit"], branch)
+    carried = pass_on(behind(next(branch_terms), "unit"))
+    out_part = grad(behind(middle_low, "unit"), attended)
+    held["attg"] = attention_back(
+        own,
+        qkv,
+        held["unit"].reshape(seq_count, mdl_count, units, short, LANES),
+        held["lse"],
+        kpos,
+        meta,
+        size,
+    )
+    for _ in members[2:-1]:
+        carried = pass_on(branch_terms.send(behind(carried, "attg")))
+    proj_back = from_units(exchange(held["attg"]))
+    proj_back, (up_part, out_part) = tied(proj_back, (up_part, out_part))
+    held["out"] = shared(out_part)
+    first = [dot(proj_back[j], full_qkv, ((1,), (1,))) for j in members]
+    first_terms = ring_terms(first)
+    term = next(first_terms)
+    (proj_back, up_part), term = tied((proj_back.reshape(-1, 3 * embed), up_part), term)
+    held["up"] = shared(up_part)
+    first_sum, first[:] = tied(pass_on(term), first)
+    qkv_part = grad(jnp.concatenate(rows_one, 0), proj_back)
+    term = first_terms.send(first_sum)
     for _ in members[3:]:
-        carried = pass_on(terms.send(behind(carried, "attg")))
-    proj_back = [
-        from_units(exchange(value), 3).reshape(mdl_count, -1, 3 * embed) for value in held["attg"]
-    ]
-    proj_back = jnp.concatenate(proj_back, 1)
-    proj_back = behind(proj_back, "down")
-    proj_back, carried = tied(proj_back, carried)
+        term = first_terms.send(pass_on(term))
+    first_sum, qkv_part = tied(pass_on(term), qkv_part)
+    held["qkv_grad"] = share(qkv_part)
+    columns = jnp.stack(jnp.split(held["out"].astype(BF16), mdl_count, 1))
+    columns = lax.all_to_all(columns, "mdl", 0, 0, tiled=True)
+    held["out_grad"] = jnp.sum(columns.astype(F32), 0)
+    second_late, first[0] = tied((second_in, hat_two), first[0])
+    second_sums = [jnp.sum(second_late[0] * second_late[1], 0), jnp.sum(second_late[0], 0)]
+    held["sums"] = second_sums
+    first_sum = behind(first_sum, "down", "sums")
+    carried, first_sum = tied(carried, first_sum)
+    carried = pass_on(branch_terms.send(carried))
     layer_out = middle + (branch[0] + carried.astype(F32))
-    first = [dot(proj_back[j], full_qkv, ((1,), (1,))) for j in members]
-    proj_back, first[1] = tied(proj_back.reshape(-1, 3 * embed), first[1])
-    first_sum = ring_scatter(first)
-    held["qkv_grad"] = share(grad(jnp.concatenate(rows_one, 0), proj_back))
-    columns = [
-        lax.dynamic_slice_in_dim(held["out"], embed * ((mdl_index - j) % mdl_count), embed, 1)
-        for j in members
-    ]
-    held["out_grad"] = columns[0] + ring_scatter(columns).astype(F32)
-    first_sum = behind(first_sum, "up", "out_grad", "qkv_grad")
     down_grad, up_grad = held["down"], held["up"]
     out_grad, qkv_grad = held["out_grad"], held["qkv_grad"]
     first_in = first[0] + first_sum.astype(F32)
     input_grad = middle_grad + norm_backward(first_in, hat_one, inv_one, norm_params[0])
-    norm_total = whole_sum(
-        jnp.stack(
-            [
-                jnp.sum(first_in * hat_one, 0),
-                jnp.sum(first_in, 0),
-                jnp.sum(second_in * hat_two, 0),
-                jnp.sum(second_in, 0),
-            ]
-        ),
-        ("mdl", "seq"),
-    )
+    norm_sums = jnp.stack(
+        [jnp.sum(first_in * hat_one, 0), jnp.sum(first_in, 0), *held["sums"]]
+    )
+    norm_sums, (qkv_grad, out_grad, layer_out) = tied(norm_sums, (qkv_grad, out_grad, layer_out))
+    norm_total = whole_sum(norm_sums, ("mdl", "seq"))
+
     def updated(weight, total, moment, average):
         if weight.ndim == 2:
             return update_param(weight, total, moment, average, weight_rate)

time: 798 us -> 778 us (0.975)
  local copies, waits for them, and re-layouts: 42.3 us -> 21.8 us
  starting transfers between devices: 50.5 us -> 35.3 us
  waiting for transfers between devices: 394 us -> 402 us
    ppermute x21 -> x18, waiting for transfers between devices: 220 us -> 289 us  [pass_on(): return lax.ppermute(value, 'mdl', ring)]
    all_to_all x2, waiting for transfers between devices: 49 us -> 7.24 us  [exchange_all(): lax.all_to_all(value.reshape(shape), ('seq', 'mdl'), 0, 0, tiled=True)]
    all_gather x1, waiting for transfers between devices: 25.8 us -> 2.57 us  [per_device(): wide = lax.all_gather(low_out, 'mdl', axis=1, tiled=True)]
    all_to_all x2, waiting for transfers between devices: 49.6 us -> 30.6 us  [exchange(): return lax.all_to_all(value, 'seq', 0, 0, tiled=True)]
    ppermute x1, waiting for transfers between devices: 0.01 us -> 16.9 us  [share(): carried = lax.ppermute(term(1).astype(BF16), 'seq', onward)]
    ppermute x21 -> x18, starting transfers between devices: 26 us -> 11.3 us  [pass_on(): return lax.ppermute(value, 'mdl', ring)]
    reduce_scatter x3, waiting for transfers between devices: 13.8 us -> 0.01 us  [shared(): lax.psum_scatter(value, 'seq', scatter_dimension=0, tiled=True).astype(F32)]
    another operation x12 -> x3, local copies, waits for them, and re-layouts: 12.6 us -> 1.38 us  [the longest x1 1.26 us: per_device(): columns = jnp.stack(jnp.split(held['out'].astype(BF16), mdl_count, 1))]
  transfers between devices with their start and end apart: 42 -> 40, of which waited for: 27 -> 29; matrix products, arithmetic and copies ran while one was open for 30% -> 29% of each run, Pallas kernels for 5% -> 5%
where the time goes in v3:
time: 778 us; the launch traced here: 770 us
  waiting for transfers between devices  402 us (52%)
  matrix products  172 us (22%)
  other arithmetic  63 us (8%)
  Pallas kernels  43.7 us (6%)
  starting transfers between devices  35.3 us (5%)
  between operations  31.5 us (4%)
  local copies, waits for them, and re-layouts  21.8 us (3%)
    ppermute x18, waiting for transfers between devices, pass_on(): return lax.ppermute(value, 'mdl', ring)  289 us
    dot_general x30, matrix products, dot(): return lax.dot_general(a, b, (dims, ((), ())), preferred_element_type=F32)  172 us
    all_to_all x2, waiting for transfers between devices, exchange(): return lax.all_to_all(value, 'seq', 0, 0, tiled=True)  30.6 us
    ppermute x2, waiting for transfers between devices, share(): lax.ppermute((term(j) + carried.astype(F32)).astype(BF16), 'seq', onward)  23.8 us
    pallas_call x1, Pallas kernels, attention_back(): pl.pallas_call(functools.partial(attend_back_kernel, size=size, factor=HD...  22.2 us
    pallas_call x1, Pallas kernels, attention(): pl.pallas_call(functools.partial(attend_kernel, size=size, factor=HD ** (...  17.4 us
    ppermute x1, waiting for transfers between devices, share(): carried = lax.ppermute(term(1).astype(BF16), 'seq', onward)  16.9 us
  transfers between devices with their start and end apart: 40, of which 29 were waited for; matrix products, arithmetic and copies ran while one was open for 29% of the time, Pallas kernels for 5%

profile of v3, /device:TPU:0, one launch (start us, length us, event | category | flops | bytes accessed | tf_op | source)
XLA Modules:
  0.0 769.5 jit_solution(3383245539266270888)
XLA Ops:
  17.2 25.5 %collective-permute-done = bf16[256,2048]{1,0:T(8,128)(2,1)} collective-permute-done((bf16[256,2048]{1,0:T(8,128)(2,1)}, bf16[256,2048]{1,0:T(8,128)(2,1)}, u32[]{:S(2)}, u32[]{:S(2)}) %collective-permute-start) | collective-permute-done | bytes 1048608 | tf_op jit(solution)/shard_map/ppermute | solution.py:358
  46.2 22.9 %collective-permute-done.1 = bf16[256,2048]{1,0:T(8,128)(2,1)} collective-permute-done((bf16[256,2048]{1,0:T(8,128)(2,1)}, bf16[256,2048]{1,0:T(8,128)(2,1)}, u32[]{:S(2)}, u32[]{:S(2)}) %collective-permute-start.1) | collective-permute-done | bytes 1048608 | tf_op jit(solution)/shard_map/ppermute | solution.py:358
  80.2 29.1 %collective-permute-done.2 = bf16[256,2048]{1,0:T(8,128)(2,1)} collective-permute-done((bf16[256,2048]{1,0:T(8,128)(2,1)}, bf16[256,2048]{1,0:T(8,128)(2,1)}, u32[]{:S(2)}, u32[]{:S(2)}) %collective-permute-start.2) | collective-permute-done | bytes 1048608 | tf_op jit(solution)/shard_map/ppermute | solution.py:358
  133.8 20.1 %collective-permute-done.3 = bf16[256,2048]{1,0:T(8,128)(2,1)} collective-permute-done((bf16[256,2048]{1,0:T(8,128)(2,1)}, bf16[256,2048]{1,0:T(8,128)(2,1)}, u32[]{:S(2)}, u32[]{:S(2)}) %collective-permute-start.3) | collective-permute-done | bytes 1048608 | tf_op jit(solution)/shard_map/ppermute | solution.py:358
  163.0 17.8 %collective-permute-done.4 = bf16[256,2048]{1,0:T(8,128)(2,1)} collective-permute-done((bf16[256,2048]{1,0:T(8,128)(2,1)}, bf16[256,2048]{1,0:T(8,128)(2,1)}, u32[]{:S(2)}, u32[]{:S(2)}) %collective-permute-start.4) | collective-permute-done | bytes 1048608 | tf_op jit(solution)/shard_map/ppermute | solution.py:358
  182.2 17.4 %attend.1 = (bf16[8,4,4,32,128]{4,3,2,1,0:T(8,128)(2,1)S(1)}, f32[4,2,1024]{2,1,0:T(2,128)S(1)}) custom-call(s32[1]{0:T(128)} %bitcast.5.own_ref, s32[1024,1]{1,0:T(8,128)S(1)} %copy-done.6, s32[4,2,1024]{2,1,0:T(2,128)S(1)} %pad_add_fusion.1.meta_ref, bf16[8,3,4,4,32,128]{5,4,3,2,1,0:T(8,128)(2,1)S(1)} %all-to-all-done.q_ref.k_ref.v_ref, ...), custom_call_target="tpu_custom_call" | custom-call | flops 5368709120 | bytes 4194304 | tf_op jit(solution)/shard_map/attend/pallas_call | solution.py:176
  205.2 42.2 %collective-permute-done.5 = bf16[256,2048]{1,0:T(8,128)(2,1)S(1)} collective-permute-done((bf16[256,2048]{1,0:T(8,128)(2,1)}, bf16[256,2048]{1,0:T(8,128)(2,1)S(1)}, u32[]{:S(2)}, u32[]{:S(2)}) %collective-permute-start.5) | collective-permute-done | bytes 1048608 | tf_op jit(solution)/shard_map/ppermute | solution.py:358
  251.1 10.8 %all-gather.14.cloned.1.call-done = bf16[2048,2048]{1,0:T(8,128)(2,1)} async-done(((bf16[256,2048]{1,0:T(8,128)(2,1)}), bf16[2048,2048]{1,0:T(8,128)(2,1)}) %all-gather.14.cloned.1.call-update) | async-done | bytes 8388624 | tf_op jit(solution)/shard_map/all_gather | solution.py:393
  271.0 26.0 %collective-permute-done.6 = bf16[256,2048]{1,0:T(8,128)(2,1)S(1)} collective-permute-done((bf16[256,2048]{1,0:T(8,128)(2,1)S(1)}, bf16[256,2048]{1,0:T(8,128)(2,1)S(1)}, u32[]{:S(2)}, u32[]{:S(2)}) %collective-permute-start.6) | collective-permute-done | bytes 1048608 | tf_op jit(solution)/shard_map/ppermute | solution.py:358
  305.6 18.1 %collective-permute-done.7 = bf16[256,2048]{1,0:T(8,128)(2,1)} collective-permute-done((bf16[256,2048]{1,0:T(8,128)(2,1)S(1)}, bf16[256,2048]{1,0:T(8,128)(2,1)}, u32[]{:S(2)}, u32[]{:S(2)}) %collective-permute-start.7) | collective-permute-done | bytes 1048608 | tf_op jit(solution)/shard_map/ppermute | solution.py:358
  329.1 7.0 fusion.40
  360.6 11.2 %collective-permute-done.9 = bf16[256,2048]{1,0:T(8,128)(2,1)S(1)} collective-permute-done((bf16[256,2048]{1,0:T(8,128)(2,1)S(1)}, bf16[256,2048]{1,0:T(8,128)(2,1)S(1)}, u32[]{:S(2)}, u32[]{:S(2)}) %collective-permute-start.9) | collective-permute-done | bytes 1048608 | tf_op jit(solution)/shard_map/ppermute | solution.py:358
  376.6 12.5 %convolution_convert_fusion.3 = bf16[2048,2048]{1,0:T(8,128)(2,1)} fusion(bf16[256,2048]{1,0:T(8,128)(2,1)S(1)} %copy-done.59, bf16[256,2048]{1,0:T(8,128)(2,1)} %collective-permute-done.4, bf16[256,2048]{1,0:T(8,128)(2,1)} %collective-permute-done.3, bf16[256,2048]{1,0:T(8,128)(2,1)} %bitcast_convert_fusion, bf16[256,2048]{1,0:T(8,128)(2,1)S(1)} %get-tuple-element.122, ...), kind=kOutput, calls=%fused_computation.4 | convolution fusion | flops 8627683328 | bytes 16777216 | tf_op jit(solution)/shard_map/dot_general | solution.py:46
  389.2 12.2 %collective-permute-done.10 = bf16[256,2048]{1,0:T(8,128)(2,1)} collective-permute-done((bf16[256,2048]{1,0:T(8,128)(2,1)}, bf16[256,2048]{1,0:T(8,128)(2,1)}, u32[]{:S(2)}, u32[]{:S(2)}) %collective-permute-start.10) | collective-permute-done | bytes 1048608 | tf_op jit(solution)/shard_map/ppermute | solution.py:358
  401.3 7.2 fusion.35
  408.9 12.4 %convolution_convert_fusion.2 = bf16[2048,2048]{1,0:T(8,128)(2,1)} fusion(bf16[256,2048]{1,0:T(8,128)(2,1)} %collective-permute-done.8, bf16[256,2048]{1,0:T(8,128)(2,1)} %collective-permute-done.7, bf16[256,2048]{1,0:T(8,128)(2,1)S(1)} %copy-done.61, bf16[256,2048]{1,0:T(8,128)(2,1)S(1)} %get-tuple-element.116, bf16[256,2048]{1,0:T(8,128)(2,1)S(1)} %copy-done.71, ...), kind=kOutput, calls=%fused_computation.3 | convolution fusion | flops 8627683328 | bytes 16777216 | tf_op jit(solution)/shard_map/dot_general | solution.py:46
  421.3 11.4 %collective-permute-done.11 = bf16[256,2048]{1,0:T(8,128)(2,1)} collective-permute-done((bf16[256,2048]{1,0:T(8,128)(2,1)}, bf16[256,2048]{1,0:T(8,128)(2,1)}, u32[]{:S(2)}, u32[]{:S(2)}) %collective-permute-start.11) | collective-permute-done | bytes 1048608 | tf_op jit(solution)/shard_map/ppermute | solution.py:358
  432.7 7.2 multiply_reduce_fusion.7
  443.2 6.7 convolution_convert_fusion.8.refs_0_
  454.2 7.9 %fusion.100 = f32[256,2048]{1,0:T(8,128)} fusion(bf16[256,2048]{1,0:T(8,128)(2,1)S(1)} %copy-done.69, bf16[2048,2048]{1,0:T(8,128)(2,1)} %all-gather.10.cloned.1.call-done), kind=kOutput, calls=%fused_computation.210 | convolution fusion | flops 2147483648 | bytes 11534336 | tf_op jit(solution)/shard_map/dot_general | solution.py:46
  462.2 7.2 fusion.99
  482.5 22.2 %attend_back.1 = bf16[8,3,4,4,32,128]{5,4,3,2,1,0:T(8,128)(2,1)S(1)} custom-call(s32[1]{0:T(128)} %bitcast.5.own_ref, s32[1024,1]{1,0:T(8,128)S(1)} %copy-done.7, s32[4,2,1024]{2,1,0:T(2,128)S(1)} %pad_add_fusion.1.meta_ref, f32[4,2,1024]{2,1,0:T(2,128)S(1)} %get-tuple-element.126.lse_ref, bf16[8,3,4,4,32,128]{5,4,3,2,1,0:T(8,128)(2,1)} %copy-done.1, ...), custom_call_target="tpu_custom_call" | custom-call | flops 13421772800 | bytes 8388608 | tf_op jit(solution)/shard_map/attend_back/pallas_call | solution.py:206
  510.8 7.3 convolution_convert_fusion.1
  518.1 30.6 %all-to-all-done.3.refs_0_ = bf16[8,3,4,4,32,128]{5,4,3,2,1,0:T(8,128)(2,1)S(1)} async-done(((bf16[8,3,4,4,32,128]{5,4,3,2,1,0:T(8,128)(2,1)}), bf16[8,3,4,4,32,128]{5,4,3,2,1,0:T(8,128)(2,1)S(1)}, u32[]{:S(2)}, u32[]{:S(2)}) %all-to-all-start.3) | async-done | bytes 3145760 | tf_op jit(solution)/shard_map/all_to_all | solution.py:302
  557.0 7.4 fusion.69
  569.3 10.8 %collective-permute-done.13 = bf16[256,2048]{1,0:T(8,128)(2,1)S(1)} collective-permute-done((bf16[256,2048]{1,0:T(8,128)(2,1)S(1)}, bf16[256,2048]{1,0:T(8,128)(2,1)S(1)}, u32[]{:S(2)}, u32[]{:S(2)}) %collective-permute-start.13) | collective-permute-done | bytes 1048608 | tf_op jit(solution)/shard_map/ppermute | solution.py:358
  581.5 22.6 %collective-permute-done.15 = bf16[256,2048]{1,0:T(8,128)(2,1)} collective-permute-done((bf16[256,2048]{1,0:T(8,128)(2,1)}, bf16[256,2048]{1,0:T(8,128)(2,1)}, u32[]{:S(2)}, u32[]{:S(2)}) %collective-permute-start.15) | collective-permute-done | bytes 1048608 | tf_op jit(solution)/shard_map/ppermute | solution.py:358
  606.3 8.4 %convolution_convert_fusion = bf16[2048,1536]{1,0:T(8,128)(2,1)S(1)} fusion(bf16[1024,1536]{1,0:T(8,128)(2,1)S(1)} %bitcast.173, bf16[256,2048]{1,0:T(8,128)(2,1)} %collective-permute-done.2, bf16[256,2048]{1,0:T(8,128)(2,1)} %collective-permute-done.1, bf16[256,2048]{1,0:T(8,128)(2,1)} %collective-permute-done, bf16[256,2048]{1,0:T(8,128)(2,1)S(1)} %copy-done.40), kind=kOutput, calls=%fused_computation.1 | convolution fusion | flops 6462373888 | bytes 13631488 | tf_op jit(solution)/shard_map/dot_general | solution.py:46
  614.7 12.9 %collective-permute-done.16 = bf16[256,2048]{1,0:T(8,128)(2,1)S(1)} collective-permute-done((bf16[256,2048]{1,0:T(8,128)(2,1)S(1)}, bf16[256,2048]{1,0:T(8,128)(2,1)S(1)}, u32[]{:S(2)}, u32[]{:S(2)}) %collective-permute-start.16) | collective-permute-done | bytes 1048608 | tf_op jit(solution)/shard_map/ppermute | solution.py:358
  667.4 16.9 %collective-permute-done.18 = bf16[256,1536]{1,0:T(8,128)(2,1)} collective-permute-done((bf16[256,1536]{1,0:T(8,128)(2,1)}, bf16[256,1536]{1,0:T(8,128)(2,1)}, u32[]{:S(2)}, u32[]{:S(2)}) %collective-permute-start.18) | collective-permute-done | bytes 786464 | tf_op jit(solution)/shard_map/ppermute | solution.py:436
  688.1 20.6 %collective-permute-done.19 = bf16[256,1536]{1,0:T(8,128)(2,1)S(1)} collective-permute-done((bf16[256,1536]{1,0:T(8,128)(2,1)S(1)}, bf16[256,1536]{1,0:T(8,128)(2,1)S(1)}, u32[]{:S(2)}, u32[]{:S(2)}) %collective-permute-start.19) | collective-permute-done | bytes 786464 | tf_op jit(solution)/shard_map/ppermute | solution.py:438
  732.4 9.9 %all-to-all-done.4 = bf16[4,256,512]{2,1,0:T(8,128)(2,1)S(1)} async-done(((bf16[4,256,512]{2,1,0:T(8,128)(2,1)}), bf16[4,256,512]{2,1,0:T(8,128)(2,1)S(1)}, u32[]{:S(2)}, u32[]{:S(2)}) %all-to-all-start.4) | async-done | bytes 1048608 | tf_op jit(solution)/shard_map/all_to_all | solution.py:550
  (340 shorter events, 235.4 us)
Async XLA Ops:
  7.2 61.9 %all-gather.6.cloned.1.call-start = ((), (), s32[]{:S(2)}) async-start(), calls=%async_computation.8 | async-start | bytes 7077888 | tf_op jit(solution)/shard_map/all_gather | solution.py:393
  14.0 97.8 %all-gather.8.cloned.1.call-start = ((), (), s32[]{:S(2)}) async-start(), calls=%async_computation.9 | async-start | bytes 1310720 | tf_op jit(solution)/shard_map/all_gather | solution.py:453
  14.1 28.6 %collective-permute-start = (bf16[256,2048]{1,0:T(8,128)(2,1)}, bf16[256,2048]{1,0:T(8,128)(2,1)}, u32[]{:S(2)}, u32[]{:S(2)}) collective-permute-start(bf16[256,2048]{1,0:T(8,128)(2,1)} %add_convert_fusion.5), channel_id=1, source_target_pairs={{0,1},{1,2},{2,3},{3,0},{4,5},{5,6},{6,7},{7,4},{8,9},{9,10},{10,1... | collective-permute-start | bytes 3145736 | tf_op jit(solution)/shard_map/ppermute | solution.py:358
  42.7 26.5 %collective-permute-start.1 = (bf16[256,2048]{1,0:T(8,128)(2,1)}, bf16[256,2048]{1,0:T(8,128)(2,1)}, u32[]{:S(2)}, u32[]{:S(2)}) collective-permute-start(bf16[256,2048]{1,0:T(8,128)(2,1)} %collective-permute-done), channel_id=1, source_target_pairs={{0,1},{1,2},{2,3},{3,0},{4,5},{5,6},{6,7},{7,4},{8,9},{9,10},{10,1... | collective-permute-start | bytes 3145736 | tf_op jit(solution)/shard_map/ppermute | solution.py:358
  69.1 40.1 %collective-permute-start.2 = (bf16[256,2048]{1,0:T(8,128)(2,1)}, bf16[256,2048]{1,0:T(8,128)(2,1)}, u32[]{:S(2)}, u32[]{:S(2)}) collective-permute-start(bf16[256,2048]{1,0:T(8,128)(2,1)} %collective-permute-done.1), channel_id=1, source_target_pairs={{0,1},{1,2},{2,3},{3,0},{4,5},{5,6},{6,7},{7,4},{8,9},{9,10},{10,1... | collective-permute-start | bytes 3145736 | tf_op jit(solution)/shard_map/ppermute | solution.py:358
  69.2 181.7 %all-gather.12.cloned.1.call-start = ((), (), s32[]{:S(2)}) async-start(), calls=%async_computation.11 | async-start | bytes 9437184 | tf_op jit(solution)/shard_map/all_gather | solution.py:393
  119.1 142.9 %all-gather.14.cloned.1.call-start = ((), (), s32[]{:S(2)}) async-start(), calls=%async_computation.12 | async-start | bytes 9437184 | tf_op jit(solution)/shard_map/all_gather | solution.py:393
  119.6 61.2 %all-to-all-start = ((bf16[8,3,4,4,32,128]{5,4,3,2,1,0:T(8,128)(2,1)}), bf16[8,3,4,4,32,128]{5,4,3,2,1,0:T(8,128)(2,1)S(1)}, u32[]{:S(2)}, u32[]{:S(2)}) async-start(bf16[8,3,4,4,32,128]{5,4,3,2,1,0:T(8,128)(2,1)} %to_units.1), calls=%async_computation | async-start | bytes 6291456 | tf_op jit(solution)/shard_map/all_to_all | solution.py:302
  123.3 205.8 %all-gather.10.cloned.1.call-start = ((), (), s32[]{:S(2)}) async-start(), calls=%async_computation.10 | async-start | bytes 9437184 | tf_op jit(solution)/shard_map/all_gather | solution.py:393
  126.4 27.5 %collective-permute-start.3 = (bf16[256,2048]{1,0:T(8,128)(2,1)}, bf16[256,2048]{1,0:T(8,128)(2,1)}, u32[]{:S(2)}, u32[]{:S(2)}) collective-permute-start(bf16[256,2048]{1,0:T(8,128)(2,1)} %bitcast_convert_fusion), channel_id=1, source_target_pairs={{0,1},{1,2},{2,3},{3,0},{4,5},{5,6},{6,7},{7,4},{8,9},{9,10},{10,1... | collective-permute-start | bytes 3145736 | tf_op jit(solution)/shard_map/ppermute | solution.py:358
  153.9 26.9 %collective-permute-start.4 = (bf16[256,2048]{1,0:T(8,128)(2,1)}, bf16[256,2048]{1,0:T(8,128)(2,1)}, u32[]{:S(2)}, u32[]{:S(2)}) collective-permute-start(bf16[256,2048]{1,0:T(8,128)(2,1)} %collective-permute-done.3), channel_id=1, source_target_pairs={{0,1},{1,2},{2,3},{3,0},{4,5},{5,6},{6,7},{7,4},{8,9},{9,10},{10,1... | collective-permute-start | bytes 3145736 | tf_op jit(solution)/shard_map/ppermute | solution.py:358
  200.6 50.3 %all-to-all-start.1 = ((bf16[32,4,32,128]{3,2,1,0:T(8,128)(2,1)}), bf16[32,4,32,128]{3,2,1,0:T(8,128)(2,1)S(1)}, u32[]{:S(2)}, u32[]{:S(2)}) async-start(bf16[32,4,32,128]{3,2,1,0:T(8,128)(2,1)} %bitcast.175), calls=%async_computation.1 | async-start | bytes 2097152 | tf_op jit(solution)/shard_map/all_to_all | solution.py:306
  203.4 447.6 %reduce-scatter.4.cloned.1.call-start = ((), (), s32[]{:S(2)}) async-start(), calls=%async_computation.13 | async-start | bytes 9437184 | tf_op jit(solution)/shard_map/reduce_scatter | solution.py:422
  203.4 44.0 %collective-permute-start.5 = (bf16[256,2048]{1,0:T(8,128)(2,1)}, bf16[256,2048]{1,0:T(8,128)(2,1)S(1)}, u32[]{:S(2)}, u32[]{:S(2)}) collective-permute-start(bf16[256,2048]{1,0:T(8,128)(2,1)} %collective-permute-done.4), channel_id=1, source_target_pairs={{0,1},{1,2},{2,3},{3,0},{4,5},{5,6},{6,7},{7,4},{8,9},{9,10},{10,1... | collective-permute-start | bytes 3145736 | tf_op jit(solution)/shard_map/ppermute | solution.py:358
  269.8 27.1 %collective-permute-start.6 = (bf16[256,2048]{1,0:T(8,128)(2,1)S(1)}, bf16[256,2048]{1,0:T(8,128)(2,1)S(1)}, u32[]{:S(2)}, u32[]{:S(2)}) collective-permute-start(bf16[256,2048]{1,0:T(8,128)(2,1)S(1)} %get-tuple-element.116), channel_id=1, source_target_pairs={{0,1},{1,2},{2,3},{3,0},{4,5},{5,6},{6,7},{7,4},{8,9},{9,10},{10,1... | collective-permute-start | bytes 3145736 | tf_op jit(solution)/shard_map/ppermute | solution.py:358
  296.9 26.8 %collective-permute-start.7 = (bf16[256,2048]{1,0:T(8,128)(2,1)S(1)}, bf16[256,2048]{1,0:T(8,128)(2,1)}, u32[]{:S(2)}, u32[]{:S(2)}) collective-permute-start(bf16[256,2048]{1,0:T(8,128)(2,1)S(1)} %collective-permute-done.6), channel_id=1, source_target_pairs={{0,1},{1,2},{2,3},{3,0},{4,5},{5,6},{6,7},{7,4},{8,9},{9,10},{10,1... | collective-permute-start | bytes 3145736 | tf_op jit(solution)/shard_map/ppermute | solution.py:358
  323.7 29.3 %collective-permute-start.8 = (bf16[256,2048]{1,0:T(8,128)(2,1)}, bf16[256,2048]{1,0:T(8,128)(2,1)}, u32[]{:S(2)}, u32[]{:S(2)}) collective-permute-start(bf16[256,2048]{1,0:T(8,128)(2,1)} %collective-permute-done.7), channel_id=1, source_target_pairs={{0,1},{1,2},{2,3},{3,0},{4,5},{5,6},{6,7},{7,4},{8,9},{9,10},{10,1... | collective-permute-start | bytes 3145736 | tf_op jit(solution)/shard_map/ppermute | solution.py:358
  342.3 29.5 %collective-permute-start.9 = (bf16[256,2048]{1,0:T(8,128)(2,1)S(1)}, bf16[256,2048]{1,0:T(8,128)(2,1)S(1)}, u32[]{:S(2)}, u32[]{:S(2)}) collective-permute-start(bf16[256,2048]{1,0:T(8,128)(2,1)S(1)} %convolution_convert_fusion.9), channel_id=1, source_target_pairs={{0,1},{1,2},{2,3},{3,0},{4,5},{5,6},{6,7},{7,4},{8,9},{9,10},{10,1... | collective-permute-start | bytes 3145736 | tf_op jit(solution)/shard_map/ppermute | solution.py:358
  376.4 25.0 %collective-permute-start.10 = (bf16[256,2048]{1,0:T(8,128)(2,1)}, bf16[256,2048]{1,0:T(8,128)(2,1)}, u32[]{:S(2)}, u32[]{:S(2)}) collective-permute-start(bf16[256,2048]{1,0:T(8,128)(2,1)} %fusion.36), channel_id=1, source_target_pairs={{0,1},{1,2},{2,3},{3,0},{4,5},{5,6},{6,7},{7,4},{8,9},{9,10},{10,1... | collective-permute-start | bytes 3145736 | tf_op jit(solution)/shard_map/ppermute | solution.py:358
  408.6 24.1 %collective-permute-start.11 = (bf16[256,2048]{1,0:T(8,128)(2,1)}, bf16[256,2048]{1,0:T(8,128)(2,1)}, u32[]{:S(2)}, u32[]{:S(2)}) collective-permute-start(bf16[256,2048]{1,0:T(8,128)(2,1)} %fusion.35), channel_id=1, source_target_pairs={{0,1},{1,2},{2,3},{3,0},{4,5},{5,6},{6,7},{7,4},{8,9},{9,10},{10,1... | collective-permute-start | bytes 3145736 | tf_op jit(solution)/shard_map/ppermute | solution.py:358
  451.1 28.1 %all-to-all-start.2 = ((bf16[32,4,32,128]{3,2,1,0:T(8,128)(2,1)}), bf16[32,4,32,128]{3,2,1,0:T(8,128)(2,1)S(1)}, u32[]{:S(2)}, u32[]{:S(2)}) async-start(bf16[32,4,32,128]{3,2,1,0:T(8,128)(2,1)} %own_units.1), calls=%async_computation.2 | async-start | bytes 2097152 | tf_op jit(solution)/shard_map/all_to_all | solution.py:306
  479.2 27.4 %collective-permute-start.12 = (bf16[256,2048]{1,0:T(8,128)(2,1)S(1)}, bf16[256,2048]{1,0:T(8,128)(2,1)}, u32[]{:S(2)}, u32[]{:S(2)}) collective-permute-start(bf16[256,2048]{1,0:T(8,128)(2,1)S(1)} %fusion.98), channel_id=1, source_target_pairs={{0,1},{1,2},{2,3},{3,0},{4,5},{5,6},{6,7},{7,4},{8,9},{9,10},{10,1... | collective-permute-start | bytes 3145736 | tf_op jit(solution)/shard_map/ppermute | solution.py:358
  506.7 42.0 %all-to-all-start.3 = ((bf16[8,3,4,4,32,128]{5,4,3,2,1,0:T(8,128)(2,1)}), bf16[8,3,4,4,32,128]{5,4,3,2,1,0:T(8,128)(2,1)S(1)}, u32[]{:S(2)}, u32[]{:S(2)}) async-start(bf16[8,3,4,4,32,128]{5,4,3,2,1,0:T(8,128)(2,1)} %copy-done.4), calls=%async_computation.3 | async-start | bytes 6291456 | tf_op jit(solution)/shard_map/all_to_all | solution.py:302
  510.7 201.5 %reduce-scatter.6.cloned.1.call-start = ((), (), s32[]{:S(2)}) async-start(), calls=%async_computation.14 | async-start | bytes 9437184 | tf_op jit(solution)/shard_map/reduce_scatter | solution.py:422
  551.0 174.2 %reduce-scatter.8.cloned.1.call-start = ((), (), s32[]{:S(2)}) async-start(), calls=%async_computation.15 | async-start | bytes 9437184 | tf_op jit(solution)/shard_map/reduce_scatter | solution.py:422
  556.7 23.5 %collective-permute-start.13 = (bf16[256,2048]{1,0:T(8,128)(2,1)S(1)}, bf16[256,2048]{1,0:T(8,128)(2,1)S(1)}, u32[]{:S(2)}, u32[]{:S(2)}) collective-permute-start(bf16[256,2048]{1,0:T(8,128)(2,1)S(1)} %fusion.75), channel_id=1, source_target_pairs={{0,1},{1,2},{2,3},{3,0},{4,5},{5,6},{6,7},{7,4},{8,9},{9,10},{10,1... | collective-permute-start | bytes 3145736 | tf_op jit(solution)/shard_map/ppermute | solution.py:358
  581.4 22.6 %collective-permute-start.15 = (bf16[256,2048]{1,0:T(8,128)(2,1)}, bf16[256,2048]{1,0:T(8,128)(2,1)}, u32[]{:S(2)}, u32[]{:S(2)}) collective-permute-start(bf16[256,2048]{1,0:T(8,128)(2,1)} %add_convert_fusion.2), channel_id=1, source_target_pairs={{0,1},{1,2},{2,3},{3,0},{4,5},{5,6},{6,7},{7,4},{8,9},{9,10},{10,1... | collective-permute-start | bytes 3145736 | tf_op jit(solution)/shard_map/ppermute | solution.py:358
  632.7 26.0 %collective-permute-start.14 = (bf16[256,2048]{1,0:T(8,128)(2,1)S(1)}, bf16[256,2048]{1,0:T(8,128)(2,1)}, u32[]{:S(2)}, u32[]{:S(2)}) collective-permute-start(bf16[256,2048]{1,0:T(8,128)(2,1)S(1)} %add_convert_fusion.3), channel_id=1, source_target_pairs={{0,1},{1,2},{2,3},{3,0},{4,5},{5,6},{6,7},{7,4},{8,9},{9,10},{10,1... | collective-permute-start | bytes 3145736 | tf_op jit(solution)/shard_map/ppermute | solution.py:358
  646.5 37.8 %collective-permute-start.18 = (bf16[256,1536]{1,0:T(8,128)(2,1)}, bf16[256,1536]{1,0:T(8,128)(2,1)}, u32[]{:S(2)}, u32[]{:S(2)}) collective-permute-start(bf16[256,1536]{1,0:T(8,128)(2,1)} %fusion.60), channel_id=1, source_target_pairs={{0,16},{4,12},{8,0},{12,28},{16,24},{20,4},{24,8},{28,20},{1,17},{... | collective-permute-start | bytes 2359304 | tf_op jit(solution)/shard_map/ppermute | solution.py:436
  660.4 50.1 %collective-permute-start.21 = (bf16[256,2048]{1,0:T(8,128)(2,1)S(1)}, bf16[256,2048]{1,0:T(8,128)(2,1)S(1)}, u32[]{:S(2)}, u32[]{:S(2)}) collective-permute-start(bf16[256,2048]{1,0:T(8,128)(2,1)S(1)} %add_convert_fusion), channel_id=1, source_target_pairs={{0,1},{1,2},{2,3},{3,0},{4,5},{5,6},{6,7},{7,4},{8,9},{9,10},{10,1... | collective-permute-start | bytes 3145736 | tf_op jit(solution)/shard_map/ppermute | solution.py:358
  686.3 22.4 %collective-permute-start.19 = (bf16[256,1536]{1,0:T(8,128)(2,1)S(1)}, bf16[256,1536]{1,0:T(8,128)(2,1)S(1)}, u32[]{:S(2)}, u32[]{:S(2)}) collective-permute-start(bf16[256,1536]{1,0:T(8,128)(2,1)S(1)} %fusion.62), channel_id=1, source_target_pairs={{0,16},{4,12},{8,0},{12,28},{16,24},{20,4},{24,8},{28,20},{1,17},{... | collective-permute-start | bytes 2359304 | tf_op jit(solution)/shard_map/ppermute | solution.py:438
  714.7 27.6 %all-to-all-start.4 = ((bf16[4,256,512]{2,1,0:T(8,128)(2,1)}), bf16[4,256,512]{2,1,0:T(8,128)(2,1)S(1)}, u32[]{:S(2)}, u32[]{:S(2)}) async-start(bf16[4,256,512]{2,1,0:T(8,128)(2,1)} %pad_maximum_fusion.1), calls=%async_computation.6 | async-start | bytes 2097152 | tf_op jit(solution)/shard_map/all_to_all | solution.py:550
  (92 other events, 1046.6 us)
Sparse Core Ops, SparseCore 0:
  14.1 49.3 all-gather.5
  69.3 42.5 all-gather.7
  119.2 77.5 all-gather.11
  198.5 63.3 all-gather.13
  264.2 53.3 all-gather.9
  432.8 79.5 reduce-scatter.3
  551.1 67.7 reduce-scatter.5
  622.3 88.6 reduce-scatter.7

commit v4 on v3

--- a/solution.py
+++ b/solution.py
@@ -544,7 +544,8 @@
     term = first_terms.send(first_sum)
     for _ in members[3:]:
         term = first_terms.send(pass_on(term))
-    first_sum, qkv_part = tied(pass_on(term), qkv_part)
+    qkv_part, term = tied(qkv_part, term)
+    first_sum = pass_on(term)
     held["qkv_grad"] = share(qkv_part)
     columns = jnp.stack(jnp.split(held["out"].astype(BF16), mdl_count, 1))
     columns = lax.all_to_all(columns, "mdl", 0, 0, tiled=True)

time: 778 us -> 773 us (level)
  waiting for transfers between devices: 402 us -> 381 us
    ppermute x1, waiting for transfers between devices: 16.9 us -> 3.48 us  [share(): carried = lax.ppermute(term(1).astype(BF16), 'seq', onward)]
    ppermute x18, waiting for transfers between devices: 289 us -> 278 us  [pass_on(): return lax.ppermute(value, 'mdl', ring)]
  transfers between devices with their start and end apart: 40 -> 40, of which waited for: 29 -> 28; matrix products, arithmetic and copies ran while one was open for 29% -> 30% of each run, Pallas kernels for 5% -> 5%
where the time goes in v4:
time: 773 us; the launch traced here: 764 us
  waiting for transfers between devices  381 us (49%)
  matrix products  179 us (23%)
  other arithmetic  68.6 us (9%)
  Pallas kernels  43.8 us (6%)
  starting transfers between devices  40.2 us (5%)
  between operations  31.3 us (4%)
  local copies, waits for them, and re-layouts  20.3 us (3%)
    ppermute x18, waiting for transfers between devices, pass_on(): return lax.ppermute(value, 'mdl', ring)  278 us
    dot_general x30, matrix products, dot(): return lax.dot_general(a, b, (dims, ((), ())), preferred_element_type=F32)  179 us
    all_to_all x2, waiting for transfers between devices, exchange(): return lax.all_to_all(value, 'seq', 0, 0, tiled=True)  30.6 us
    ppermute x2, waiting for transfers between devices, share(): lax.ppermute((term(j) + carried.astype(F32)).astype(BF16), 'seq', onward)  23.6 us
    pallas_call x1, Pallas kernels, attention_back(): pl.pallas_call(functools.partial(attend_back_kernel, size=size, factor=HD...  22.2 us
    pallas_call x1, Pallas kernels, attention(): pl.pallas_call(functools.partial(attend_kernel, size=size, factor=HD ** (...  17.4 us
  transfers between devices with their start and end apart: 40, of which 28 were waited for; matrix products, arithmetic and copies ran while one was open for 30% of the time, Pallas kernels for 5%

profile of v4, /device:TPU:0, one launch (start us, length us, event | category | flops | bytes accessed | tf_op | source)
XLA Modules:
  0.0 764.1 jit_solution(5275488019267203034)
XLA Ops:
  17.2 25.5 %collective-permute-done = bf16[256,2048]{1,0:T(8,128)(2,1)} collective-permute-done((bf16[256,2048]{1,0:T(8,128)(2,1)}, bf16[256,2048]{1,0:T(8,128)(2,1)}, u32[]{:S(2)}, u32[]{:S(2)}) %collective-permute-start) | collective-permute-done | bytes 1048608 | tf_op jit(solution)/shard_map/ppermute | solution.py:358
  46.2 22.9 %collective-permute-done.1 = bf16[256,2048]{1,0:T(8,128)(2,1)} collective-permute-done((bf16[256,2048]{1,0:T(8,128)(2,1)}, bf16[256,2048]{1,0:T(8,128)(2,1)}, u32[]{:S(2)}, u32[]{:S(2)}) %collective-permute-start.1) | collective-permute-done | bytes 1048608 | tf_op jit(solution)/shard_map/ppermute | solution.py:358
  80.2 29.1 %collective-permute-done.2 = bf16[256,2048]{1,0:T(8,128)(2,1)} collective-permute-done((bf16[256,2048]{1,0:T(8,128)(2,1)}, bf16[256,2048]{1,0:T(8,128)(2,1)}, u32[]{:S(2)}, u32[]{:S(2)}) %collective-permute-start.2) | collective-permute-done | bytes 1048608 | tf_op jit(solution)/shard_map/ppermute | solution.py:358
  133.8 20.1 %collective-permute-done.3 = bf16[256,2048]{1,0:T(8,128)(2,1)} collective-permute-done((bf16[256,2048]{1,0:T(8,128)(2,1)}, bf16[256,2048]{1,0:T(8,128)(2,1)}, u32[]{:S(2)}, u32[]{:S(2)}) %collective-permute-start.3) | collective-permute-done | bytes 1048608 | tf_op jit(solution)/shard_map/ppermute | solution.py:358
  163.0 17.8 %collective-permute-done.4 = bf16[256,2048]{1,0:T(8,128)(2,1)} collective-permute-done((bf16[256,2048]{1,0:T(8,128)(2,1)}, bf16[256,2048]{1,0:T(8,128)(2,1)}, u32[]{:S(2)}, u32[]{:S(2)}) %collective-permute-start.4) | collective-permute-done | bytes 1048608 | tf_op jit(solution)/shard_map/ppermute | solution.py:358
  182.2 17.4 %attend.1 = (bf16[8,4,4,32,128]{4,3,2,1,0:T(8,128)(2,1)S(1)}, f32[4,2,1024]{2,1,0:T(2,128)S(1)}) custom-call(s32[1]{0:T(128)} %bitcast.5.own_ref, s32[1024,1]{1,0:T(8,128)S(1)} %copy-done.6, s32[4,2,1024]{2,1,0:T(2,128)S(1)} %pad_add_fusion.1.meta_ref, bf16[8,3,4,4,32,128]{5,4,3,2,1,0:T(8,128)(2,1)S(1)} %all-to-all-done.q_ref.k_ref.v_ref, ...), custom_call_target="tpu_custom_call" | custom-call | flops 5368709120 | bytes 4194304 | tf_op jit(solution)/shard_map/attend/pallas_call | solution.py:176
  205.2 42.2 %collective-permute-done.5 = bf16[256,2048]{1,0:T(8,128)(2,1)S(1)} collective-permute-done((bf16[256,2048]{1,0:T(8,128)(2,1)}, bf16[256,2048]{1,0:T(8,128)(2,1)S(1)}, u32[]{:S(2)}, u32[]{:S(2)}) %collective-permute-start.5) | collective-permute-done | bytes 1048608 | tf_op jit(solution)/shard_map/ppermute | solution.py:358
  251.1 10.8 %all-gather.14.cloned.1.call-done = bf16[2048,2048]{1,0:T(8,128)(2,1)} async-done(((bf16[256,2048]{1,0:T(8,128)(2,1)}), bf16[2048,2048]{1,0:T(8,128)(2,1)}) %all-gather.14.cloned.1.call-update) | async-done | bytes 8388624 | tf_op jit(solution)/shard_map/all_gather | solution.py:393
  261.9 6.6 fusion.96
  271.0 26.0 %collective-permute-done.6 = bf16[256,2048]{1,0:T(8,128)(2,1)S(1)} collective-permute-done((bf16[256,2048]{1,0:T(8,128)(2,1)S(1)}, bf16[256,2048]{1,0:T(8,128)(2,1)S(1)}, u32[]{:S(2)}, u32[]{:S(2)}) %collective-permute-start.6) | collective-permute-done | bytes 1048608 | tf_op jit(solution)/shard_map/ppermute | solution.py:358
  305.6 18.1 %collective-permute-done.7 = bf16[256,2048]{1,0:T(8,128)(2,1)} collective-permute-done((bf16[256,2048]{1,0:T(8,128)(2,1)S(1)}, bf16[256,2048]{1,0:T(8,128)(2,1)}, u32[]{:S(2)}, u32[]{:S(2)}) %collective-permute-start.7) | collective-permute-done | bytes 1048608 | tf_op jit(solution)/shard_map/ppermute | solution.py:358
  329.1 7.0 fusion.40
  360.6 11.2 %collective-permute-done.9 = bf16[256,2048]{1,0:T(8,128)(2,1)S(1)} collective-permute-done((bf16[256,2048]{1,0:T(8,128)(2,1)S(1)}, bf16[256,2048]{1,0:T(8,128)(2,1)S(1)}, u32[]{:S(2)}, u32[]{:S(2)}) %collective-permute-start.9) | collective-permute-done | bytes 1048608 | tf_op jit(solution)/shard_map/ppermute | solution.py:358
  376.6 12.5 %convolution_convert_fusion.3 = bf16[2048,2048]{1,0:T(8,128)(2,1)} fusion(bf16[256,2048]{1,0:T(8,128)(2,1)S(1)} %copy-done.56, bf16[256,2048]{1,0:T(8,128)(2,1)} %collective-permute-done.4, bf16[256,2048]{1,0:T(8,128)(2,1)} %collective-permute-done.3, bf16[256,2048]{1,0:T(8,128)(2,1)} %bitcast_convert_fusion, bf16[256,2048]{1,0:T(8,128)(2,1)S(1)} %get-tuple-element.122, ...), kind=kOutput, calls=%fused_computation.4 | convolution fusion | flops 8627683328 | bytes 16777216 | tf_op jit(solution)/shard_map/dot_general | solution.py:46
  389.2 12.2 %collective-permute-done.10 = bf16[256,2048]{1,0:T(8,128)(2,1)} collective-permute-done((bf16[256,2048]{1,0:T(8,128)(2,1)}, bf16[256,2048]{1,0:T(8,128)(2,1)}, u32[]{:S(2)}, u32[]{:S(2)}) %collective-permute-start.10) | collective-permute-done | bytes 1048608 | tf_op jit(solution)/shard_map/ppermute | solution.py:358
  401.4 7.2 fusion.35
  408.9 12.4 %convolution_convert_fusion.2 = bf16[2048,2048]{1,0:T(8,128)(2,1)} fusion(bf16[256,2048]{1,0:T(8,128)(2,1)} %collective-permute-done.8, bf16[256,2048]{1,0:T(8,128)(2,1)} %collective-permute-done.7, bf16[256,2048]{1,0:T(8,128)(2,1)S(1)} %copy-done.58, bf16[256,2048]{1,0:T(8,128)(2,1)S(1)} %get-tuple-element.116, bf16[256,2048]{1,0:T(8,128)(2,1)S(1)} %copy-done.68, ...), kind=kOutput, calls=%fused_computation.3 | convolution fusion | flops 8627683328 | bytes 16777216 | tf_op jit(solution)/shard_map/dot_general | solution.py:46
  421.3 11.4 %collective-permute-done.11 = bf16[256,2048]{1,0:T(8,128)(2,1)} collective-permute-done((bf16[256,2048]{1,0:T(8,128)(2,1)}, bf16[256,2048]{1,0:T(8,128)(2,1)}, u32[]{:S(2)}, u32[]{:S(2)}) %collective-permute-start.11) | collective-permute-done | bytes 1048608 | tf_op jit(solution)/shard_map/ppermute | solution.py:358
  432.7 7.2 multiply_reduce_fusion.7
  443.2 6.7 convolution_convert_fusion.8.refs_0_
  454.2 7.9 %fusion.100 = f32[256,2048]{1,0:T(8,128)} fusion(bf16[256,2048]{1,0:T(8,128)(2,1)S(1)} %copy-done.66, bf16[2048,2048]{1,0:T(8,128)(2,1)} %all-gather.10.cloned.1.call-done), kind=kOutput, calls=%fused_computation.210 | convolution fusion | flops 2147483648 | bytes 11534336 | tf_op jit(solution)/shard_map/dot_general | solution.py:46
  462.2 7.2 fusion.99
  482.5 22.2 %attend_back.1 = bf16[8,3,4,4,32,128]{5,4,3,2,1,0:T(8,128)(2,1)S(1)} custom-call(s32[1]{0:T(128)} %bitcast.5.own_ref, s32[1024,1]{1,0:T(8,128)S(1)} %copy-done.7, s32[4,2,1024]{2,1,0:T(2,128)S(1)} %pad_add_fusion.1.meta_ref, f32[4,2,1024]{2,1,0:T(2,128)S(1)} %get-tuple-element.126.lse_ref, bf16[8,3,4,4,32,128]{5,4,3,2,1,0:T(8,128)(2,1)} %copy-done.1, ...), custom_call_target="tpu_custom_call" | custom-call | flops 13421772800 | bytes 8388608 | tf_op jit(solution)/shard_map/attend_back/pallas_call | solution.py:206
  510.8 7.3 convolution_convert_fusion.1
  518.1 30.6 %all-to-all-done.3.refs_0_ = bf16[8,3,4,4,32,128]{5,4,3,2,1,0:T(8,128)(2,1)S(1)} async-done(((bf16[8,3,4,4,32,128]{5,4,3,2,1,0:T(8,128)(2,1)}), bf16[8,3,4,4,32,128]{5,4,3,2,1,0:T(8,128)(2,1)S(1)}, u32[]{:S(2)}, u32[]{:S(2)}) %all-to-all-start.3) | async-done | bytes 3145760 | tf_op jit(solution)/shard_map/all_to_all | solution.py:302
  551.0 6.6 fusion.75
  557.9 7.1 fusion.69
  583.2 8.5 %convolution_convert_fusion = bf16[2048,1536]{1,0:T(8,128)(2,1)S(1)} fusion(bf16[1024,1536]{1,0:T(8,128)(2,1)S(1)} %bitcast.173, bf16[256,2048]{1,0:T(8,128)(2,1)} %collective-permute-done.2, bf16[256,2048]{1,0:T(8,128)(2,1)} %collective-permute-done.1, bf16[256,2048]{1,0:T(8,128)(2,1)} %collective-permute-done, bf16[256,2048]{1,0:T(8,128)(2,1)S(1)} %copy-done.37), kind=kOutput, calls=%fused_computation.1 | convolution fusion | flops 6462373888 | bytes 13631488 | tf_op jit(solution)/shard_map/dot_general | solution.py:46
  591.7 13.6 %collective-permute-done.15 = bf16[256,2048]{1,0:T(8,128)(2,1)S(1)} collective-permute-done((bf16[256,2048]{1,0:T(8,128)(2,1)S(1)}, bf16[256,2048]{1,0:T(8,128)(2,1)S(1)}, u32[]{:S(2)}, u32[]{:S(2)}) %collective-permute-start.15) | collective-permute-done | bytes 1048608 | tf_op jit(solution)/shard_map/ppermute | solution.py:358
  640.3 21.5 %collective-permute-done.14 = bf16[256,2048]{1,0:T(8,128)(2,1)} collective-permute-done((bf16[256,2048]{1,0:T(8,128)(2,1)}, bf16[256,2048]{1,0:T(8,128)(2,1)}, u32[]{:S(2)}, u32[]{:S(2)}) %collective-permute-start.14) | collective-permute-done | bytes 1048608 | tf_op jit(solution)/shard_map/ppermute | solution.py:358
  678.8 23.6 %collective-permute-done.20 = bf16[256,1536]{1,0:T(8,128)(2,1)S(1)} collective-permute-done((bf16[256,1536]{1,0:T(8,128)(2,1)S(1)}, bf16[256,1536]{1,0:T(8,128)(2,1)S(1)}, u32[]{:S(2)}, u32[]{:S(2)}) %collective-permute-start.20) | collective-permute-done | bytes 786464 | tf_op jit(solution)/shard_map/ppermute | solution.py:438
  722.9 13.3 %all-to-all-done.4 = bf16[4,256,512]{2,1,0:T(8,128)(2,1)S(1)} async-done(((bf16[4,256,512]{2,1,0:T(8,128)(2,1)}), bf16[4,256,512]{2,1,0:T(8,128)(2,1)S(1)}, u32[]{:S(2)}, u32[]{:S(2)}) %all-to-all-start.4) | async-done | bytes 1048608 | tf_op jit(solution)/shard_map/all_to_all | solution.py:551
  (329 shorter events, 239.0 us)
Async XLA Ops:
  7.2 61.9 %all-gather.6.cloned.1.call-start = ((), (), s32[]{:S(2)}) async-start(), calls=%async_computation.8 | async-start | bytes 7077888 | tf_op jit(solution)/shard_map/all_gather | solution.py:393
  14.0 97.8 %all-gather.8.cloned.1.call-start = ((), (), s32[]{:S(2)}) async-start(), calls=%async_computation.9 | async-start | bytes 1310720 | tf_op jit(solution)/shard_map/all_gather | solution.py:453
  14.1 28.6 %collective-permute-start = (bf16[256,2048]{1,0:T(8,128)(2,1)}, bf16[256,2048]{1,0:T(8,128)(2,1)}, u32[]{:S(2)}, u32[]{:S(2)}) collective-permute-start(bf16[256,2048]{1,0:T(8,128)(2,1)} %add_convert_fusion.5), channel_id=1, source_target_pairs={{0,1},{1,2},{2,3},{3,0},{4,5},{5,6},{6,7},{7,4},{8,9},{9,10},{10,1... | collective-permute-start | bytes 3145736 | tf_op jit(solution)/shard_map/ppermute | solution.py:358
  42.7 26.5 %collective-permute-start.1 = (bf16[256,2048]{1,0:T(8,128)(2,1)}, bf16[256,2048]{1,0:T(8,128)(2,1)}, u32[]{:S(2)}, u32[]{:S(2)}) collective-permute-start(bf16[256,2048]{1,0:T(8,128)(2,1)} %collective-permute-done), channel_id=1, source_target_pairs={{0,1},{1,2},{2,3},{3,0},{4,5},{5,6},{6,7},{7,4},{8,9},{9,10},{10,1... | collective-permute-start | bytes 3145736 | tf_op jit(solution)/shard_map/ppermute | solution.py:358
  69.1 40.1 %collective-permute-start.2 = (bf16[256,2048]{1,0:T(8,128)(2,1)}, bf16[256,2048]{1,0:T(8,128)(2,1)}, u32[]{:S(2)}, u32[]{:S(2)}) collective-permute-start(bf16[256,2048]{1,0:T(8,128)(2,1)} %collective-permute-done.1), channel_id=1, source_target_pairs={{0,1},{1,2},{2,3},{3,0},{4,5},{5,6},{6,7},{7,4},{8,9},{9,10},{10,1... | collective-permute-start | bytes 3145736 | tf_op jit(solution)/shard_map/ppermute | solution.py:358
  69.2 181.8 %all-gather.12.cloned.1.call-start = ((), (), s32[]{:S(2)}) async-start(), calls=%async_computation.11 | async-start | bytes 9437184 | tf_op jit(solution)/shard_map/all_gather | solution.py:393
  119.1 142.9 %all-gather.14.cloned.1.call-start = ((), (), s32[]{:S(2)}) async-start(), calls=%async_computation.12 | async-start | bytes 9437184 | tf_op jit(solution)/shard_map/all_gather | solution.py:393
  119.6 61.2 %all-to-all-start = ((bf16[8,3,4,4,32,128]{5,4,3,2,1,0:T(8,128)(2,1)}), bf16[8,3,4,4,32,128]{5,4,3,2,1,0:T(8,128)(2,1)S(1)}, u32[]{:S(2)}, u32[]{:S(2)}) async-start(bf16[8,3,4,4,32,128]{5,4,3,2,1,0:T(8,128)(2,1)} %to_units.1), calls=%async_computation | async-start | bytes 6291456 | tf_op jit(solution)/shard_map/all_to_all | solution.py:302
  123.3 205.8 %all-gather.10.cloned.1.call-start = ((), (), s32[]{:S(2)}) async-start(), calls=%async_computation.10 | async-start | bytes 9437184 | tf_op jit(solution)/shard_map/all_gather | solution.py:393
  126.4 27.5 %collective-permute-start.3 = (bf16[256,2048]{1,0:T(8,128)(2,1)}, bf16[256,2048]{1,0:T(8,128)(2,1)}, u32[]{:S(2)}, u32[]{:S(2)}) collective-permute-start(bf16[256,2048]{1,0:T(8,128)(2,1)} %bitcast_convert_fusion), channel_id=1, source_target_pairs={{0,1},{1,2},{2,3},{3,0},{4,5},{5,6},{6,7},{7,4},{8,9},{9,10},{10,1... | collective-permute-start | bytes 3145736 | tf_op jit(solution)/shard_map/ppermute | solution.py:358
  153.9 26.9 %collective-permute-start.4 = (bf16[256,2048]{1,0:T(8,128)(2,1)}, bf16[256,2048]{1,0:T(8,128)(2,1)}, u32[]{:S(2)}, u32[]{:S(2)}) collective-permute-start(bf16[256,2048]{1,0:T(8,128)(2,1)} %collective-permute-done.3), channel_id=1, source_target_pairs={{0,1},{1,2},{2,3},{3,0},{4,5},{5,6},{6,7},{7,4},{8,9},{9,10},{10,1... | collective-permute-start | bytes 3145736 | tf_op jit(solution)/shard_map/ppermute | solution.py:358
  200.6 50.3 %all-to-all-start.1 = ((bf16[32,4,32,128]{3,2,1,0:T(8,128)(2,1)}), bf16[32,4,32,128]{3,2,1,0:T(8,128)(2,1)S(1)}, u32[]{:S(2)}, u32[]{:S(2)}) async-start(bf16[32,4,32,128]{3,2,1,0:T(8,128)(2,1)} %bitcast.175), calls=%async_computation.1 | async-start | bytes 2097152 | tf_op jit(solution)/shard_map/all_to_all | solution.py:306
  203.4 435.4 %reduce-scatter.4.cloned.1.call-start = ((), (), s32[]{:S(2)}) async-start(), calls=%async_computation.13 | async-start | bytes 9437184 | tf_op jit(solution)/shard_map/reduce_scatter | solution.py:422
  203.4 44.0 %collective-permute-start.5 = (bf16[256,2048]{1,0:T(8,128)(2,1)}, bf16[256,2048]{1,0:T(8,128)(2,1)S(1)}, u32[]{:S(2)}, u32[]{:S(2)}) collective-permute-start(bf16[256,2048]{1,0:T(8,128)(2,1)} %collective-permute-done.4), channel_id=1, source_target_pairs={{0,1},{1,2},{2,3},{3,0},{4,5},{5,6},{6,7},{7,4},{8,9},{9,10},{10,1... | collective-permute-start | bytes 3145736 | tf_op jit(solution)/shard_map/ppermute | solution.py:358
  269.8 27.1 %collective-permute-start.6 = (bf16[256,2048]{1,0:T(8,128)(2,1)S(1)}, bf16[256,2048]{1,0:T(8,128)(2,1)S(1)}, u32[]{:S(2)}, u32[]{:S(2)}) collective-permute-start(bf16[256,2048]{1,0:T(8,128)(2,1)S(1)} %get-tuple-element.116), channel_id=1, source_target_pairs={{0,1},{1,2},{2,3},{3,0},{4,5},{5,6},{6,7},{7,4},{8,9},{9,10},{10,1... | collective-permute-start | bytes 3145736 | tf_op jit(solution)/shard_map/ppermute | solution.py:358
  297.0 26.8 %collective-permute-start.7 = (bf16[256,2048]{1,0:T(8,128)(2,1)S(1)}, bf16[256,2048]{1,0:T(8,128)(2,1)}, u32[]{:S(2)}, u32[]{:S(2)}) collective-permute-start(bf16[256,2048]{1,0:T(8,128)(2,1)S(1)} %collective-permute-done.6), channel_id=1, source_target_pairs={{0,1},{1,2},{2,3},{3,0},{4,5},{5,6},{6,7},{7,4},{8,9},{9,10},{10,1... | collective-permute-start | bytes 3145736 | tf_op jit(solution)/shard_map/ppermute | solution.py:358
  323.8 29.3 %collective-permute-start.8 = (bf16[256,2048]{1,0:T(8,128)(2,1)}, bf16[256,2048]{1,0:T(8,128)(2,1)}, u32[]{:S(2)}, u32[]{:S(2)}) collective-permute-start(bf16[256,2048]{1,0:T(8,128)(2,1)} %collective-permute-done.7), channel_id=1, source_target_pairs={{0,1},{1,2},{2,3},{3,0},{4,5},{5,6},{6,7},{7,4},{8,9},{9,10},{10,1... | collective-permute-start | bytes 3145736 | tf_op jit(solution)/shard_map/ppermute | solution.py:358
  342.3 29.5 %collective-permute-start.9 = (bf16[256,2048]{1,0:T(8,128)(2,1)S(1)}, bf16[256,2048]{1,0:T(8,128)(2,1)S(1)}, u32[]{:S(2)}, u32[]{:S(2)}) collective-permute-start(bf16[256,2048]{1,0:T(8,128)(2,1)S(1)} %convolution_convert_fusion.9), channel_id=1, source_target_pairs={{0,1},{1,2},{2,3},{3,0},{4,5},{5,6},{6,7},{7,4},{8,9},{9,10},{10,1... | collective-permute-start | bytes 3145736 | tf_op jit(solution)/shard_map/ppermute | solution.py:358
  376.4 25.0 %collective-permute-start.10 = (bf16[256,2048]{1,0:T(8,128)(2,1)}, bf16[256,2048]{1,0:T(8,128)(2,1)}, u32[]{:S(2)}, u32[]{:S(2)}) collective-permute-start(bf16[256,2048]{1,0:T(8,128)(2,1)} %fusion.36), channel_id=1, source_target_pairs={{0,1},{1,2},{2,3},{3,0},{4,5},{5,6},{6,7},{7,4},{8,9},{9,10},{10,1... | collective-permute-start | bytes 3145736 | tf_op jit(solution)/shard_map/ppermute | solution.py:358
  408.6 24.1 %collective-permute-start.11 = (bf16[256,2048]{1,0:T(8,128)(2,1)}, bf16[256,2048]{1,0:T(8,128)(2,1)}, u32[]{:S(2)}, u32[]{:S(2)}) collective-permute-start(bf16[256,2048]{1,0:T(8,128)(2,1)} %fusion.35), channel_id=1, source_target_pairs={{0,1},{1,2},{2,3},{3,0},{4,5},{5,6},{6,7},{7,4},{8,9},{9,10},{10,1... | collective-permute-start | bytes 3145736 | tf_op jit(solution)/shard_map/ppermute | solution.py:358
  451.1 28.1 %all-to-all-start.2 = ((bf16[32,4,32,128]{3,2,1,0:T(8,128)(2,1)}), bf16[32,4,32,128]{3,2,1,0:T(8,128)(2,1)S(1)}, u32[]{:S(2)}, u32[]{:S(2)}) async-start(bf16[32,4,32,128]{3,2,1,0:T(8,128)(2,1)} %own_units.1), calls=%async_computation.2 | async-start | bytes 2097152 | tf_op jit(solution)/shard_map/all_to_all | solution.py:306
  479.2 27.4 %collective-permute-start.12 = (bf16[256,2048]{1,0:T(8,128)(2,1)S(1)}, bf16[256,2048]{1,0:T(8,128)(2,1)}, u32[]{:S(2)}, u32[]{:S(2)}) collective-permute-start(bf16[256,2048]{1,0:T(8,128)(2,1)S(1)} %fusion.98), channel_id=1, source_target_pairs={{0,1},{1,2},{2,3},{3,0},{4,5},{5,6},{6,7},{7,4},{8,9},{9,10},{10,1... | collective-permute-start | bytes 3145736 | tf_op jit(solution)/shard_map/ppermute | solution.py:358
  506.7 42.0 %all-to-all-start.3 = ((bf16[8,3,4,4,32,128]{5,4,3,2,1,0:T(8,128)(2,1)}), bf16[8,3,4,4,32,128]{5,4,3,2,1,0:T(8,128)(2,1)S(1)}, u32[]{:S(2)}, u32[]{:S(2)}) async-start(bf16[8,3,4,4,32,128]{5,4,3,2,1,0:T(8,128)(2,1)} %copy-done.4), calls=%async_computation.3 | async-start | bytes 6291456 | tf_op jit(solution)/shard_map/all_to_all | solution.py:302
  510.8 194.4 %reduce-scatter.6.cloned.1.call-start = ((), (), s32[]{:S(2)}) async-start(), calls=%async_computation.14 | async-start | bytes 9437184 | tf_op jit(solution)/shard_map/reduce_scatter | solution.py:422
  551.0 164.8 %reduce-scatter.8.cloned.1.call-start = ((), (), s32[]{:S(2)}) async-start(), calls=%async_computation.15 | async-start | bytes 9437184 | tf_op jit(solution)/shard_map/reduce_scatter | solution.py:422
  557.7 23.7 %collective-permute-start.13 = (bf16[256,2048]{1,0:T(8,128)(2,1)}, bf16[256,2048]{1,0:T(8,128)(2,1)}, u32[]{:S(2)}, u32[]{:S(2)}) collective-permute-start(bf16[256,2048]{1,0:T(8,128)(2,1)} %fusion.75), channel_id=1, source_target_pairs={{0,1},{1,2},{2,3},{3,0},{4,5},{5,6},{6,7},{7,4},{8,9},{9,10},{10,1... | collective-permute-start | bytes 3145736 | tf_op jit(solution)/shard_map/ppermute | solution.py:358
  611.6 28.7 %collective-permute-start.16 = (bf16[256,2048]{1,0:T(8,128)(2,1)}, bf16[256,2048]{1,0:T(8,128)(2,1)S(1)}, u32[]{:S(2)}, u32[]{:S(2)}) collective-permute-start(bf16[256,2048]{1,0:T(8,128)(2,1)} %add_convert_fusion.1), channel_id=1, source_target_pairs={{0,1},{1,2},{2,3},{3,0},{4,5},{5,6},{6,7},{7,4},{8,9},{9,10},{10,1... | collective-permute-start | bytes 3145736 | tf_op jit(solution)/shard_map/ppermute | solution.py:358
  623.0 38.9 %collective-permute-start.14 = (bf16[256,2048]{1,0:T(8,128)(2,1)}, bf16[256,2048]{1,0:T(8,128)(2,1)}, u32[]{:S(2)}, u32[]{:S(2)}) collective-permute-start(bf16[256,2048]{1,0:T(8,128)(2,1)} %add_convert_fusion.3), channel_id=1, source_target_pairs={{0,1},{1,2},{2,3},{3,0},{4,5},{5,6},{6,7},{7,4},{8,9},{9,10},{10,1... | collective-permute-start | bytes 3145736 | tf_op jit(solution)/shard_map/ppermute | solution.py:358
  637.7 33.8 %collective-permute-start.19 = (bf16[256,1536]{1,0:T(8,128)(2,1)}, bf16[256,1536]{1,0:T(8,128)(2,1)}, u32[]{:S(2)}, u32[]{:S(2)}) collective-permute-start(bf16[256,1536]{1,0:T(8,128)(2,1)} %fusion.62), channel_id=1, source_target_pairs={{0,16},{4,12},{8,0},{12,28},{16,24},{20,4},{24,8},{28,20},{1,17},{... | collective-permute-start | bytes 2359304 | tf_op jit(solution)/shard_map/ppermute | solution.py:438
  664.5 47.7 %collective-permute-start.21 = (bf16[256,2048]{1,0:T(8,128)(2,1)}, bf16[256,2048]{1,0:T(8,128)(2,1)}, u32[]{:S(2)}, u32[]{:S(2)}) collective-permute-start(bf16[256,2048]{1,0:T(8,128)(2,1)} %add_convert_fusion), channel_id=1, source_target_pairs={{0,1},{1,2},{2,3},{3,0},{4,5},{5,6},{6,7},{7,4},{8,9},{9,10},{10,1... | collective-permute-start | bytes 3145736 | tf_op jit(solution)/shard_map/ppermute | solution.py:358
  674.2 28.2 %collective-permute-start.20 = (bf16[256,1536]{1,0:T(8,128)(2,1)S(1)}, bf16[256,1536]{1,0:T(8,128)(2,1)S(1)}, u32[]{:S(2)}, u32[]{:S(2)}) collective-permute-start(bf16[256,1536]{1,0:T(8,128)(2,1)S(1)} %fusion.64), channel_id=1, source_target_pairs={{0,16},{4,12},{8,0},{12,28},{16,24},{20,4},{24,8},{28,20},{1,17},{... | collective-permute-start | bytes 2359304 | tf_op jit(solution)/shard_map/ppermute | solution.py:438
  707.5 28.7 %all-to-all-start.4 = ((bf16[4,256,512]{2,1,0:T(8,128)(2,1)}), bf16[4,256,512]{2,1,0:T(8,128)(2,1)S(1)}, u32[]{:S(2)}, u32[]{:S(2)}) async-start(bf16[4,256,512]{2,1,0:T(8,128)(2,1)} %pad_maximum_fusion.1), calls=%async_computation.6 | async-start | bytes 2097152 | tf_op jit(solution)/shard_map/all_to_all | solution.py:551
  (87 other events, 1046.5 us)
Sparse Core Ops, SparseCore 0:
  14.1 49.3 all-gather.5
  69.3 42.5 all-gather.7
  119.2 77.5 all-gather.11
  198.5 63.3 all-gather.13
  264.2 53.3 all-gather.9
  432.8 79.5 reduce-scatter.3
  551.1 67.7 reduce-scatter.5
  622.4 78.6 reduce-scatter.7
